TPU v7x, 256 devices: a whole 4x4x8 slice. The times are simulated.
256 devices in a mesh: replica: 8 (over x, core), outer: 4 (over y), link: 8 (over z).
Axes of the slice: x: 4, y: 4, z: 8, core: 2. Of those that a mesh axis runs over, the one named last changes fastest.
Arguments:
- link_in: bfloat16 [8, 16384, 256], P('replica', ('outer', 'link')), may hold values from -6 to 6
- path_in: bfloat16 [8, 4096, 256], P('replica', ('outer', 'link')), may hold values from -6 to 6
- hop_slots: int32 [8, 4096, 24], P('replica', ('outer', 'link')), may hold values from 0 to 2047
- hop_lens: int32 [8, 4096], P('replica', ('outer', 'link')), may hold values from 2 to 24
- failed: int32 [8, 16384], P('replica', ('outer', 'link')), may hold values 0 or 1
- serve_index: int32 [8, 32, 32, 64], P('replica', None, ('outer', 'link')), may hold values from 0 to 511
- link_grad: bfloat16 [8, 16384, 256], P('replica', ('outer', 'link')), may hold values from -6 to 6
- path_grad: bfloat16 [8, 4096, 256], P('replica', ('outer', 'link')), may hold values from -6 to 6
- gru_wx: bfloat16 [256, 768], replicated, may hold values from -0.375 to 0.375
- gru_wh: bfloat16 [256, 768], replicated, may hold values from -0.375 to 0.375
- gru_bias: float32 [768], replicated, may hold values from -3 to 3
- mlp_w1: bfloat16 [512, 256], replicated, may hold values from -0.25 to 0.25
- mlp_b1: float32 [256], replicated, may hold values from -3 to 3
- mlp_w2: bfloat16 [256, 256], replicated, may hold values from -0.375 to 0.375
- mlp_b2: float32 [256], replicated, may hold values from -3 to 3
Outputs:
- link_out: bfloat16 [8, 16384, 256], P('replica', ('outer', 'link'))
- path_out: bfloat16 [8, 4096, 256], P('replica', ('outer', 'link'))
- link_in_grad: float32 [8, 16384, 256], P('replica', ('outer', 'link'))
- path_in_grad: float32 [8, 4096, 256], P('replica', ('outer', 'link'))
- grad_wx: float32 [256, 768], replicated
- grad_wh: float32 [256, 768], replicated
- grad_bias: float32 [768], replicated
- grad_w1: float32 [512, 256], replicated
- grad_b1: float32 [256], replicated
- grad_w2: float32 [256, 256], replicated
- grad_b2: float32 [256], replicated
Inputs may be any that keep to these rules, and one draw needn't show every extreme that they name: `serve_index`: entry [s, d, o, c] names, among the 512 links of owner device o, the link in request slot c of device d; a link may fill several slots. `hop_slots`: slot o * 64 + c is request slot c of the flow's own device towards owner o; entries at hops past the flow's length are ignored. 1 marks a failed link.
All inputs are finite; a program needn't handle non-finite values. No bound on the sum of `failed` on one device may be relied on, other than what follows from the above.
Results may differ from a plain program's by a relative error of at most 0.0067.
Values may be sent and summed in bfloat16 or wider, within the bound.
No kernel may reach another device: no remote copies, remote signals or barrier semaphores. Data moves between devices by JAX's collectives and lax.ppermute only.
A program may use at most 128 MiB of HBM per device.

v0:
```python
import jax
import jax.numpy as jnp
from jax import lax
from jax.sharding import PartitionSpec as P


def gate_terms(state_now, hop_input, input_weight, hidden_weight, gate_bias):
    from_input = jnp.dot(hop_input, input_weight, preferred_element_type=jnp.float32) + gate_bias
    from_state = jnp.dot(
        state_now.astype(jnp.bfloat16), hidden_weight, preferred_element_type=jnp.float32
    )
    return (from_input, from_state)


def gru_cell(state_now, from_input, from_state):
    feat_width = state_now.shape[1]
    update = jax.nn.sigmoid(from_input[:, :feat_width] + from_state[:, :feat_width])
    reset = jax.nn.sigmoid(
        from_input[:, feat_width : 2 * feat_width] + from_state[:, feat_width : 2 * feat_width]
    )
    candidate = jnp.tanh(from_input[:, 2 * feat_width :] + reset * from_state[:, 2 * feat_width :])
    return (candidate + update * (state_now - candidate), update, reset, candidate)


def gru_forward(path_start, hop_inputs, live_mask, input_weight, hidden_weight, gate_bias):

    def advance(state_now, scan_item):
        hop_input, live_now = scan_item
        from_input, from_state = gate_terms(
            state_now, hop_input, input_weight, hidden_weight, gate_bias
        )
        stepped = gru_cell(state_now, from_input, from_state)[0]
        state_next = jnp.where(live_now[:, None] > 0, stepped, state_now)
        return (state_next, (state_next,))

    return lax.scan(advance, path_start.astype(jnp.float32), (hop_inputs, live_mask))[1]


def back_step(
    carried, hop_input, state_now, live_now, hop_grad, from_input, from_state, input_tr, hidden_tr
):
    grad_state, grad_wx, grad_wh, grad_bias = carried
    feat_width = state_now.shape[1]
    live_col = live_now[:, None]
    grad_state = grad_state + live_col * hop_grad
    update, reset, candidate = gru_cell(state_now, from_input, from_state)[1:]
    pre_update = grad_state * (state_now - candidate) * update * (1.0 - update)
    pre_cand = grad_state * (1.0 - update) * (1.0 - candidate * candidate)
    pre_reset = pre_cand * from_state[:, 2 * feat_width :] * reset * (1.0 - reset)
    grad_in = jnp.concatenate([pre_update, pre_reset, pre_cand], axis=1) * live_col
    grad_hid = jnp.concatenate([pre_update, pre_reset, pre_cand * reset], axis=1) * live_col
    in_bf = grad_in.astype(jnp.bfloat16)
    hid_bf = grad_hid.astype(jnp.bfloat16)
    grad_prev = jnp.where(
        live_col > 0,
        grad_state * update + jnp.dot(hid_bf, hidden_tr, preferred_element_type=jnp.float32),
        grad_state,
    )
    grad_input = jnp.dot(in_bf, input_tr, preferred_element_type=jnp.float32)
    grad_wx = grad_wx + jnp.dot(hop_input.T, in_bf, preferred_element_type=jnp.float32)
    grad_wh = grad_wh + jnp.dot(
        state_now.astype(jnp.bfloat16).T, hid_bf, preferred_element_type=jnp.float32
    )
    grad_bias = grad_bias + jnp.sum(grad_in, axis=0)
    return ((grad_prev, grad_wx, grad_wh, grad_bias), grad_input)


def gru_backward(
    path_start,
    states,
    hop_inputs,
    live_mask,
    hop_grads,
    path_grad,
    input_weight,
    hidden_weight,
    gate_bias,
):
    feat_width = path_start.shape[1]
    prior_states = jnp.concatenate([path_start.astype(jnp.float32)[None], states[:-1]], axis=0)
    input_tr = input_weight.T
    hidden_tr = hidden_weight.T
    initial = (
        path_grad.astype(jnp.float32),
        jnp.zeros((feat_width, 3 * feat_width), jnp.float32),
        jnp.zeros((feat_width, 3 * feat_width), jnp.float32),
        jnp.zeros((3 * feat_width,), jnp.float32),
    )

    def retreat(carried, scan_item):
        hop_input, state_now, live_now, hop_grad = scan_item
        from_input, from_state = gate_terms(
            state_now, hop_input, input_weight, hidden_weight, gate_bias
        )
        return back_step(
            carried,
            hop_input,
            state_now,
            live_now,
            hop_grad,
            from_input,
            from_state,
            input_tr,
            hidden_tr,
        )

    scan_items = (hop_inputs, prior_states, live_mask, hop_grads)
    return lax.scan(retreat, initial, scan_items, reverse=True)


def link_forward(link_rows, agg_bf, keep_col, mlp_w1, mlp_b1, mlp_w2, mlp_b2):
    feat_width = link_rows.shape[1]
    pre_act = (
        jnp.dot(link_rows, mlp_w1[:feat_width], preferred_element_type=jnp.float32)
        + jnp.dot(agg_bf, mlp_w1[feat_width:], preferred_element_type=jnp.float32)
        + mlp_b1
    )
    activ = jax.nn.silu(pre_act).astype(jnp.bfloat16)
    value = (
        link_rows.astype(jnp.float32)
        + jnp.dot(activ, mlp_w2, preferred_element_type=jnp.float32)
        + mlp_b2
    )
    return ((keep_col * value).astype(jnp.bfloat16), pre_act, activ)


def link_backward(link_grad_rows, link_rows, agg_bf, keep_col, pre_act, activ, mlp_w1, mlp_w2):
    feat_width = link_rows.shape[1]
    grad_val = keep_col * link_grad_rows.astype(jnp.float32)
    val_bf = grad_val.astype(jnp.bfloat16)
    grad_w2 = jnp.dot(activ.T, val_bf, preferred_element_type=jnp.float32)
    grad_b2 = jnp.sum(grad_val, axis=0)
    grad_act = jnp.dot(val_bf, mlp_w2.T, preferred_element_type=jnp.float32)
    sigma = jax.nn.sigmoid(pre_act)
    grad_pre = grad_act * sigma * (1.0 + pre_act * (1.0 - sigma))
    pre_bf = grad_pre.astype(jnp.bfloat16)
    grad_w1 = jnp.concatenate(
        [
            jnp.dot(link_rows.T, pre_bf, preferred_element_type=jnp.float32),
            jnp.dot(agg_bf.T, pre_bf, preferred_element_type=jnp.float32),
        ],
        axis=0,
    )
    grad_b1 = jnp.sum(grad_pre, axis=0)
    link_direct = grad_val + jnp.dot(
        pre_bf, mlp_w1[:feat_width].T, preferred_element_type=jnp.float32
    )
    agg_grad = jnp.dot(pre_bf, mlp_w1[feat_width:].T, preferred_element_type=jnp.float32).astype(
        jnp.bfloat16
    )
    return (link_direct, agg_grad, (grad_w1, grad_b1, grad_w2, grad_b2))


def swap_slots(blocks):
    return lax.all_to_all(blocks, ("outer", "link"), split_axis=0, concat_axis=0, tiled=True)


def body(
    link_in,
    path_in,
    hop_slots,
    hop_lens,
    failed,
    serve_index,
    link_grad,
    path_grad,
    gru_wx,
    gru_wh,
    gru_bias,
    mlp_w1,
    mlp_b1,
    mlp_w2,
    mlp_b2,
):
    link_rows = link_in[0]
    feat_width = link_rows.shape[1]
    link_count = link_rows.shape[0]
    serve_rows = serve_index[0, :, 0, :]
    group_size, slot_cap = serve_rows.shape
    serve_flat = serve_rows.reshape(-1)
    slot_ids = hop_slots[0].T
    hop_count, flow_count = slot_ids.shape
    flat_slots = slot_ids.reshape(-1)
    live_mask = (jnp.arange(hop_count, dtype=jnp.int32)[:, None] < hop_lens[0][None, :]).astype(
        jnp.float32
    )
    fetched = swap_slots(jnp.take(link_rows, serve_rows, axis=0))
    hop_inputs = jnp.take(fetched.reshape(group_size * slot_cap, feat_width), slot_ids, axis=0)
    states = gru_forward(path_in[0], hop_inputs, live_mask, gru_wx, gru_wh, gru_bias)[0]
    partial_value = jax.ops.segment_sum(
        (states * live_mask[:, :, None]).reshape(hop_count * flow_count, feat_width),
        flat_slots,
        num_segments=group_size * slot_cap,
    ).astype(jnp.bfloat16)
    arrived = swap_slots(partial_value.reshape(group_size, slot_cap, feat_width))
    aggregate = jax.ops.segment_sum(
        arrived.reshape(group_size * slot_cap, feat_width).astype(jnp.float32),
        serve_flat,
        num_segments=link_count,
    )
    agg_bf = aggregate.astype(jnp.bfloat16)
    keep_col = (1 - failed[0]).astype(jnp.float32)[:, None]
    link_out, pre_act, activ = link_forward(
        link_rows, agg_bf, keep_col, mlp_w1, mlp_b1, mlp_w2, mlp_b2
    )
    path_out = states[-1].astype(jnp.bfloat16)
    link_direct, agg_grad, mlp_terms = link_backward(
        link_grad[0], link_rows, agg_bf, keep_col, pre_act, activ, mlp_w1, mlp_w2
    )
    returned = swap_slots(jnp.take(agg_grad, serve_rows, axis=0))
    hop_grads = (
        jnp.take(returned.reshape(group_size * slot_cap, feat_width), slot_ids, axis=0).astype(
            jnp.float32
        )
        * live_mask[:, :, None]
    )
    finished, grad_inputs = gru_backward(
        path_in[0], states, hop_inputs, live_mask, hop_grads, path_grad[0], gru_wx, gru_wh, gru_bias
    )
    dpart = jax.ops.segment_sum(
        grad_inputs.reshape(hop_count * flow_count, feat_width),
        flat_slots,
        num_segments=group_size * slot_cap,
    ).astype(jnp.bfloat16)
    owned = swap_slots(dpart.reshape(group_size, slot_cap, feat_width))
    link_back = link_direct + jax.ops.segment_sum(
        owned.reshape(group_size * slot_cap, feat_width).astype(jnp.float32),
        serve_flat,
        num_segments=link_count,
    )
    summed = lax.psum(
        (
            finished[1],
            finished[2],
            finished[3],
            mlp_terms[0],
            mlp_terms[1],
            mlp_terms[2],
            mlp_terms[3],
        ),
        ("replica", "outer", "link"),
    )
    device_count = lax.axis_size("replica") * lax.axis_size("outer") * lax.axis_size("link")
    grad_scale = float(device_count * link_count) ** (-0.5)
    return (
        link_out[None],
        path_out[None],
        link_back[None],
        finished[0][None],
        summed[0] * grad_scale,
        summed[1] * grad_scale,
        summed[2] * grad_scale,
        summed[3] * grad_scale,
        summed[4] * grad_scale,
        summed[5] * grad_scale,
        summed[6] * grad_scale,
    )


def solution(mesh):
    return jax.shard_map(
        body,
        mesh=mesh,
        in_specs=(
            P("replica", ("outer", "link"), None),
            P("replica", ("outer", "link"), None),
            P("replica", ("outer", "link"), None),
            P("replica", ("outer", "link")),
            P("replica", ("outer", "link")),
            P("replica", None, ("outer", "link"), None),
            P("replica", ("outer", "link"), None),
            P("replica", ("outer", "link"), None),
            P(),
            P(),
            P(),
            P(),
            P(),
            P(),
            P(),
        ),
        out_specs=(
            P("replica", ("outer", "link"), None),
            P("replica", ("outer", "link"), None),
            P("replica", ("outer", "link"), None),
            P("replica", ("outer", "link"), None),
            P(),
            P(),
            P(),
            P(),
            P(),
            P(),
            P(),
        ),
        check_vma=False,
    )
```

profile of v0, /device:TPU:2, one launch (start us, length us, event | category | flops | bytes accessed | tf_op | source)
XLA Modules:
  0.0 706.7 jit_solution(12861078215785412026)
XLA Ops:
  8.8 7.6 %gather_fusion = bf16[2048,256]{1,0:T(8,128)(2,1)S(1)} fusion(bf16[512,256]{1,0:T(8,128)(2,1)} %bitcast.135, s32[2048]{0:T(1024)S(1)} %broadcast_clamp_fusion), kind=kCustom, calls=%fused_computation.clone | custom fusion | bytes 2105344 | tf_op jit(solution)/shard_map/jit(_take)/gather | solution.py:187
  16.4 1.2 broadcast_select_fusion.2
  17.7 11.5 %all-to-all-start = ((bf16[32,64,256]{2,1,0:T(8,128)(2,1)}), bf16[32,64,256]{2,1,0:T(8,128)(2,1)S(1)}, u32[]{:S(2)}, u32[]{:S(2)}) async-start(bf16[32,64,256]{2,1,0:T(8,128)(2,1)} %broadcast_select_fusion.2), calls=%async_computation | async-start | bytes 2097152 | tf_op jit(solution)/shard_map/all_to_all | solution.py:155
  29.9 27.9 %all-to-all-done = bf16[32,64,256]{2,1,0:T(8,128)(2,1)S(1)} async-done(((bf16[32,64,256]{2,1,0:T(8,128)(2,1)}), bf16[32,64,256]{2,1,0:T(8,128)(2,1)S(1)}, u32[]{:S(2)}, u32[]{:S(2)}) %all-to-all-start) | async-done | bytes 1048608 | tf_op jit(solution)/shard_map/all_to_all | solution.py:155
  57.8 13.0 %gather_fusion.1 = bf16[3072,256]{1,0:T(8,128)(2,1)} fusion(bf16[2048,256]{1,0:T(8,128)(2,1)S(1)} %bitcast.137, s32[3072]{0:T(1024)S(1)} %bitcast_clamp_fusion), kind=kCustom, calls=%fused_computation.1.clone | custom fusion | bytes 3158016 | tf_op jit(solution)/shard_map/jit(_take)/gather | solution.py:188
  70.7 1.7 broadcast_select_fusion
  72.5 2.0 broadcast.84.clone
  74.6 29.4 %while.35 = (s32[]{:T(128)}, f32[128,256]{1,0:T(8,128)S(1)}, f32[24,128,256]{2,1,0:T(8,128)}, f32[24,128]{1,0:T(8,128)S(1)}, bf16[24,128,256]{2,1,0:T(8,128)(2,1...) while((s32[]{:T(128)}, f32[128,256]{1,0:T(8,128)S(1)}, ...), condition=%wide.region_1.4_spmd, body=%wide.region_0.3_spmd.sunk | while | flops 101253248 | bytes 2954097 | solution.py:36
  104.0 4.6 broadcast_multiply_fusion
  108.5 17.9 %scatter_custom_fusion = f32[2048,256]{1,0:T(8,128)S(1)} fusion(s32[3072]{0:T(1024)S(1)} %bitcast.155, f32[3072,256]{1,0:T(8,128)} %bitcast.148, f32[]{:T(128)} %constant.108.clone.1), kind=kCustom, calls=%fused_computation.102 | custom fusion | flops 786432 | bytes 2097664 | tf_op jit(solution)/shard_map/scatter-add | solution.py:190
  127.6 5.2 all-to-all-start.1
  135.5 25.6 %all-to-all-done.1 = bf16[32,64,256]{2,1,0:T(8,128)(2,1)S(1)} async-done(((bf16[32,64,256]{2,1,0:T(8,128)(2,1)}), bf16[32,64,256]{2,1,0:T(8,128)(2,1)S(1)}, u32[]{:S(2)}, u32[]{:S(2)}) %all-to-all-start.1) | async-done | bytes 1048608 | tf_op jit(solution)/shard_map/all_to_all | solution.py:155
  161.1 11.9 %scatter_custom_fusion.1 = f32[512,256]{1,0:T(8,128)S(1)} fusion(s32[2048]{0:T(1024)} %reshape.174, bf16[2048,256]{1,0:T(8,128)(2,1)S(1)} %bitcast.146, f32[]{:T(128)} %constant.108.clone.1), kind=kCustom, calls=%fused_computation.84 | custom fusion | flops 1048576 | bytes 1573376 | tf_op jit(solution)/shard_map/scatter-add | solution.py:196
  173.9 2.1 fusion.85
  177.0 7.5 %gather_fusion.2 = bf16[2048,256]{1,0:T(8,128)(2,1)S(1)} fusion(bf16[512,256]{1,0:T(8,128)(2,1)S(1)} %convolution_convert_fusion, s32[2048]{0:T(1024)S(1)} %broadcast_clamp_fusion), kind=kCustom, calls=%fused_computation.2.clone | custom fusion | bytes 2105344 | tf_op jit(solution)/shard_map/jit(_take)/gather | solution.py:210
  184.5 1.2 broadcast_select_fusion.1
  185.7 4.9 all-to-all-start.2
  192.7 1.5 bitcast_convert_fusion.3
  194.2 2.1 slice.91
  196.4 1.8 pad_maximum_fusion.1
  200.7 18.2 %all-to-all-done.2 = bf16[32,64,256]{2,1,0:T(8,128)(2,1)S(1)} async-done(((bf16[32,64,256]{2,1,0:T(8,128)(2,1)}), bf16[32,64,256]{2,1,0:T(8,128)(2,1)S(1)}, u32[]{:S(2)}, u32[]{:S(2)}) %all-to-all-start.2) | async-done | bytes 1048608 | tf_op jit(solution)/shard_map/all_to_all | solution.py:155
  218.9 12.9 %gather_fusion.3 = bf16[3072,256]{1,0:T(8,128)(2,1)} fusion(bf16[2048,256]{1,0:T(8,128)(2,1)S(1)} %bitcast.136, s32[3072]{0:T(1024)S(1)} %copy-done.32), kind=kCustom, calls=%fused_computation.3.clone | custom fusion | bytes 3158016 | tf_op jit(solution)/shard_map/jit(_take)/gather | solution.py:212
  231.9 4.1 convert_multiply_fusion
  236.0 2.1 broadcast.84
  238.1 176.1 %while.36 = (s32[]{:T(128)}, f32[128,256]{1,0:T(8,128)S(1)}, f32[256,768]{1,0:T(8,128)S(1)}, f32[256,768]{1,0:T(8,128)S(1)}, f32[768]{0:T(1024)S(1)}, /*index=5*...) while((s32[]{:T(128)}, f32[128,256]{1,0:T(8,128)S(1)}, ...), condition=%wide.region_6.9_spmd.clone, body=%wide.region_4.8_spmd.clone.sunk | while | flops 306152320 | bytes 12996093 | solution.py:108
  242.0 1.3 convolution_add_fusion.15
  243.3 1.2 convolution_add_fusion.14
  249.3 1.3 convolution_add_fusion.15
  256.7 1.3 convolution_add_fusion.15
  264.0 1.3 convolution_add_fusion.15
  265.3 1.2 convolution_add_fusion.14
  271.3 1.3 convolution_add_fusion.15
  272.6 1.2 convolution_add_fusion.14
  278.6 1.3 convolution_add_fusion.15
  279.9 1.2 convolution_add_fusion.14
  286.0 1.3 convolution_add_fusion.15
  293.3 1.3 convolution_add_fusion.15
  294.6 1.2 convolution_add_fusion.14
  300.7 1.3 convolution_add_fusion.15
  308.0 1.3 convolution_add_fusion.15
  315.3 1.3 convolution_add_fusion.15
  316.6 1.2 convolution_add_fusion.14
  322.7 1.3 convolution_add_fusion.15
  324.0 1.2 convolution_add_fusion.14
  330.0 1.3 convolution_add_fusion.15
  337.4 1.3 convolution_add_fusion.15
  344.7 1.3 convolution_add_fusion.15
  352.0 1.3 convolution_add_fusion.15
  359.4 1.3 convolution_add_fusion.15
  366.7 1.3 convolution_add_fusion.15
  374.0 1.3 convolution_add_fusion.15
  381.4 1.3 convolution_add_fusion.15
  388.7 1.3 convolution_add_fusion.15
  396.0 1.3 convolution_add_fusion.15
  403.4 1.3 convolution_add_fusion.15
  410.7 1.3 convolution_add_fusion.15
  415.5 1.5 slice.215
  417.0 17.9 %scatter_custom_fusion.2 = f32[2048,256]{1,0:T(8,128)S(1)} fusion(s32[3072]{0:T(1024)} %bitcast.154, f32[3072,256]{1,0:T(8,128)} %bitcast.147, f32[]{:T(128)} %constant.108.clone.1), kind=kCustom, calls=%fused_computation.100 | custom fusion | flops 786432 | bytes 2097664 | tf_op jit(solution)/shard_map/scatter-add | solution.py:220
  436.0 5.1 all-to-all-start.3
  442.4 76.8 %all-reduce = (f32[768]{0:T(1024)S(1)}, f32[256]{0:T(256)S(1)}, f32[256]{0:T(256)S(1)}) all-reduce(f32[768]{0:T(1024)S(1)} %get-tuple-element.357, f32[256]{0:T(256)S(1)} %copy-done.39, f32[256]{0:T(256)S(1)} %fusion.64), channel_id=1, replica_groups=mesh['replica'=8,'outer'=4,'link'=8] {'replica','outer','link'}, use_global_device_ids=true, to_apply=%region_11.14 | all-reduce | flops 1280 | bytes 10240 | tf_op jit(solution)/shard_map/psum | solution.py:231
  520.9 160.5 %all-reduce.4.cloned.1.call-done = (f32[256,768]{1,0:T(8,128)}, f32[256,768]{1,0:T(8,128)}, f32[512,256]{1,0:T(8,128)}, f32[256,256]{1,0:T(8,128)}) async-done(((f32[256,768]{1,0:T(8,128)}, f32[256,768]{1,0:T(8,128)}, f32[512,256]{1,0:T(8,128)}, f32[256,256]{1,0:T(8,128)}), (f32[256,768]{1,0:T(8,128)}, f32[256,768]{1,0:T(8,128)}, f32[512,256]{1,0:T(8,128)}, ...) | async-done | bytes 2359312 | tf_op jit(solution)/shard_map/psum | solution.py:231
  681.5 1.8 broadcast_multiply_fusion.4
  683.3 1.9 broadcast_multiply_fusion.3
  687.1 12.0 %scatter_custom_fusion.3 = f32[512,256]{1,0:T(8,128)S(1)} fusion(f32[512,256]{1,0:T(8,128)S(1)} %convolution_add_fusion.5, s32[2048]{0:T(1024)} %reshape.174, bf16[2048,256]{1,0:T(8,128)(2,1)S(1)} %bitcast.145), kind=kCustom, calls=%fused_computation.82 | custom fusion | flops 1048576 | bytes 1572864 | tf_op jit(solution)/shard_map/scatter-add | solution.py:226
  (519 shorter events, 184.1 us)
Async XLA Ops:
  7.2 166.7 %copy-start = (bf16[256,256]{1,0:T(8,128)(2,1)S(1)}, bf16[256,256]{1,0:T(8,128)(2,1)}, u32[]{:S(2)}) copy-start(bf16[256,256]{1,0:T(8,128)(2,1)} %param.36) | copy-start | bytes 393220
  16.4 12.8 %copy-start.34 = (s32[1,128,24]{1,2,0:T(8,128)S(1)}, s32[1,128,24]{1,2,0:T(8,128)}, u32[]{:S(2)}) copy-start(s32[1,128,24]{1,2,0:T(8,128)} %param.25) | copy-start | bytes 36868
  16.4 12.8 %copy-start.40 = (s32[1,128]{1,0:T(1,128)S(1)}, s32[1,128]{1,0:T(1,128)}, u32[]{:S(2)}) copy-start(s32[1,128]{1,0:T(1,128)} %param.26) | copy-start | bytes 1540
  16.4 12.8 %copy-start.33 = (bf16[1,128,256]{2,1,0:T(8,128)(2,1)S(1)}, bf16[1,128,256]{2,1,0:T(8,128)(2,1)}, u32[]{:S(2)}) copy-start(bf16[1,128,256]{2,1,0:T(8,128)(2,1)} %param.24) | copy-start | bytes 196612
  17.7 40.1 %all-to-all-start = ((bf16[32,64,256]{2,1,0:T(8,128)(2,1)}), bf16[32,64,256]{2,1,0:T(8,128)(2,1)S(1)}, u32[]{:S(2)}, u32[]{:S(2)}) async-start(bf16[32,64,256]{2,1,0:T(8,128)(2,1)} %broadcast_select_fusion.2), calls=%async_computation | async-start | bytes 2097152 | tf_op jit(solution)/shard_map/all_to_all | solution.py:155
  29.2 41.6 %copy-start.31 = (s32[3072]{0:T(1024)}, s32[3072]{0:T(1024)S(1)}, u32[]{:S(2)}) copy-start(s32[3072]{0:T(1024)S(1)} %bitcast_clamp_fusion) | copy-start | bytes 36868
  29.2 41.5 %copy-start.35 = (pred[24,128]{1,0:T(8,128)(4,1)}, pred[24,128]{1,0:T(8,128)(4,1)S(1)}, u32[]{:S(2)}) copy-start(pred[24,128]{1,0:T(8,128)(4,1)S(1)} %get-tuple-element.474) | copy-start | bytes 9220
  72.5 2.1 copy-start.2
  72.5 2.1 copy-start.3
  72.5 2.1 copy-start.25
  104.0 4.6 copy-start.12
  104.0 4.6 copy-start.29
  126.5 8.8 %copy-start.1 = (bf16[1,512,256]{2,1,0:T(8,128)(2,1)S(1)}, bf16[1,512,256]{2,1,0:T(8,128)(2,1)}, u32[]{:S(2)}) copy-start(bf16[1,512,256]{2,1,0:T(8,128)(2,1)} %param.23) | copy-start | bytes 786436
  126.5 8.8 %copy-start.13 = (bf16[512,256]{1,0:T(8,128)(2,1)S(1)}, bf16[512,256]{1,0:T(8,128)(2,1)}, u32[]{:S(2)}) copy-start(bf16[512,256]{1,0:T(8,128)(2,1)} %param.34) | copy-start | bytes 786436
  127.6 5.8 copy-start.28
  127.6 7.1 %copy-start.38 = (s32[1,512]{1,0:T(1,128)S(1)}, s32[1,512]{1,0:T(1,128)}, u32[]{:S(2)}) copy-start(s32[1,512]{1,0:T(1,128)} %param.27) | copy-start | bytes 6148
  127.6 45.4 %copy-start.14 = (bf16[512,256]{1,0:T(8,128)(2,1)S(1)}, bf16[512,256]{1,0:T(8,128)(2,1)}, u32[]{:S(2)}) copy-start(bf16[512,256]{1,0:T(8,128)(2,1)} %param.34) | copy-start | bytes 786436
  127.6 33.5 %all-to-all-start.1 = ((bf16[32,64,256]{2,1,0:T(8,128)(2,1)}), bf16[32,64,256]{2,1,0:T(8,128)(2,1)S(1)}, u32[]{:S(2)}, u32[]{:S(2)}) async-start(bf16[32,64,256]{2,1,0:T(8,128)(2,1)} %bitcast.142), calls=%async_computation.1 | async-start | bytes 2097152 | tf_op jit(solution)/shard_map/all_to_all | solution.py:155
  173.9 2.1 copy-start.20
  185.7 33.2 %all-to-all-start.2 = ((bf16[32,64,256]{2,1,0:T(8,128)(2,1)}), bf16[32,64,256]{2,1,0:T(8,128)(2,1)S(1)}, u32[]{:S(2)}, u32[]{:S(2)}) async-start(bf16[32,64,256]{2,1,0:T(8,128)(2,1)} %broadcast_select_fusion.1), calls=%async_computation.2 | async-start | bytes 2097152 | tf_op jit(solution)/shard_map/all_to_all | solution.py:155
  190.6 490.8 %all-reduce.4.cloned.1.call-start = ((), (), s32[]{:S(2)}) async-start(), calls=%async_computation.4 | async-start | bytes 4718592 | tf_op jit(solution)/shard_map/psum | solution.py:231
  194.2 2.1 copy-start.23
  196.3 1.8 copy-start.10
  198.2 1.4 copy-start.16
  198.2 1.4 copy-start.21
  198.2 1.4 copy-start.37
  198.8 20.2 %copy-start.32 = (s32[3072]{0:T(1024)S(1)}, s32[3072]{0:T(1024)}, u32[]{:S(2)}) copy-start(s32[3072]{0:T(1024)} %copy-done.31) | copy-start | bytes 36868
  218.9 12.9 %copy-start.30 = (f32[24,128]{1,0:T(8,128)S(1)}, f32[24,128]{1,0:T(8,128)}, u32[]{:S(2)}) copy-start(f32[24,128]{1,0:T(8,128)} %copy-done.29) | copy-start | bytes 36868
  218.9 13.0 %copy-start.36 = (pred[24,128]{1,0:T(8,128)(4,1)S(1)}, pred[24,128]{1,0:T(8,128)(4,1)}, u32[]{:S(2)}) copy-start(pred[24,128]{1,0:T(8,128)(4,1)} %copy-done.35) | copy-start | bytes 9220
  236.0 2.1 copy-start.5
  236.0 2.1 copy-start.7
  236.0 2.1 copy-start.26
  239.2 2.4 copy-start.27
  246.6 2.4 copy-start.27
  253.9 2.4 copy-start.27
  261.2 2.4 copy-start.27
  268.6 2.4 copy-start.27
  275.9 2.4 copy-start.27
  283.2 2.4 copy-start.27
  290.6 2.4 copy-start.27
  297.9 2.4 copy-start.27
  305.2 2.4 copy-start.27
  312.6 2.4 copy-start.27
  319.9 2.4 copy-start.27
  327.2 2.4 copy-start.27
  334.6 2.4 copy-start.27
  341.9 2.4 copy-start.27
  349.3 2.4 copy-start.27
  356.6 2.4 copy-start.27
  363.9 2.4 copy-start.27
  371.3 2.4 copy-start.27
  378.6 2.4 copy-start.27
  385.9 2.4 copy-start.27
  393.3 2.4 copy-start.27
  400.6 2.4 copy-start.27
  407.9 2.4 copy-start.27
  414.1 20.8 %copy-start.8 = (f32[128,256]{1,0:T(8,128)}, f32[128,256]{1,0:T(8,128)S(1)}, u32[]{:S(2)}) copy-start(f32[128,256]{1,0:T(8,128)S(1)} %get-tuple-element.354) | copy-start | bytes 393220
  434.9 6.2 copy-start.41
  436.0 5.1 copy-start.22
  436.0 6.1 copy-start.11
  436.0 6.1 copy-start.15
  436.0 251.0 %all-to-all-start.3 = ((bf16[32,64,256]{2,1,0:T(8,128)(2,1)}), bf16[32,64,256]{2,1,0:T(8,128)(2,1)S(1)}, u32[]{:S(2)}, u32[]{:S(2)}) async-start(bf16[32,64,256]{2,1,0:T(8,128)(2,1)} %bitcast.141), calls=%async_computation.3 | async-start | bytes 2097152 | tf_op jit(solution)/shard_map/all_to_all | solution.py:155
  681.5 3.7 copy-start.19
  681.5 4.6 copy-start.18
  (6 other events, 6.0 us)
Sparse Core Ops, SparseCore 0:
  415.4 265.9 all-reduce.3
where the time goes:
time: 711 us; the launch traced here: 707 us
  waiting for transfers between devices  232 us (33%)
  matrix products  158 us (22%)
  other arithmetic  141 us (20%)
  blocking collectives  76.8 us (11%)
  local copies, waits for them, and re-layouts  54.8 us (8%)
  starting transfers between devices  26.9 us (4%)
  between operations  14.5 us (2%)
    psum x1, waiting for transfers between devices, body(): lax.psum((finished[1], finished[2], finished[3], mlp_terms[0], mlp_terms[...  161 us
    psum x1, blocking collectives, body(): lax.psum((finished[1], finished[2], finished[3], mlp_terms[0], mlp_terms[...  76.8 us
    all_to_all x4, waiting for transfers between devices, swap_slots(): lax.all_to_all(blocks, ('outer', 'link'), split_axis=0, concat_axis=0, ti...  71.6 us
    dot_general x48, matrix products, gate_terms(): jnp.dot(hop_input, input_weight, preferred_element_type=jnp.float32)  31.8 us
    dot_general x48, matrix products, gate_terms(): jnp.dot(state_now.astype(jnp.bfloat16), hidden_weight, preferred_element_...  31.7 us
    dot_general x24, matrix products, back_step(): jnp.dot(state_now.astype(jnp.bfloat16).T, hid_bf, preferred_element_type=...  31 us
    dot_general x24, matrix products, back_step(): jnp.dot(hop_input.T, in_bf, preferred_element_type=jnp.float32)  29.4 us
    all_to_all x4, starting transfers between devices, swap_slots(): lax.all_to_all(blocks, ('outer', 'link'), split_axis=0, concat_axis=0, ti...  26.7 us
  transfers between devices with their start and end apart: 5, of which 4 were waited for; matrix products, arithmetic and copies ran while one was open for 6% of the time, Pallas kernels for 0%

commit v1 on v0

v1 whole, which is shorter than its diff:
```python
import jax
import jax.numpy as jnp
from jax import lax
from jax.experimental import pallas as pl
from jax.experimental.pallas import tpu as pltpu
from jax.sharding import PartitionSpec as P

F32 = jnp.float32
BF = jnp.bfloat16
INTERPRET = False
OL = ("outer", "link")


def dot(a, b):
    return jnp.dot(a, b, preferred_element_type=F32)


def dot_nt(a, b):
    return lax.dot_general(a, b, (((1,), (1,)), ((), ())), preferred_element_type=F32)


def dot_tn(a, b):
    return lax.dot_general(a, b, (((0,), (0,)), ((), ())), preferred_element_type=F32)


def sigmoid(v):
    return 0.5 * jnp.tanh(0.5 * v) + 0.5


def pick_cols(col, width):
    lanes = lax.broadcasted_iota(jnp.int32, (col.shape[0], width), 1)
    return jnp.where(lanes == col, 1.0, 0.0).astype(BF)


def pick_rows(row, height, base=0):
    subs = lax.broadcasted_iota(jnp.int32, (height, row.shape[1]), 0) + base
    return jnp.where(subs == row, 1.0, 0.0).astype(BF)


def call(kernel, outs, **kw):
    return pl.pallas_call(kernel, out_shape=outs, interpret=INTERPRET, **kw)


def sds(shape, dtype):
    return jax.ShapeDtypeStruct(shape, dtype)


def gather_rows(table, serve_col, out_ref, per=8):
    cap, group = serve_col.shape
    links = table.shape[0]
    for o in range(0, group, per):
        sel = jnp.concatenate(
            [pick_cols(serve_col[:, k : k + 1], links) for k in range(o, o + per)], axis=0
        )
        out_ref[o * cap : (o + per) * cap, :] = dot(sel, table).astype(BF)


def serve_kernel(table_ref, col_ref, out_ref):
    gather_rows(table_ref[...], col_ref[...], out_ref)


def fetch_hops(table_ref, slot_ref, out_ref, per=4):
    flows, hops = slot_ref.shape
    slots = table_ref.shape[0]
    table = table_ref[...]
    cols = slot_ref[...]
    for t in range(0, hops, per):
        sel = jnp.concatenate(
            [pick_cols(cols[:, k : k + 1], slots) for k in range(t, t + per)], axis=0
        )
        rows = dot(sel, table).astype(out_ref.dtype)
        for k in range(per):
            out_ref[t + k] = rows[k * flows : (k + 1) * flows]


def sum_slots(row_ref, rows, out_ref, block=512):
    hops = row_ref.shape[0]
    slots = out_ref.shape[0]
    idx = row_ref[...]
    for q in range(0, slots, block):
        sel = jnp.concatenate([pick_rows(idx[t : t + 1, :], block, q) for t in range(hops)], axis=1)
        out_ref[q : q + block, :] = dot(sel, rows).astype(BF)


def forward_kernel(
    table_ref, slot_ref, row_ref, lens_ref, path_ref, wx_ref, wh_ref, bias_ref,
    x_ref, state_ref, part_ref, pathout_ref, gi_ref, hb_ref,
):
    hops, flows, width = x_ref.shape
    fetch_hops(table_ref, slot_ref, x_ref)
    per = 4
    for t in range(0, hops, per):
        rows = x_ref[t : t + per].reshape(per * flows, width)
        gi = dot(rows, wx_ref[...]) + bias_ref[...]
        gi_ref[t : t + per] = gi.reshape(per, flows, 3 * width)
    lens = lens_ref[...]

    def step(t, h):
        state_ref[t] = h
        gs = dot(h.astype(BF), wh_ref[...])
        gi = gi_ref[t]
        z = sigmoid(gi[:, :width] + gs[:, :width])
        r = sigmoid(gi[:, width : 2 * width] + gs[:, width : 2 * width])
        n = jnp.tanh(gi[:, 2 * width :] + r * gs[:, 2 * width :])
        h = jnp.where(t < lens, n + z * (h - n), h)
        hb_ref[t] = h.astype(BF)
        return h

    h = lax.fori_loop(0, hops, step, path_ref[...].astype(F32), unroll=2)
    pathout_ref[...] = h.astype(BF)
    sum_slots(row_ref, hb_ref[...].reshape(hops * flows, width), part_ref)


def coef_kernel(x_ref, state_ref, lens_ref, wx_ref, wh_ref, bias_ref, coef_ref):
    per, flows, width = x_ref.shape
    first = pl.program_id(0) * per
    rows = x_ref[...].reshape(per * flows, width)
    gi = dot(rows, wx_ref[...]) + bias_ref[...]
    h = state_ref[...].reshape(per * flows, width)
    gs = dot(h.astype(BF), wh_ref[...])
    z = sigmoid(gi[:, :width] + gs[:, :width])
    r = sigmoid(gi[:, width : 2 * width] + gs[:, width : 2 * width])
    gs3 = gs[:, 2 * width :]
    n = jnp.tanh(gi[:, 2 * width :] + r * gs3)
    cz = (h - n) * z * (1.0 - z)
    cn = (1.0 - z) * (1.0 - n * n)
    cr = cn * gs3 * r * (1.0 - r)
    for k in range(per):
        live = (first + k) < lens_ref[...]
        s = slice(k * flows, (k + 1) * flows)
        coef_ref[k, 0] = jnp.where(live, z[s], 1.0)
        coef_ref[k, 1] = jnp.where(live, cz[s], 0.0)
        coef_ref[k, 2] = jnp.where(live, cr[s], 0.0)
        coef_ref[k, 3] = jnp.where(live, cn[s], 0.0)
        coef_ref[k, 4] = r[s]


def link_kernel(
    got_ref, srow_ref, scol_ref, link_ref, lgrad_ref, keep_ref, w1_ref, b1_ref, w2_ref,
    out_ref, agg_ref, act_ref, du_ref, db1_ref,
):
    links, width = link_ref.shape
    sel = jnp.concatenate(
        [pick_rows(srow_ref[k : k + 1, :], links) for k in range(srow_ref.shape[0])], axis=1
    )
    agg = dot(sel, got_ref[...]).astype(BF)
    agg_ref[...] = agg
    u = dot(link_ref[...], w1_ref[:width, :]) + dot(agg, w1_ref[width:, :]) + b1_ref[...]
    s = sigmoid(u)
    act_ref[...] = (u * s).astype(BF)
    gv = (keep_ref[...] * lgrad_ref[...].astype(F32)).astype(BF)
    du = dot_nt(gv, w2_ref[...]) * s * (1.0 + u * (1.0 - s))
    db1_ref[...] = jnp.sum(du, axis=0, keepdims=True)
    du = du.astype(BF)
    du_ref[...] = du
    dagg = dot_nt(du, w1_ref[width:, :]).astype(BF)
    gather_rows(dagg, scol_ref[...], out_ref)


def link_rest_kernel(
    link_ref, lgrad_ref, keep_ref, agg_ref, act_ref, du_ref, db1_ref, w1_ref, w2_ref, b2_ref,
    lout_ref, direct_ref, pack_ref,
):
    _, width = link_ref.shape
    link = link_ref[...]
    keep = keep_ref[...]
    act = act_ref[...]
    du = du_ref[...]
    value = link.astype(F32) + dot(act, w2_ref[...]) + b2_ref[...]
    lout_ref[...] = (keep * value).astype(BF)
    gv = keep * lgrad_ref[...].astype(F32)
    direct_ref[...] = gv + dot_nt(du, w1_ref[:width, :])
    pack_ref[0:width, :] = dot_tn(link, du).astype(BF)
    pack_ref[width : 2 * width, :] = dot_tn(agg_ref[...], du).astype(BF)
    pack_ref[2 * width : 3 * width, :] = dot_tn(act, gv.astype(BF)).astype(BF)
    db2 = jnp.sum(gv, axis=0, keepdims=True)
    tail = jnp.concatenate([db1_ref[...], db2, jnp.zeros((14, width), F32)], axis=0)
    pack_ref[3 * width :, :] = tail.astype(BF)


def backward_kernel(
    table_ref, slot_ref, row_ref, pgrad_ref, wx_ref, wh_ref, coef_hbm,
    part_ref, pathgrad_ref, dgi_ref, dgs_ref, db_ref,
    hg_ref, coef_ref, dx_ref, sem,
):
    hops, flows, width = hg_ref.shape

    def load(t):
        return pltpu.make_async_copy(coef_hbm.at[t], coef_ref.at[t], sem.at[t])

    for t in range(hops - 1, -1, -1):
        load(t).start()
    fetch_hops(table_ref, slot_ref, hg_ref)
    db_ref[...] = jnp.zeros(db_ref.shape, F32)

    def fold(v):
        return jnp.sum(v.reshape(flows // 8, 8, width), axis=0)

    def step(k, g):
        t = hops - 1 - k
        load(t).wait()
        g = g + hg_ref[t].astype(F32)
        az = g * coef_ref[t, 1]
        ar = g * coef_ref[t, 2]
        an = g * coef_ref[t, 3]
        azb = az.astype(BF)
        arb = ar.astype(BF)
        anr = (an * coef_ref[t, 4]).astype(BF)
        dgs = jnp.concatenate([azb, arb, anr], axis=1)
        nxt = g * coef_ref[t, 0] + dot_nt(dgs, wh_ref[...])
        dgs_ref[t] = dgs
        dgi_ref[t] = jnp.concatenate([azb, arb, an.astype(BF)], axis=1)
        db_ref[:, :width] += fold(az)
        db_ref[:, width : 2 * width] += fold(ar)
        db_ref[:, 2 * width :] += fold(an)
        return nxt

    g = lax.fori_loop(0, hops, step, pgrad_ref[...].astype(F32), unroll=2)
    pathgrad_ref[...] = g
    per = 4
    for t in range(0, hops, per):
        rows = dgi_ref[t : t + per].reshape(per * flows, 3 * width)
        dx_ref[t * flows : (t + per) * flows, :] = dot_nt(rows, wx_ref[...]).astype(BF)
    sum_slots(row_ref, dx_ref[...], part_ref)


def weight_kernel(x_ref, state_ref, dgi_ref, dgs_ref, db_ref, mlp_ref, pack_ref, awx_ref, awh_ref):
    per, flows, width = x_ref.shape
    i = pl.program_id(0)
    x = x_ref[...].reshape(per * flows, width)
    h = state_ref[...].reshape(per * flows, width).astype(BF)
    gx = dot_tn(x, dgi_ref[...].reshape(per * flows, 3 * width))
    gh = dot_tn(h, dgs_ref[...].reshape(per * flows, 3 * width))

    @pl.when(i == 0)
    def _():
        awx_ref[...] = gx
        awh_ref[...] = gh

    @pl.when(i > 0)
    def _():
        awx_ref[...] += gx
        awh_ref[...] += gh

    @pl.when(i == pl.num_programs(0) - 1)
    def _():
        for k in range(3):
            s = slice(k * width, (k + 1) * width)
            pack_ref[k * width : (k + 1) * width, :] = awx_ref[:, s].astype(BF)
            pack_ref[(3 + k) * width : (4 + k) * width, :] = awh_ref[:, s].astype(BF)
        base = 9 * width
        pack_ref[6 * width : base + 16, :] = mlp_ref[...]
        b = jnp.sum(db_ref[...], axis=0, keepdims=True)
        tail = jnp.concatenate(
            [b[:, k * width : (k + 1) * width] for k in range(3)] + [jnp.zeros((13, width), F32)],
            axis=0,
        )
        pack_ref[base + 16 : base + 32, :] = tail.astype(BF)
        rest = pack_ref.shape[0] - base - 32
        pack_ref[base + 32 :, :] = jnp.zeros((rest, width), BF)


def finish_kernel(got_ref, srow_ref, direct_ref, out_ref):
    links = direct_ref.shape[0]
    sel = jnp.concatenate(
        [pick_rows(srow_ref[k : k + 1, :], links) for k in range(srow_ref.shape[0])], axis=1
    )
    out_ref[...] = direct_ref[...] + dot(sel, got_ref[...])


def swap(blocks, axes=OL, groups=None):
    return lax.all_to_all(
        blocks, axes, split_axis=0, concat_axis=0, tiled=True, axis_index_groups=groups
    )


def swap_named(rows, group):
    return swap(rows.reshape(group, -1, rows.shape[1])).reshape(rows.shape)


def total(v):
    return jnp.sum(v.astype(F32), axis=0).astype(BF)


def pair_kernel(place_ref, pack_ref, got_ref, *out_refs):
    x = place_ref[0]
    core = place_ref[1]
    chips = got_ref.shape[0]
    for k in range(chips):
        c = lax.rem(x + k, chips)
        both = pack_ref[core * chips + c].astype(F32) + got_ref[c].astype(F32)
        out_refs[k][...] = both.astype(BF)


def unpack_kernel(place_ref, *refs, scale):
    x = place_ref[0]
    core = place_ref[1]
    chips = (len(refs) - 8) // 2
    mine = refs[:chips]
    got = refs[chips : 2 * chips]
    wx_ref, wh_ref, bias_ref, w1_ref, b1_ref, w2_ref, b2_ref, all_ref = refs[2 * chips :]
    rows, width = mine[0].shape
    for k in range(chips):
        c = lax.rem(x - k + chips, chips)
        all_ref[pl.ds(pl.multiple_of((core * chips + c) * rows, 64), rows), :] = mine[k][...]
        all_ref[pl.ds(pl.multiple_of(((1 - core) * chips + c) * rows, 64), rows), :] = got[k][...]
    take = lambda a, n: all_ref[a : a + n, :].astype(F32) * scale
    for k in range(3):
        s = slice(k * width, (k + 1) * width)
        wx_ref[:, s] = take(k * width, width)
        wh_ref[:, s] = take((3 + k) * width, width)
    w1_ref[...] = take(6 * width, 2 * width)
    w2_ref[...] = take(8 * width, width)
    tail = take(9 * width, 32)
    b1_ref[...] = tail[0:1]
    b2_ref[...] = tail[1:2]
    for k in range(3):
        bias_ref[:, k * width : (k + 1) * width] = tail[16 + k : 17 + k]


def sum_everywhere(pack, scale):
    rows, width = pack.shape
    reps = lax.axis_size("replica")
    group = lax.axis_size("outer") * lax.axis_size("link")
    rep = lax.axis_index("replica")
    chips = reps // 2
    part = rows // reps
    place = jnp.stack([rep // 2, rep % 2]).astype(jnp.int32)
    pairs = [(i, i ^ 1) for i in range(reps)]
    ahead = [[(i, (i + 2 * k) % reps) for i in range(reps)] for k in range(chips)]
    halves = pack.reshape(2, rows // 2, width)
    smem = pl.BlockSpec(memory_space=pltpu.SMEM)
    vmem = pl.BlockSpec(memory_space=pltpu.VMEM)
    other = jnp.where(rep % 2 == 0, halves[1], halves[0])
    got = lax.ppermute(other, "replica", pairs)
    mine = call(
        pair_kernel, (sds((part, width), BF),) * chips, in_specs=[smem, vmem, vmem]
    )(place, pack.reshape(reps, part, width), got.reshape(chips, part, width))
    got = [lax.ppermute(mine[k], "replica", ahead[k]) for k in range(1, chips)]
    mine = sum((g.astype(F32) for g in got), mine[0].astype(F32)).astype(BF)
    mine = total(swap(mine.reshape(group, part // group, width)))
    mine = swap(jnp.broadcast_to(mine[None], (group,) + mine.shape)).reshape(part, width)
    mine = [mine] + [lax.ppermute(mine, "replica", ahead[k]) for k in range(1, chips)]
    got = [lax.ppermute(m, "replica", pairs) for m in mine]
    return call(
        lambda *refs: unpack_kernel(*refs, scale=scale),
        (
            sds((width, 3 * width), F32),
            sds((width, 3 * width), F32),
            sds((1, 3 * width), F32),
            sds((2 * width, width), F32),
            sds((1, width), F32),
            sds((width, width), F32),
            sds((1, width), F32),
        ),
        in_specs=[smem] + [vmem] * (2 * chips),
        scratch_shapes=[pltpu.VMEM((rows, width), BF)],
    )(place, *mine, *got)


def body(
    link_in, path_in, hop_slots, hop_lens, failed, serve_index, link_grad, path_grad,
    gru_wx, gru_wh, gru_bias, mlp_w1, mlp_b1, mlp_w2, mlp_b2,
):
    link_rows = link_in[0]
    links, width = link_rows.shape
    serve_rows = serve_index[0, :, 0, :]
    group, cap = serve_rows.shape
    slots = group * cap
    serve_col = serve_rows.T
    serve_row = serve_rows.reshape(slots // 128, 128)
    flows, hops = hop_slots.shape[1:]
    lens_col = hop_lens[0][:, None]
    slot_col = jnp.where(jnp.arange(hops, dtype=jnp.int32)[None, :] < lens_col, hop_slots[0], -1)
    slot_row = slot_col.T
    keep = (1 - failed[0]).astype(F32)[:, None]
    bias = gru_bias[None]
    wide = 3 * width

    sent = call(serve_kernel, sds((slots, width), BF))(link_rows, serve_col)
    fetched = swap_named(sent, group)
    x, states, part, path_out = call(
        forward_kernel,
        (
            sds((hops, flows, width), BF),
            sds((hops, flows, width), F32),
            sds((slots, width), BF),
            sds((flows, width), BF),
        ),
        scratch_shapes=[
            pltpu.VMEM((hops, flows, wide), F32),
            pltpu.VMEM((hops, flows, width), BF),
        ],
    )(fetched, slot_col, slot_row, lens_col, path_in[0], gru_wx, gru_wh, bias)
    arrived = swap_named(part, group)

    per = 4
    steps = lambda *tail: pl.BlockSpec((per,) + tail, lambda i: (i,) + (0,) * len(tail))
    whole = lambda *shape: pl.BlockSpec(shape, lambda i: (0,) * len(shape))
    coef = call(
        coef_kernel,
        sds((hops, 5, flows, width), F32),
        grid=(hops // per,),
        in_specs=[
            steps(flows, width),
            steps(flows, width),
            whole(flows, 1),
            whole(width, wide),
            whole(width, wide),
            whole(1, wide),
        ],
        out_specs=steps(5, flows, width),
    )(x, states, lens_col, gru_wx, gru_wh, bias)

    sent, agg, act, du, db1 = call(
        link_kernel,
        (
            sds((slots, width), BF),
            sds((links, width), BF),
            sds((links, width), BF),
            sds((links, width), BF),
            sds((1, width), F32),
        ),
    )(arrived, serve_row, serve_col, link_rows, link_grad[0], keep, mlp_w1, mlp_b1[None], mlp_w2)
    returned = swap_named(sent, group)
    link_out, direct, mlp_pack = call(
        link_rest_kernel,
        (
            sds((links, width), BF),
            sds((links, width), F32),
            sds((3 * width + 16, width), BF),
        ),
    )(link_rows, link_grad[0], keep, agg, act, du, db1, mlp_w1, mlp_w2, mlp_b2[None])

    vmem = pl.BlockSpec(memory_space=pltpu.VMEM)
    dpart, path_back, dgi, dgs, db = call(
        backward_kernel,
        (
            sds((slots, width), BF),
            sds((flows, width), F32),
            sds((hops, flows, wide), BF),
            sds((hops, flows, wide), BF),
            sds((8, wide), F32),
        ),
        in_specs=[vmem] * 6 + [pl.BlockSpec(memory_space=pl.ANY)],
        scratch_shapes=[
            pltpu.VMEM((hops, flows, width), BF),
            pltpu.VMEM((hops, 5, flows, width), F32),
            pltpu.VMEM((hops * flows, width), BF),
            pltpu.SemaphoreType.DMA((hops,)),
        ],
    )(returned, slot_col, slot_row, path_grad[0], gru_wx, gru_wh, coef)
    owned = swap_named(dpart, group)

    pack = call(
        weight_kernel,
        sds((10 * width, width), BF),
        grid=(hops // per,),
        in_specs=[
            steps(flows, width),
            steps(flows, width),
            steps(flows, wide),
            steps(flows, wide),
            whole(8, wide),
            whole(3 * width + 16, width),
        ],
        out_specs=whole(10 * width, width),
        scratch_shapes=[pltpu.VMEM((width, wide), F32), pltpu.VMEM((width, wide), F32)],
    )(x, states, dgi, dgs, db, mlp_pack)
    link_back = call(finish_kernel, sds((links, width), F32))(owned, serve_row, direct)

    count = lax.axis_size("replica") * lax.axis_size("outer") * lax.axis_size("link")
    scale = float(count * links) ** (-0.5)
    wx, wh, bias, w1, b1, w2, b2 = sum_everywhere(pack, scale)
    return (
        link_out[None],
        path_out[None],
        link_back[None],
        path_back[None],
        wx,
        wh,
        bias.reshape(wide),
        w1,
        b1.reshape(width),
        w2,
        b2.reshape(width),
    )


def solution(mesh):
    over = P("replica", OL, None)
    flat = P("replica", OL)

    return jax.shard_map(
        body,
        mesh=mesh,
        in_specs=(
            over, over, over, flat, flat, P("replica", None, OL, None), over, over,
            P(), P(), P(), P(), P(), P(), P(),
        ),
        out_specs=(over, over, over, over, P(), P(), P(), P(), P(), P(), P()),
        check_vma=False,
    )
```

time: 711 us -> 257 us (0.36)
  matrix products: 158 us -> 0 us
  waiting for transfers between devices: 232 us -> 90.6 us
  other arithmetic: 141 us -> 5.58 us
  Pallas kernels: 0 us -> 74.6 us
  blocking collectives: 76.8 us -> 32 us
  local copies, waits for them, and re-layouts: 54.8 us -> 11.1 us
  between operations: 14.5 us -> 0.94 us
  starting transfers between devices: 26.9 us -> 37.2 us
    psum x1 -> x0, waiting for transfers between devices: 161 us -> none  [body(): lax.psum((finished[1], finished[2], finished[3], mlp_terms[0], mlp_terms[...]
    dot_general x201 -> x0, matrix products: 158 us -> none  [the longest x48 31.8 us: gate_terms(): jnp.dot(hop_input, input_weight, preferred_element_type=jnp.float32)]
    psum x1 -> x0, blocking collectives: 76.8 us -> none  [body(): lax.psum((finished[1], finished[2], finished[3], mlp_terms[0], mlp_terms[...]
    pallas_call x0 -> x10, Pallas kernels: none -> 74.6 us  [the longest x1 19.5 us: body(): call(backward_kernel, (sds((slots, width), BF), sds((flows, width), F32),...]
    scatter-add x4 -> x0, other arithmetic: 59.7 us -> none  [the longest x1 17.9 us: body(): jax.ops.segment_sum(grad_inputs.reshape(hop_count * flow_count, feat_widt...]
    mul x81 -> x0, other arithmetic: 45 us -> none  [the longest x24 26.4 us: back_step(): pre_update = grad_state * (state_now - candidate) * update * (1.0 - update)]
    gather x4 -> x0, local copies, waits for them, and re-layouts: 41 us -> none  [the longest x1 13 us: body(): jnp.take(fetched.reshape(group_size * slot_cap, feat_width), slot_ids, ax...]
    all_to_all x0 -> x2, blocking collectives: none -> 32 us  [swap(): lax.all_to_all(blocks, axes, split_axis=0, concat_axis=0, tiled=True, axi...]
  transfers between devices with their start and end apart: 5 -> 15, of which waited for: 4 -> 12; matrix products, arithmetic and copies ran while one was open for 6% -> 3% of each run, Pallas kernels for 0% -> 6%
where the time goes in v1:
time: 257 us; the launch traced here: 252 us
  waiting for transfers between devices  90.6 us (35%)
  Pallas kernels  74.6 us (29%)
  starting transfers between devices  37.2 us (14%)
  blocking collectives  32 us (12%)
  local copies, waits for them, and re-layouts  11.1 us (4%)
  other arithmetic  5.58 us (2%)
    all_to_all x4, waiting for transfers between devices, swap(): lax.all_to_all(blocks, axes, split_axis=0, concat_axis=0, tiled=True, axi...  74.7 us
    all_to_all x2, blocking collectives, swap(): lax.all_to_all(blocks, axes, split_axis=0, concat_axis=0, tiled=True, axi...  32 us
    all_to_all x4, starting transfers between devices, swap(): lax.all_to_all(blocks, axes, split_axis=0, concat_axis=0, tiled=True, axi...  26.4 us
    pallas_call x1, Pallas kernels, body(): call(backward_kernel, (sds((slots, width), BF), sds((flows, width), F32),...  19.5 us
    pallas_call x1, Pallas kernels, body(): call(forward_kernel, (sds((hops, flows, width), BF), sds((hops, flows, wi...  15.9 us
    pallas_call x1, Pallas kernels, body(): call(coef_kernel, sds((hops, 5, flows, width), F32), grid=(hops // per,),...  10.5 us
    pallas_call x1, Pallas kernels, body(): call(weight_kernel, sds((10 * width, width), BF), grid=(hops // per,), in...  9.69 us
    unnamed x38, local copies, waits for them, and re-layouts  7.41 us
  transfers between devices with their start and end apart: 15, of which 12 were waited for; matrix products, arithmetic and copies ran while one was open for 3% of the time, Pallas kernels for 6%

profile of v1, /device:TPU:2, one launch (start us, length us, event | category | flops | bytes accessed | tf_op | source)
XLA Modules:
  0.0 252.1 jit_solution(16475708319605075877)
XLA Ops:
  0.7 1.4 copy.31
  2.1 2.8 %shard_map.230 = bf16[2048,256]{1,0:T(8,128)(2,1)} custom-call(bf16[512,256]{1,0:T(8,128)(2,1)} %bitcast.43, s32[64,32]{1,0:T(8,128)} %bitcast.52), custom_call_target="tpu_custom_call" | custom-call | tf_op jit(solution)/shard_map/pallas_call | solution.py:380
  4.9 11.6 %all-to-all-start = ((bf16[32,64,256]{2,1,0:T(8,128)(2,1)}), bf16[32,64,256]{2,1,0:T(8,128)(2,1)S(1)}, u32[]{:S(2)}, u32[]{:S(2)}) async-start(bf16[32,64,256]{2,1,0:T(8,128)(2,1)} %bitcast.42), calls=%async_computation | async-start | bytes 2097152 | tf_op jit(solution)/shard_map/all_to_all | solution.py:272
  16.5 0.7 copy.32.slot_ref
  17.2 0.7 copy.33.lens_ref
  18.0 0.6 broadcast_in_dim.34.bias_ref
  18.6 0.6 fusion.row_ref
  19.2 25.9 %all-to-all-done = bf16[32,64,256]{2,1,0:T(8,128)(2,1)S(1)} async-done(((bf16[32,64,256]{2,1,0:T(8,128)(2,1)}), bf16[32,64,256]{2,1,0:T(8,128)(2,1)S(1)}, u32[]{:S(2)}, u32[]{:S(2)}) %all-to-all-start) | async-done | bytes 1048608 | tf_op jit(solution)/shard_map/all_to_all | solution.py:272
  45.1 1.0 copy-done.3
  46.1 15.9 %shard_map.231 = (bf16[24,128,256]{2,1,0:T(8,128)(2,1)}, f32[24,128,256]{2,1,0:T(8,128)}, bf16[2048,256]{1,0:T(8,128)(2,1)}, bf16[128,256]{1,0:T(8,128)(2,1)}) custom-call(bf16[2048,256]{1,0:T(8,128)(2,1)} %bitcast.41, s32[128,24]{1,0:T(8,128)} %copy.32.slot_ref, s32[24,128]{1,0:T(8,128)} %fusion.row_ref, s32[128,1]{1,0:T(8,128)} %copy.33.lens_ref, ...), custom_call_target="tpu_custom_call" | custom-call | tf_op jit(solution)/shard_map/pallas_call | solution.py:382
  62.0 5.1 %all-to-all-start.1 = ((bf16[32,64,256]{2,1,0:T(8,128)(2,1)}), bf16[32,64,256]{2,1,0:T(8,128)(2,1)S(1)}, u32[]{:S(2)}, u32[]{:S(2)}) async-start(bf16[32,64,256]{2,1,0:T(8,128)(2,1)} %bitcast.47), calls=%async_computation.1 | async-start | bytes 2097152 | tf_op jit(solution)/shard_map/all_to_all | solution.py:272
  67.1 0.9 copy.35.keep_ref
  68.0 0.5 broadcast.16
  68.5 0.7 reduce.5
  69.2 0.7 reshape_squeeze.3.srow_ref
  69.8 25.5 %all-to-all-done.1 = bf16[32,64,256]{2,1,0:T(8,128)(2,1)S(1)} async-done(((bf16[32,64,256]{2,1,0:T(8,128)(2,1)}), bf16[32,64,256]{2,1,0:T(8,128)(2,1)S(1)}, u32[]{:S(2)}, u32[]{:S(2)}) %all-to-all-start.1) | async-done | bytes 1048608 | tf_op jit(solution)/shard_map/all_to_all | solution.py:272
  95.3 1.0 copy-done.2
  96.3 5.2 %shard_map.232 = (bf16[2048,256]{1,0:T(8,128)(2,1)}, bf16[512,256]{1,0:T(8,128)(2,1)}, bf16[512,256]{1,0:T(8,128)(2,1)}, bf16[512,256]{1,0:T(8,128)(2,1)}, f32[1,256]{1,0:T(1,128)}) custom-call(bf16[2048,256]{1,0:T(8,128)(2,1)} %bitcast.40, s32[16,128]{1,0:T(8,128)} %reshape_squeeze.3.srow_ref, s32[64,32]{1,0:T(8,128)} %bitcast.53, ...), custom_call_target="tpu_custom_call" | custom-call | tf_op jit(solution)/shard_map/pallas_call | solution.py:415
  101.6 5.1 %all-to-all-start.2 = ((bf16[32,64,256]{2,1,0:T(8,128)(2,1)}), bf16[32,64,256]{2,1,0:T(8,128)(2,1)S(1)}, u32[]{:S(2)}, u32[]{:S(2)}) async-start(bf16[32,64,256]{2,1,0:T(8,128)(2,1)} %bitcast.46), calls=%async_computation.2 | async-start | bytes 2097152 | tf_op jit(solution)/shard_map/all_to_all | solution.py:272
  106.7 10.5 %shard_map.234.coef_hbm = f32[24,5,128,256]{3,2,1,0:T(8,128)} custom-call(bf16[24,128,256]{2,1,0:T(8,128)(2,1)} %get-tuple-element.47.x_ref, f32[24,128,256]{2,1,0:T(8,128)} %get-tuple-element.48.state_ref, s32[128,1]{1,0:T(8,128)} %copy.33.lens_ref, bf16[256,768]{1,0:T(8,128)(2,1)} %wx_ref.5, bf16[256,768]{1,0:T(8,128)(2,1)} %wh_ref.5, ...), custom_call_target="tpu_custom_call" | custom-call | tf_op jit(solution)/shard_map/pallas_call | solution.py:400
  117.2 2.8 %shard_map.233 = (bf16[512,256]{1,0:T(8,128)(2,1)}, f32[512,256]{1,0:T(8,128)}, bf16[784,256]{1,0:T(8,128)(2,1)}) custom-call(bf16[512,256]{1,0:T(8,128)(2,1)} %bitcast.45, bf16[512,256]{1,0:T(8,128)(2,1)} %bitcast.49, f32[512,1]{1,0:T(8,128)} %copy.35.keep_ref, bf16[512,256]{1,0:T(8,128)(2,1)} %get-tuple-element.40.agg_ref, ...), custom_call_target="tpu_custom_call" | custom-call | tf_op jit(solution)/shard_map/pallas_call | solution.py:426
  120.0 14.8 %all-to-all-done.2 = bf16[32,64,256]{2,1,0:T(8,128)(2,1)S(1)} async-done(((bf16[32,64,256]{2,1,0:T(8,128)(2,1)}), bf16[32,64,256]{2,1,0:T(8,128)(2,1)S(1)}, u32[]{:S(2)}, u32[]{:S(2)}) %all-to-all-start.2) | async-done | bytes 1048608 | tf_op jit(solution)/shard_map/all_to_all | solution.py:272
  134.8 1.0 copy-done
  135.8 19.5 %shard_map.235 = (bf16[2048,256]{1,0:T(8,128)(2,1)}, f32[128,256]{1,0:T(8,128)}, bf16[24,128,768]{2,1,0:T(8,128)(2,1)}, bf16[24,128,768]{2,1,0:T(8,128)(2,1)}, f32[8,768]{1,0:T(8,128)}) custom-call(bf16[2048,256]{1,0:T(8,128)(2,1)} %bitcast.38, s32[128,24]{1,0:T(8,128)} %copy.32.slot_ref, s32[24,128]{1,0:T(8,128)} %fusion.row_ref, ...), custom_call_target="tpu_custom_call" | custom-call | tf_op jit(solution)/shard_map/pallas_call | solution.py:436
  155.3 9.7 %shard_map.237 = bf16[2560,256]{1,0:T(8,128)(2,1)} custom-call(bf16[24,128,256]{2,1,0:T(8,128)(2,1)} %get-tuple-element.47.x_ref, f32[24,128,256]{2,1,0:T(8,128)} %get-tuple-element.48.state_ref, bf16[24,128,768]{2,1,0:T(8,128)(2,1)} %get-tuple-element.52.dgi_ref, bf16[24,128,768]{2,1,0:T(8,128)(2,1)} %get-tuple-element.53.dgs_ref, ...), custom_call_target="tpu_custom_call" | custom-call | tf_op jit(solution)/shard_map/pallas_call | solution.py:455
  165.0 1.4 slice_select_fusion
  166.3 0.1 collective-permute-start
  166.4 0.6 pad_add_fusion.place_ref.refs_0_
  167.0 1.5 collective-permute-done
  168.5 0.8 copy-done.5
  169.3 2.4 shard_map.238
  171.7 0.5 collective-permute-start.3
  172.3 2.4 collective-permute-start.2
  174.7 1.8 collective-permute-start.1
  176.5 1.7 collective-permute-done.3
  178.2 4.4 %collective-permute-done.2 = bf16[320,256]{1,0:T(8,128)(2,1)S(1)} collective-permute-done((bf16[320,256]{1,0:T(8,128)(2,1)}, bf16[320,256]{1,0:T(8,128)(2,1)S(1)}, u32[]{:S(2)}, u32[]{:S(2)}) %collective-permute-start.2) | collective-permute-done | bytes 163872 | tf_op jit(solution)/shard_map/ppermute | solution.py:339
  182.6 0.9 collective-permute-done.1
  183.5 1.0 add_convert_fusion
  184.5 0.1 reshape.100
  184.6 16.4 %all_to_all.30 = bf16[32,10,256]{2,1,0:T(8,128)(2,1)S(1)} all-to-all(bf16[32,10,256]{2,1,0:T(8,128)(2,1)S(1)} %reshape.100), channel_id=1, replica_groups=mesh['replica'=8,'outer'=4,'link'=8] {'outer','link'}, dimensions={0} | all-to-all | bytes 327680 | tf_op jit(solution)/shard_map/all_to_all | solution.py:272
  201.0 0.1 reduce_sum.12
  201.1 15.6 %all_to_all.31 = bf16[32,10,256]{2,1,0:T(8,128)(2,1)S(1)} all-to-all(bf16[32,10,256]{2,1,0:T(8,128)(2,1)S(1)} %broadcast_in_dim.41), channel_id=1, replica_groups=mesh['replica'=8,'outer'=4,'link'=8] {'outer','link'}, dimensions={0} | all-to-all | bytes 327680 | tf_op jit(solution)/shard_map/all_to_all | solution.py:272
  216.7 4.5 %all-to-all-start.3 = ((bf16[32,64,256]{2,1,0:T(8,128)(2,1)}), bf16[32,64,256]{2,1,0:T(8,128)(2,1)S(1)}, u32[]{:S(2)}, u32[]{:S(2)}) async-start(bf16[32,64,256]{2,1,0:T(8,128)(2,1)} %bitcast.21), calls=%async_computation.3 | async-start | bytes 2097152 | tf_op jit(solution)/shard_map/all_to_all | solution.py:272
  221.2 0.1 reshape.101.refs_1_
  221.3 0.0 copy-start.4
  221.3 2.6 %collective-permute-start.4 = (bf16[320,256]{1,0:T(8,128)(2,1)S(1)}, bf16[320,256]{1,0:T(8,128)(2,1)S(1)}, u32[]{:S(2)}, u32[]{:S(2)}) collective-permute-start(bf16[320,256]{1,0:T(8,128)(2,1)S(1)} %reshape.101.refs_1_), channel_id=1, source_target_pairs={{0,64},{32,96},{64,128},{96,160},{128,192},{160,224},{192,0},{224,... | collective-permute-start | bytes 491528 | tf_op jit(solution)/shard_map/ppermute | solution.py:343
  223.9 3.3 %collective-permute-start.5 = (bf16[320,256]{1,0:T(8,128)(2,1)S(1)}, bf16[320,256]{1,0:T(8,128)(2,1)S(1)}, u32[]{:S(2)}, u32[]{:S(2)}) collective-permute-start(bf16[320,256]{1,0:T(8,128)(2,1)S(1)} %reshape.101.refs_1_), channel_id=1, source_target_pairs={{0,128},{32,160},{64,192},{96,224},{128,0},{160,32},{192,64},{224,... | collective-permute-start | bytes 491528 | tf_op jit(solution)/shard_map/ppermute | solution.py:343
  227.3 0.0 collective-permute-start.6
  227.3 0.0 collective-permute-start.7
  227.3 2.6 %collective-permute-done.4.refs_2_ = bf16[320,256]{1,0:T(8,128)(2,1)S(1)} collective-permute-done((bf16[320,256]{1,0:T(8,128)(2,1)S(1)}, bf16[320,256]{1,0:T(8,128)(2,1)S(1)}, u32[]{:S(2)}, u32[]{:S(2)}) %collective-permute-start.4) | collective-permute-done | bytes 163872 | tf_op jit(solution)/shard_map/ppermute | solution.py:343
  229.9 0.0 collective-permute-start.8
  229.9 1.9 collective-permute-done.5.refs_3_
  231.8 0.0 collective-permute-start.9
  231.8 1.7 collective-permute-done.6.refs_4_
  233.5 0.0 collective-permute-start.10
  233.5 0.0 collective-permute-done.8.refs_6_
  233.5 0.0 collective-permute-done.9.refs_7_
  233.5 1.3 collective-permute-done.10.refs_8_
  234.9 0.6 copy-done.12
  235.6 3.0 %shard_map.239 = (f32[256,768]{1,0:T(8,128)}, f32[256,768]{1,0:T(8,128)}, f32[1,768]{1,0:T(1,128)}, f32[512,256]{1,0:T(8,128)}, f32[1,256]{1,0:T(1,128)}, /*index=5*/f32[256,256]{1,0:T(8,128)}, f32[1,256]{1,0:T(1,128)}) custom-call(s32[2]{0:T(128)} %pad_add_fusion.place_ref.refs_0_, bf16[320,256]{1,0:T(8,128)(2,1)} %copy-done.4, bf16[320,256]{1,0:T(8,128)(2,1)} %copy-done.6, ...), custom_call_target="tpu_custom_call" | custom-call | tf_op jit(solution)/shard_map/pallas_call | solution.py:345
  238.5 1.3 reduce.2
  239.8 8.5 %all-to-all-done.3 = bf16[32,64,256]{2,1,0:T(8,128)(2,1)S(1)} async-done(((bf16[32,64,256]{2,1,0:T(8,128)(2,1)}), bf16[32,64,256]{2,1,0:T(8,128)(2,1)S(1)}, u32[]{:S(2)}, u32[]{:S(2)}) %all-to-all-start.3) | async-done | bytes 1048608 | tf_op jit(solution)/shard_map/all_to_all | solution.py:272
  248.3 1.0 copy-done.1
  249.3 2.9 %shard_map.236 = f32[512,256]{1,0:T(8,128)} custom-call(bf16[2048,256]{1,0:T(8,128)(2,1)} %bitcast.39, s32[16,128]{1,0:T(8,128)} %reshape_squeeze.3.srow_ref, f32[512,256]{1,0:T(8,128)} %get-tuple-element.50.direct_ref), custom_call_target="tpu_custom_call" | custom-call | tf_op jit(solution)/shard_map/pallas_call | solution.py:470
  (33 shorter events, 0.1 us)
Async XLA Ops:
  0.6 15.9 %copy-start.14 = (s32[1,128,24]{1,2,0:T(8,128)S(1)}, s32[1,128,24]{1,2,0:T(8,128)}, u32[]{:S(2)}) copy-start(s32[1,128,24]{1,2,0:T(8,128)} %param.17) | copy-start | bytes 36868
  0.7 15.9 %copy-start.15 = (s32[1,128]{1,0:T(1,128)S(1)}, s32[1,128]{1,0:T(1,128)}, u32[]{:S(2)}) copy-start(s32[1,128]{1,0:T(1,128)} %param.18) | copy-start | bytes 1540
  0.7 17.3 %copy-start.16 = (f32[768]{0:T(1024)S(1)}, f32[768]{0:T(1024)}, u32[]{:S(2)}) copy-start(f32[768]{0:T(1024)} %param.25) | copy-start | bytes 9220
  4.9 62.2 %copy-start.17 = (s32[1,512]{1,0:T(1,128)S(1)}, s32[1,512]{1,0:T(1,128)}, u32[]{:S(2)}) copy-start(s32[1,512]{1,0:T(1,128)} %param.19) | copy-start | bytes 6148
  4.9 63.6 %copy-start.13 = (s32[1,32,1,64]{3,2,1,0:T(1,128)S(1)}, s32[1,32,1,64]{3,2,1,0:T(1,128)}, u32[]{:S(2)}) copy-start(s32[1,32,1,64]{3,2,1,0:T(1,128)} %param.20) | copy-start | bytes 24580
  4.9 40.2 %all-to-all-start = ((bf16[32,64,256]{2,1,0:T(8,128)(2,1)}), bf16[32,64,256]{2,1,0:T(8,128)(2,1)S(1)}, u32[]{:S(2)}, u32[]{:S(2)}) async-start(bf16[32,64,256]{2,1,0:T(8,128)(2,1)} %bitcast.42), calls=%async_computation | async-start | bytes 2097152 | tf_op jit(solution)/shard_map/all_to_all | solution.py:272
  45.1 1.0 copy-start.3
  62.0 33.4 %all-to-all-start.1 = ((bf16[32,64,256]{2,1,0:T(8,128)(2,1)}), bf16[32,64,256]{2,1,0:T(8,128)(2,1)S(1)}, u32[]{:S(2)}, u32[]{:S(2)}) async-start(bf16[32,64,256]{2,1,0:T(8,128)(2,1)} %bitcast.47), calls=%async_computation.1 | async-start | bytes 2097152 | tf_op jit(solution)/shard_map/all_to_all | solution.py:272
  95.3 1.0 copy-start.2
  101.6 33.2 %all-to-all-start.2 = ((bf16[32,64,256]{2,1,0:T(8,128)(2,1)}), bf16[32,64,256]{2,1,0:T(8,128)(2,1)S(1)}, u32[]{:S(2)}, u32[]{:S(2)}) async-start(bf16[32,64,256]{2,1,0:T(8,128)(2,1)} %bitcast.46), calls=%async_computation.2 | async-start | bytes 2097152 | tf_op jit(solution)/shard_map/all_to_all | solution.py:272
  134.8 1.0 copy-start
  166.3 2.2 collective-permute-start
  168.5 0.8 copy-start.5
  171.7 6.5 %collective-permute-start.3 = (bf16[320,256]{1,0:T(8,128)(2,1)}, bf16[320,256]{1,0:T(8,128)(2,1)S(1)}, u32[]{:S(2)}, u32[]{:S(2)}) collective-permute-start(bf16[320,256]{1,0:T(8,128)(2,1)} %get-tuple-element.59), channel_id=1, source_target_pairs={{0,192},{32,224},{64,0},{96,32},{128,64},{160,96},{192,128},{224,1... | collective-permute-start | bytes 491528 | tf_op jit(solution)/shard_map/ppermute | solution.py:339
  172.3 10.4 %collective-permute-start.2 = (bf16[320,256]{1,0:T(8,128)(2,1)}, bf16[320,256]{1,0:T(8,128)(2,1)S(1)}, u32[]{:S(2)}, u32[]{:S(2)}) collective-permute-start(bf16[320,256]{1,0:T(8,128)(2,1)} %get-tuple-element.58), channel_id=1, source_target_pairs={{0,128},{32,160},{64,192},{96,224},{128,0},{160,32},{192,64},{224,... | collective-permute-start | bytes 491528 | tf_op jit(solution)/shard_map/ppermute | solution.py:339
  174.7 8.8 %collective-permute-start.1 = (bf16[320,256]{1,0:T(8,128)(2,1)}, bf16[320,256]{1,0:T(8,128)(2,1)S(1)}, u32[]{:S(2)}, u32[]{:S(2)}) collective-permute-start(bf16[320,256]{1,0:T(8,128)(2,1)} %get-tuple-element.57), channel_id=1, source_target_pairs={{0,64},{32,96},{64,128},{96,160},{128,192},{160,224},{192,0},{224,... | collective-permute-start | bytes 491528 | tf_op jit(solution)/shard_map/ppermute | solution.py:339
  216.7 31.6 %all-to-all-start.3 = ((bf16[32,64,256]{2,1,0:T(8,128)(2,1)}), bf16[32,64,256]{2,1,0:T(8,128)(2,1)S(1)}, u32[]{:S(2)}, u32[]{:S(2)}) async-start(bf16[32,64,256]{2,1,0:T(8,128)(2,1)} %bitcast.21), calls=%async_computation.3 | async-start | bytes 2097152 | tf_op jit(solution)/shard_map/all_to_all | solution.py:272
  221.3 13.6 %copy-start.4 = (bf16[320,256]{1,0:T(8,128)(2,1)}, bf16[320,256]{1,0:T(8,128)(2,1)S(1)}, u32[]{:S(2)}) copy-start(bf16[320,256]{1,0:T(8,128)(2,1)S(1)} %reshape.101.refs_1_) | copy-start | bytes 491524
  221.3 8.6 %collective-permute-start.4 = (bf16[320,256]{1,0:T(8,128)(2,1)S(1)}, bf16[320,256]{1,0:T(8,128)(2,1)S(1)}, u32[]{:S(2)}, u32[]{:S(2)}) collective-permute-start(bf16[320,256]{1,0:T(8,128)(2,1)S(1)} %reshape.101.refs_1_), channel_id=1, source_target_pairs={{0,64},{32,96},{64,128},{96,160},{128,192},{160,224},{192,0},{224,... | collective-permute-start | bytes 491528 | tf_op jit(solution)/shard_map/ppermute | solution.py:343
  223.9 7.9 %collective-permute-start.5 = (bf16[320,256]{1,0:T(8,128)(2,1)S(1)}, bf16[320,256]{1,0:T(8,128)(2,1)S(1)}, u32[]{:S(2)}, u32[]{:S(2)}) collective-permute-start(bf16[320,256]{1,0:T(8,128)(2,1)S(1)} %reshape.101.refs_1_), channel_id=1, source_target_pairs={{0,128},{32,160},{64,192},{96,224},{128,0},{160,32},{192,64},{224,... | collective-permute-start | bytes 491528 | tf_op jit(solution)/shard_map/ppermute | solution.py:343
  227.3 6.2 %collective-permute-start.6 = (bf16[320,256]{1,0:T(8,128)(2,1)S(1)}, bf16[320,256]{1,0:T(8,128)(2,1)S(1)}, u32[]{:S(2)}, u32[]{:S(2)}) collective-permute-start(bf16[320,256]{1,0:T(8,128)(2,1)S(1)} %reshape.101.refs_1_), channel_id=1, source_target_pairs={{0,192},{32,224},{64,0},{96,32},{128,64},{160,96},{192,128},{224,1... | collective-permute-start | bytes 491528 | tf_op jit(solution)/shard_map/ppermute | solution.py:343
  227.3 6.2 %collective-permute-start.7 = (bf16[320,256]{1,0:T(8,128)(2,1)S(1)}, bf16[320,256]{1,0:T(8,128)(2,1)S(1)}, u32[]{:S(2)}, u32[]{:S(2)}) collective-permute-start(bf16[320,256]{1,0:T(8,128)(2,1)S(1)} %reshape.101.refs_1_), channel_id=1, source_target_pairs={{0,32},{32,0},{64,96},{96,64},{128,160},{160,128},{192,224},{224,1... | collective-permute-start | bytes 491528 | tf_op jit(solution)/shard_map/ppermute | solution.py:344
  229.9 4.9 %copy-start.6 = (bf16[320,256]{1,0:T(8,128)(2,1)}, bf16[320,256]{1,0:T(8,128)(2,1)S(1)}, u32[]{:S(2)}) copy-start(bf16[320,256]{1,0:T(8,128)(2,1)S(1)} %collective-permute-done.4.refs_2_) | copy-start | bytes 491524
  229.9 3.6 %collective-permute-start.8 = (bf16[320,256]{1,0:T(8,128)(2,1)S(1)}, bf16[320,256]{1,0:T(8,128)(2,1)S(1)}, u32[]{:S(2)}, u32[]{:S(2)}) collective-permute-start(bf16[320,256]{1,0:T(8,128)(2,1)S(1)} %collective-permute-done.4.refs_2_), channel_id=1, source_target_pairs={{0,32},{32,0},{64,96},{96,64},{128,160},{160,128},{192,224},{224,1... | collective-permute-start | bytes 491528 | tf_op jit(solution)/shard_map/ppermute | solution.py:344
  231.8 3.1 %copy-start.7 = (bf16[320,256]{1,0:T(8,128)(2,1)}, bf16[320,256]{1,0:T(8,128)(2,1)S(1)}, u32[]{:S(2)}) copy-start(bf16[320,256]{1,0:T(8,128)(2,1)S(1)} %collective-permute-done.5.refs_3_) | copy-start | bytes 491524
  231.8 1.7 collective-permute-start.9
  233.5 1.4 copy-start.8
  233.5 1.4 collective-permute-start.10
  233.5 1.4 copy-start.9
  233.5 1.4 copy-start.10
  233.5 1.4 copy-start.11
  234.9 0.7 copy-start.12
  248.3 1.0 copy-start.1

commit v2 on v1

--- a/solution.py
+++ b/solution.py
@@ -37,26 +37,42 @@
     return jnp.where(subs == row, 1.0, 0.0).astype(BF)
 
 
-def call(kernel, outs, **kw):
-    return pl.pallas_call(kernel, out_shape=outs, interpret=INTERPRET, **kw)
+def call(kernel, outs, mib=16, **kw):
+    return pl.pallas_call(
+        kernel,
+        out_shape=outs,
+        interpret=INTERPRET,
+        compiler_params=pltpu.CompilerParams(vmem_limit_bytes=mib * 1024 * 1024),
+        **kw,
+    )
 
 
 def sds(shape, dtype):
     return jax.ShapeDtypeStruct(shape, dtype)
 
 
-def gather_rows(table, serve_col, out_ref, per=8):
+def send(buf_ref, out_hbm, sem, first, rows, k):
+    part = pl.ds(first, rows)
+    return pltpu.make_async_copy(buf_ref.at[part, :], out_hbm.at[part, :], sem.at[k])
+
+
+def gather_rows(table, serve_col, buf_ref, out_hbm, sem, per=8):
     cap, group = serve_col.shape
     links = table.shape[0]
-    for o in range(0, group, per):
+    copies = []
+    for k, o in enumerate(range(0, group, per)):
         sel = jnp.concatenate(
-            [pick_cols(serve_col[:, k : k + 1], links) for k in range(o, o + per)], axis=0
+            [pick_cols(serve_col[:, i : i + 1], links) for i in range(o, o + per)], axis=0
         )
-        out_ref[o * cap : (o + per) * cap, :] = dot(sel, table).astype(BF)
-
-
-def serve_kernel(table_ref, col_ref, out_ref):
-    gather_rows(table_ref[...], col_ref[...], out_ref)
+        buf_ref[o * cap : (o + per) * cap, :] = dot(sel, table).astype(BF)
+        copies.append(send(buf_ref, out_hbm, sem, o * cap, per * cap, k))
+        copies[-1].start()
+    return copies
+
+
+def serve_kernel(table_ref, col_ref, out_hbm, buf_ref, sem):
+    for copy in gather_rows(table_ref[...], jnp.transpose(col_ref[...]), buf_ref, out_hbm, sem):
+        copy.wait()
 
 
 def fetch_hops(table_ref, slot_ref, out_ref, per=4):
@@ -73,21 +89,32 @@
             out_ref[t + k] = rows[k * flows : (k + 1) * flows]
 
 
-def sum_slots(row_ref, rows, out_ref, block=512):
+def sum_slots(row_ref, rows, buf_ref, out_hbm, sem, block=512):
     hops = row_ref.shape[0]
-    slots = out_ref.shape[0]
+    slots = buf_ref.shape[0]
     idx = row_ref[...]
-    for q in range(0, slots, block):
+    copies = []
+    for k, q in enumerate(range(0, slots, block)):
         sel = jnp.concatenate([pick_rows(idx[t : t + 1, :], block, q) for t in range(hops)], axis=1)
-        out_ref[q : q + block, :] = dot(sel, rows).astype(BF)
+        buf_ref[q : q + block, :] = dot(sel, rows).astype(BF)
+        copies.append(send(buf_ref, out_hbm, sem, q, block, k))
+        copies[-1].start()
+    return copies
 
 
 def forward_kernel(
     table_ref, slot_ref, row_ref, lens_ref, path_ref, wx_ref, wh_ref, bias_ref,
-    x_ref, state_ref, part_ref, pathout_ref, gi_ref, hb_ref,
+    x_hbm, state_hbm, prior_hbm, part_hbm, pathout_ref,
+    x_ref, state_ref, prior_ref, gi_ref, hb_ref, part_ref, sem, sem_part,
 ):
     hops, flows, width = x_ref.shape
+    outs = [
+        pltpu.make_async_copy(x_ref, x_hbm, sem.at[0]),
+        pltpu.make_async_copy(state_ref, state_hbm, sem.at[1]),
+        pltpu.make_async_copy(prior_ref, prior_hbm, sem.at[2]),
+    ]
     fetch_hops(table_ref, slot_ref, x_ref)
+    outs[0].start()
     per = 4
     for t in range(0, hops, per):
         rows = x_ref[t : t + per].reshape(per * flows, width)
@@ -97,7 +124,9 @@
 
     def step(t, h):
         state_ref[t] = h
-        gs = dot(h.astype(BF), wh_ref[...])
+        hb = h.astype(BF)
+        prior_ref[t] = hb
+        gs = dot(hb, wh_ref[...])
         gi = gi_ref[t]
         z = sigmoid(gi[:, :width] + gs[:, :width])
         r = sigmoid(gi[:, width : 2 * width] + gs[:, width : 2 * width])
@@ -106,9 +135,15 @@
         hb_ref[t] = h.astype(BF)
         return h
 
-    h = lax.fori_loop(0, hops, step, path_ref[...].astype(F32), unroll=2)
+    h = lax.fori_loop(0, hops, step, path_ref[...].astype(F32), unroll=4)
+    outs[1].start()
+    outs[2].start()
     pathout_ref[...] = h.astype(BF)
-    sum_slots(row_ref, hb_ref[...].reshape(hops * flows, width), part_ref)
+    outs += sum_slots(
+        row_ref, hb_ref[...].reshape(hops * flows, width), part_ref, part_hbm, sem_part
+    )
+    for out in outs:
+        out.wait()
 
 
 def coef_kernel(x_ref, state_ref, lens_ref, wx_ref, wh_ref, bias_ref, coef_ref):
@@ -137,41 +172,46 @@
 
 def link_kernel(
     got_ref, srow_ref, scol_ref, link_ref, lgrad_ref, keep_ref, w1_ref, b1_ref, w2_ref,
-    out_ref, agg_ref, act_ref, du_ref, db1_ref,
+    out_hbm, mid_hbm, db1_ref,
+    buf_ref, mid_ref, sem, sem_out,
 ):
     links, width = link_ref.shape
     sel = jnp.concatenate(
         [pick_rows(srow_ref[k : k + 1, :], links) for k in range(srow_ref.shape[0])], axis=1
     )
     agg = dot(sel, got_ref[...]).astype(BF)
-    agg_ref[...] = agg
+    mid_ref[:links, :] = agg
     u = dot(link_ref[...], w1_ref[:width, :]) + dot(agg, w1_ref[width:, :]) + b1_ref[...]
     s = sigmoid(u)
-    act_ref[...] = (u * s).astype(BF)
+    mid_ref[links : 2 * links, :] = (u * s).astype(BF)
     gv = (keep_ref[...] * lgrad_ref[...].astype(F32)).astype(BF)
     du = dot_nt(gv, w2_ref[...]) * s * (1.0 + u * (1.0 - s))
     db1_ref[...] = jnp.sum(du, axis=0, keepdims=True)
     du = du.astype(BF)
-    du_ref[...] = du
+    mid_ref[2 * links :, :] = du
     dagg = dot_nt(du, w1_ref[width:, :]).astype(BF)
-    gather_rows(dagg, scol_ref[...], out_ref)
+    copies = [pltpu.make_async_copy(mid_ref, mid_hbm, sem.at[0])]
+    copies[0].start()
+    copies += gather_rows(dagg, jnp.transpose(scol_ref[...]), buf_ref, out_hbm, sem_out)
+    for copy in copies:
+        copy.wait()
 
 
 def link_rest_kernel(
-    link_ref, lgrad_ref, keep_ref, agg_ref, act_ref, du_ref, db1_ref, w1_ref, w2_ref, b2_ref,
+    link_ref, lgrad_ref, keep_ref, mid_ref, db1_ref, w1_ref, w2_ref, b2_ref,
     lout_ref, direct_ref, pack_ref,
 ):
-    _, width = link_ref.shape
+    links, width = link_ref.shape
     link = link_ref[...]
     keep = keep_ref[...]
-    act = act_ref[...]
-    du = du_ref[...]
+    act = mid_ref[links : 2 * links, :]
+    du = mid_ref[2 * links :, :]
     value = link.astype(F32) + dot(act, w2_ref[...]) + b2_ref[...]
     lout_ref[...] = (keep * value).astype(BF)
     gv = keep * lgrad_ref[...].astype(F32)
     direct_ref[...] = gv + dot_nt(du, w1_ref[:width, :])
     pack_ref[0:width, :] = dot_tn(link, du).astype(BF)
-    pack_ref[width : 2 * width, :] = dot_tn(agg_ref[...], du).astype(BF)
+    pack_ref[width : 2 * width, :] = dot_tn(mid_ref[:links, :], du).astype(BF)
     pack_ref[2 * width : 3 * width, :] = dot_tn(act, gv.astype(BF)).astype(BF)
     db2 = jnp.sum(gv, axis=0, keepdims=True)
     tail = jnp.concatenate([db1_ref[...], db2, jnp.zeros((14, width), F32)], axis=0)
@@ -180,13 +220,16 @@
 
 def backward_kernel(
     table_ref, slot_ref, row_ref, pgrad_ref, wx_ref, wh_ref, coef_hbm,
-    part_ref, pathgrad_ref, dgi_ref, dgs_ref, db_ref,
-    hg_ref, coef_ref, dx_ref, sem,
+    part_hbm, pathgrad_ref, gate_hbm, db_ref,
+    hg_ref, coef_ref, gate_ref, dx_ref, part_ref, sem_in, sem_out, sem_part,
 ):
     hops, flows, width = hg_ref.shape
 
     def load(t):
-        return pltpu.make_async_copy(coef_hbm.at[t], coef_ref.at[t], sem.at[t])
+        return pltpu.make_async_copy(coef_hbm.at[t], coef_ref.at[t], sem_in.at[t])
+
+    def store(t):
+        return pltpu.make_async_copy(gate_ref.at[t], gate_hbm.at[t], sem_out.at[t])
 
     for t in range(hops - 1, -1, -1):
         load(t).start()
@@ -203,34 +246,41 @@
         az = g * coef_ref[t, 1]
         ar = g * coef_ref[t, 2]
         an = g * coef_ref[t, 3]
-        azb = az.astype(BF)
-        arb = ar.astype(BF)
-        anr = (an * coef_ref[t, 4]).astype(BF)
-        dgs = jnp.concatenate([azb, arb, anr], axis=1)
+        dgs = jnp.concatenate(
+            [az.astype(BF), ar.astype(BF), (an * coef_ref[t, 4]).astype(BF)], axis=1
+        )
         nxt = g * coef_ref[t, 0] + dot_nt(dgs, wh_ref[...])
-        dgs_ref[t] = dgs
-        dgi_ref[t] = jnp.concatenate([azb, arb, an.astype(BF)], axis=1)
+        gate_ref[t, :, :width] = an.astype(BF)
+        gate_ref[t, :, width:] = dgs
+        store(t).start()
         db_ref[:, :width] += fold(az)
         db_ref[:, width : 2 * width] += fold(ar)
         db_ref[:, 2 * width :] += fold(an)
         return nxt
 
-    g = lax.fori_loop(0, hops, step, pgrad_ref[...].astype(F32), unroll=2)
+    g = lax.fori_loop(0, hops, step, pgrad_ref[...].astype(F32), unroll=4)
     pathgrad_ref[...] = g
+    wx = jnp.concatenate([wx_ref[:, 2 * width :], wx_ref[:, : 2 * width]], axis=1)
     per = 4
     for t in range(0, hops, per):
-        rows = dgi_ref[t : t + per].reshape(per * flows, 3 * width)
-        dx_ref[t * flows : (t + per) * flows, :] = dot_nt(rows, wx_ref[...]).astype(BF)
-    sum_slots(row_ref, dx_ref[...], part_ref)
-
-
-def weight_kernel(x_ref, state_ref, dgi_ref, dgs_ref, db_ref, mlp_ref, pack_ref, awx_ref, awh_ref):
+        rows = gate_ref[t : t + per, :, : 3 * width].reshape(per * flows, 3 * width)
+        dx_ref[t * flows : (t + per) * flows, :] = dot_nt(rows, wx).astype(BF)
+    for copy in sum_slots(row_ref, dx_ref[...], part_ref, part_hbm, sem_part):
+        copy.wait()
+    for t in range(hops):
+        store(t).wait()
+
+
+def weight_kernel(
+    place_ref, x_ref, prior_ref, gate_ref, db_ref, mlp_ref,
+    mine_ref, other_ref, pack_ref, awx_ref, awh_ref,
+):
     per, flows, width = x_ref.shape
     i = pl.program_id(0)
-    x = x_ref[...].reshape(per * flows, width)
-    h = state_ref[...].reshape(per * flows, width).astype(BF)
-    gx = dot_tn(x, dgi_ref[...].reshape(per * flows, 3 * width))
-    gh = dot_tn(h, dgs_ref[...].reshape(per * flows, 3 * width))
+    rows = per * flows
+    gates = gate_ref[...].reshape(rows, 4 * width)
+    gx = dot_tn(x_ref[...].reshape(rows, width), gates[:, : 3 * width])
+    gh = dot_tn(prior_ref[...].reshape(rows, width), gates[:, width:])
 
     @pl.when(i == 0)
     def _():
@@ -246,7 +296,8 @@
     def _():
         for k in range(3):
             s = slice(k * width, (k + 1) * width)
-            pack_ref[k * width : (k + 1) * width, :] = awx_ref[:, s].astype(BF)
+            to = (k + 2) % 3
+            pack_ref[to * width : (to + 1) * width, :] = awx_ref[:, s].astype(BF)
             pack_ref[(3 + k) * width : (4 + k) * width, :] = awh_ref[:, s].astype(BF)
         base = 9 * width
         pack_ref[6 * width : base + 16, :] = mlp_ref[...]
@@ -258,6 +309,10 @@
         pack_ref[base + 16 : base + 32, :] = tail.astype(BF)
         rest = pack_ref.shape[0] - base - 32
         pack_ref[base + 32 :, :] = jnp.zeros((rest, width), BF)
+        half = mine_ref.shape[0]
+        core = place_ref[1]
+        mine_ref[...] = pack_ref[pl.ds(pl.multiple_of(core * half, 256), half), :]
+        other_ref[...] = pack_ref[pl.ds(pl.multiple_of((1 - core) * half, 256), half), :]
 
 
 def finish_kernel(got_ref, srow_ref, direct_ref, out_ref):
@@ -284,11 +339,11 @@
 
 def pair_kernel(place_ref, pack_ref, got_ref, *out_refs):
     x = place_ref[0]
-    core = place_ref[1]
-    chips = got_ref.shape[0]
+    chips = len(out_refs)
+    part = out_refs[0].shape[0]
     for k in range(chips):
-        c = lax.rem(x + k, chips)
-        both = pack_ref[core * chips + c].astype(F32) + got_ref[c].astype(F32)
+        rows = pl.ds(pl.multiple_of(lax.rem(x + k, chips) * part, 64), part)
+        both = pack_ref[rows, :].astype(F32) + got_ref[rows, :].astype(F32)
         out_refs[k][...] = both.astype(BF)
 
 
@@ -315,39 +370,44 @@
     b1_ref[...] = tail[0:1]
     b2_ref[...] = tail[1:2]
     for k in range(3):
-        bias_ref[:, k * width : (k + 1) * width] = tail[16 + k : 17 + k]
-
-
-def sum_everywhere(pack, scale):
-    rows, width = pack.shape
+        bias_ref[k * width : (k + 1) * width] = tail[16 + k]
+
+
+def whereabouts():
+    rep = lax.axis_index("replica")
+    return jnp.stack([rep // 2, rep % 2]).astype(jnp.int32)
+
+
+def sum_everywhere(mine, other, place, scale):
+    rows, width = mine.shape
+    rows = 2 * rows
     reps = lax.axis_size("replica")
     group = lax.axis_size("outer") * lax.axis_size("link")
-    rep = lax.axis_index("replica")
     chips = reps // 2
     part = rows // reps
-    place = jnp.stack([rep // 2, rep % 2]).astype(jnp.int32)
     pairs = [(i, i ^ 1) for i in range(reps)]
     ahead = [[(i, (i + 2 * k) % reps) for i in range(reps)] for k in range(chips)]
-    halves = pack.reshape(2, rows // 2, width)
     smem = pl.BlockSpec(memory_space=pltpu.SMEM)
     vmem = pl.BlockSpec(memory_space=pltpu.VMEM)
-    other = jnp.where(rep % 2 == 0, halves[1], halves[0])
     got = lax.ppermute(other, "replica", pairs)
     mine = call(
         pair_kernel, (sds((part, width), BF),) * chips, in_specs=[smem, vmem, vmem]
-    )(place, pack.reshape(reps, part, width), got.reshape(chips, part, width))
+    )(place, mine, got)
     got = [lax.ppermute(mine[k], "replica", ahead[k]) for k in range(1, chips)]
     mine = sum((g.astype(F32) for g in got), mine[0].astype(F32)).astype(BF)
     mine = total(swap(mine.reshape(group, part // group, width)))
     mine = swap(jnp.broadcast_to(mine[None], (group,) + mine.shape)).reshape(part, width)
-    mine = [mine] + [lax.ppermute(mine, "replica", ahead[k]) for k in range(1, chips)]
+    whole = [mine]
+    for k in range(1, chips):
+        whole.append(lax.ppermute(mine, "replica", ahead[k]))
+    mine = whole
     got = [lax.ppermute(m, "replica", pairs) for m in mine]
     return call(
         lambda *refs: unpack_kernel(*refs, scale=scale),
         (
             sds((width, 3 * width), F32),
             sds((width, 3 * width), F32),
-            sds((1, 3 * width), F32),
+            sds((3 * width,), F32),
             sds((2 * width, width), F32),
             sds((1, width), F32),
             sds((width, width), F32),
@@ -367,7 +427,6 @@
     serve_rows = serve_index[0, :, 0, :]
     group, cap = serve_rows.shape
     slots = group * cap
-    serve_col = serve_rows.T
     serve_row = serve_rows.reshape(slots // 128, 128)
     flows, hops = hop_slots.shape[1:]
     lens_col = hop_lens[0][:, None]
@@ -377,19 +436,39 @@
     bias = gru_bias[None]
     wide = 3 * width
 
-    sent = call(serve_kernel, sds((slots, width), BF))(link_rows, serve_col)
+    vmem = pl.BlockSpec(memory_space=pltpu.VMEM)
+    smem = pl.BlockSpec(memory_space=pltpu.SMEM)
+    hbm = pl.BlockSpec(memory_space=pltpu.HBM)
+    blocks = group // 8
+    rows_out = [pltpu.VMEM((slots, width), BF)]
+    sent = call(
+        serve_kernel,
+        sds((slots, width), BF),
+        out_specs=hbm,
+        scratch_shapes=rows_out + [pltpu.SemaphoreType.DMA((blocks,))],
+    )(link_rows, serve_rows)
     fetched = swap_named(sent, group)
-    x, states, part, path_out = call(
+    place = whereabouts()
+    x, states, priors, part, path_out = call(
         forward_kernel,
         (
             sds((hops, flows, width), BF),
             sds((hops, flows, width), F32),
+            sds((hops, flows, width), BF),
             sds((slots, width), BF),
             sds((flows, width), BF),
         ),
+        mib=62,
+        out_specs=[hbm] * 4 + [vmem],
         scratch_shapes=[
+            pltpu.VMEM((hops, flows, width), BF),
+            pltpu.VMEM((hops, flows, width), F32),
+            pltpu.VMEM((hops, flows, width), BF),
             pltpu.VMEM((hops, flows, wide), F32),
             pltpu.VMEM((hops, flows, width), BF),
+            *rows_out,
+            pltpu.SemaphoreType.DMA((3,)),
+            pltpu.SemaphoreType.DMA((slots // 512,)),
         ],
     )(fetched, slot_col, slot_row, lens_col, path_in[0], gru_wx, gru_wh, bias)
     arrived = swap_named(part, group)
@@ -400,6 +479,7 @@
     coef = call(
         coef_kernel,
         sds((hops, 5, flows, width), F32),
+        mib=58,
         grid=(hops // per,),
         in_specs=[
             steps(flows, width),
@@ -412,16 +492,22 @@
         out_specs=steps(5, flows, width),
     )(x, states, lens_col, gru_wx, gru_wh, bias)
 
-    sent, agg, act, du, db1 = call(
+    sent, mids, db1 = call(
         link_kernel,
         (
             sds((slots, width), BF),
-            sds((links, width), BF),
-            sds((links, width), BF),
-            sds((links, width), BF),
+            sds((3 * links, width), BF),
             sds((1, width), F32),
         ),
-    )(arrived, serve_row, serve_col, link_rows, link_grad[0], keep, mlp_w1, mlp_b1[None], mlp_w2)
+        mib=62,
+        out_specs=[hbm, hbm, vmem],
+        scratch_shapes=rows_out
+        + [
+            pltpu.VMEM((3 * links, width), BF),
+            pltpu.SemaphoreType.DMA((1,)),
+            pltpu.SemaphoreType.DMA((blocks,)),
+        ],
+    )(arrived, serve_row, serve_rows, link_rows, link_grad[0], keep, mlp_w1, mlp_b1[None], mlp_w2)
     returned = swap_named(sent, group)
     link_out, direct, mlp_pack = call(
         link_rest_kernel,
@@ -430,48 +516,58 @@
             sds((links, width), F32),
             sds((3 * width + 16, width), BF),
         ),
-    )(link_rows, link_grad[0], keep, agg, act, du, db1, mlp_w1, mlp_w2, mlp_b2[None])
-
-    vmem = pl.BlockSpec(memory_space=pltpu.VMEM)
-    dpart, path_back, dgi, dgs, db = call(
+        mib=58,
+    )(link_rows, link_grad[0], keep, mids, db1, mlp_w1, mlp_w2, mlp_b2[None])
+
+    dpart, path_back, gates, db = call(
         backward_kernel,
         (
             sds((slots, width), BF),
             sds((flows, width), F32),
-            sds((hops, flows, wide), BF),
-            sds((hops, flows, wide), BF),
+            sds((hops, flows, 4 * width), BF),
             sds((8, wide), F32),
         ),
-        in_specs=[vmem] * 6 + [pl.BlockSpec(memory_space=pl.ANY)],
+        mib=51,
+        in_specs=[vmem] * 6 + [hbm],
+        out_specs=[hbm, vmem, hbm, vmem],
         scratch_shapes=[
             pltpu.VMEM((hops, flows, width), BF),
             pltpu.VMEM((hops, 5, flows, width), F32),
+            pltpu.VMEM((hops, flows, 4 * width), BF),
             pltpu.VMEM((hops * flows, width), BF),
+            *rows_out,
             pltpu.SemaphoreType.DMA((hops,)),
+            pltpu.SemaphoreType.DMA((hops,)),
+            pltpu.SemaphoreType.DMA((slots // 512,)),
         ],
     )(returned, slot_col, slot_row, path_grad[0], gru_wx, gru_wh, coef)
     owned = swap_named(dpart, group)
 
-    pack = call(
+    mine, other = call(
         weight_kernel,
-        sds((10 * width, width), BF),
+        (sds((5 * width, width), BF),) * 2,
+        mib=58,
         grid=(hops // per,),
         in_specs=[
+            smem,
             steps(flows, width),
             steps(flows, width),
-            steps(flows, wide),
-            steps(flows, wide),
+            steps(flows, 4 * width),
             whole(8, wide),
             whole(3 * width + 16, width),
         ],
-        out_specs=whole(10 * width, width),
-        scratch_shapes=[pltpu.VMEM((width, wide), F32), pltpu.VMEM((width, wide), F32)],
-    )(x, states, dgi, dgs, db, mlp_pack)
-    link_back = call(finish_kernel, sds((links, width), F32))(owned, serve_row, direct)
+        out_specs=[whole(5 * width, width)] * 2,
+        scratch_shapes=[
+            pltpu.VMEM((10 * width, width), BF),
+            pltpu.VMEM((width, wide), F32),
+            pltpu.VMEM((width, wide), F32),
+        ],
+    )(place, x, priors, gates, db, mlp_pack)
+    link_back = call(finish_kernel, sds((links, width), F32), mib=58)(owned, serve_row, direct)
 
     count = lax.axis_size("replica") * lax.axis_size("outer") * lax.axis_size("link")
     scale = float(count * links) ** (-0.5)
-    wx, wh, bias, w1, b1, w2, b2 = sum_everywhere(pack, scale)
+    wx, wh, bias, w1, b1, w2, b2 = sum_everywhere(mine, other, place, scale)
     return (
         link_out[None],
         path_out[None],
@@ -479,7 +575,7 @@
         path_back[None],
         wx,
         wh,
-        bias.reshape(wide),
+        bias,
         w1,
         b1.reshape(width),
         w2,

time: 257 us -> 248 us (0.965); the launches traced: 252 us -> 246 us
  Pallas kernels: 74.6 us -> 70.1 us
  other arithmetic: 5.58 us -> 2.05 us
  waiting for transfers between devices: 90.6 us -> 93.5 us
    all_to_all x4, waiting for transfers between devices: 74.7 us -> 79.8 us  [swap(): lax.all_to_all(blocks, axes, split_axis=0, concat_axis=0, tiled=True, axi...]
    ppermute x3, waiting for transfers between devices: 6.16 us -> 2.95 us  [sum_everywhere(): whole.append(lax.ppermute(mine, 'replica', ahead[k]))]
    unnamed x38 -> x37, local copies, waits for them, and re-layouts: 7.41 us -> 6.84 us
  transfers between devices with their start and end apart: 15 -> 15, of which waited for: 12 -> 11; matrix products, arithmetic and copies ran while one was open for 3% -> 2% of each run, Pallas kernels for 6% -> 6%
where the time goes in v2:
time: 248 us; the launch traced here: 246 us
  waiting for transfers between devices  93.5 us (38%)
  Pallas kernels  70.1 us (28%)
  starting transfers between devices  37 us (15%)
  blocking collectives  32.3 us (13%)
  local copies, waits for them, and re-layouts  10.6 us (4%)
    all_to_all x4, waiting for transfers between devices, swap(): lax.all_to_all(blocks, axes, split_axis=0, concat_axis=0, tiled=True, axi...  79.8 us
    all_to_all x2, blocking collectives, swap(): lax.all_to_all(blocks, axes, split_axis=0, concat_axis=0, tiled=True, axi...  32.3 us
    all_to_all x4, starting transfers between devices, swap(): lax.all_to_all(blocks, axes, split_axis=0, concat_axis=0, tiled=True, axi...  26.2 us
    pallas_call x1, Pallas kernels, body(): call(backward_kernel, (sds((slots, width), BF), sds((flows, width), F32),...  18.7 us
    pallas_call x1, Pallas kernels, body(): call(forward_kernel, (sds((hops, flows, width), BF), sds((hops, flows, wi...  16.1 us
    pallas_call x1, Pallas kernels, body(): call(coef_kernel, sds((hops, 5, flows, width), F32), mib=58, grid=(hops /...  10.5 us
    pallas_call x1, Pallas kernels, body(): call(weight_kernel, (sds((5 * width, width), BF),) * 2, mib=58, grid=(hop...  8.89 us
    ppermute x3, waiting for transfers between devices, sum_everywhere(): got = [lax.ppermute(mine[k], 'replica', ahead[k]) for k in range(1, chips)]  7.04 us
  transfers between devices with their start and end apart: 15, of which 11 were waited for; matrix products, arithmetic and copies ran while one was open for 2% of the time, Pallas kernels for 6%

profile of v2, /device:TPU:2, one launch (start us, length us, event | category | flops | bytes accessed | tf_op | source)
XLA Modules:
  0.0 246.5 jit_solution(10980632560821040479)
XLA Ops:
  0.7 0.0 copy-start.2
  0.7 0.9 copy-done.2
  1.6 0.7 copy-done.5
  2.3 1.8 shard_map.230
  4.1 0.0 copy-start.17
  4.1 0.0 copy-start.6
  4.1 11.5 %all-to-all-start = ((bf16[32,64,256]{2,1,0:T(8,128)(2,1)}), bf16[32,64,256]{2,1,0:T(8,128)(2,1)S(1)}, u32[]{:S(2)}, u32[]{:S(2)}) async-start(bf16[32,64,256]{2,1,0:T(8,128)(2,1)} %bitcast.4), calls=%async_computation | async-start | bytes 2097152 | tf_op jit(solution)/shard_map/all_to_all | solution.py:327
  15.7 0.7 copy.30.slot_ref
  16.4 0.7 copy.31.lens_ref
  17.1 0.6 broadcast_in_dim.34.bias_ref
  17.7 0.6 fusion.row_ref
  18.3 25.9 %all-to-all-done = bf16[32,64,256]{2,1,0:T(8,128)(2,1)S(1)} async-done(((bf16[32,64,256]{2,1,0:T(8,128)(2,1)}), bf16[32,64,256]{2,1,0:T(8,128)(2,1)S(1)}, u32[]{:S(2)}, u32[]{:S(2)}) %all-to-all-start) | async-done | bytes 1048608 | tf_op jit(solution)/shard_map/all_to_all | solution.py:327
  44.3 1.0 copy-done.12
  45.2 16.1 %shard_map.231 = (bf16[24,128,256]{2,1,0:T(8,128)(2,1)}, f32[24,128,256]{2,1,0:T(8,128)}, bf16[24,128,256]{2,1,0:T(8,128)(2,1)}, bf16[2048,256]{1,0:T(8,128)(2,1)}, bf16[128,256]{1,0:T(8,128)(2,1)}) custom-call(bf16[2048,256]{1,0:T(8,128)(2,1)} %bitcast.41, s32[128,24]{1,0:T(8,128)} %copy.30.slot_ref, s32[24,128]{1,0:T(8,128)} %fusion.row_ref, ...), custom_call_target="tpu_custom_call" | custom-call | tf_op jit(solution)/shard_map/pallas_call | solution.py:452
  61.3 5.3 %all-to-all-start.1 = ((bf16[32,64,256]{2,1,0:T(8,128)(2,1)}), bf16[32,64,256]{2,1,0:T(8,128)(2,1)S(1)}, u32[]{:S(2)}, u32[]{:S(2)}) async-start(bf16[32,64,256]{2,1,0:T(8,128)(2,1)} %bitcast.44), calls=%async_computation.1 | async-start | bytes 2097152 | tf_op jit(solution)/shard_map/all_to_all | solution.py:327
  66.7 0.9 copy.33.keep_ref
  67.5 0.5 broadcast.15
  68.0 0.7 reduce.4
  68.7 0.7 reshape_squeeze.3.srow_ref
  69.4 25.3 %all-to-all-done.1 = bf16[32,64,256]{2,1,0:T(8,128)(2,1)S(1)} async-done(((bf16[32,64,256]{2,1,0:T(8,128)(2,1)}), bf16[32,64,256]{2,1,0:T(8,128)(2,1)S(1)}, u32[]{:S(2)}, u32[]{:S(2)}) %all-to-all-start.1) | async-done | bytes 1048608 | tf_op jit(solution)/shard_map/all_to_all | solution.py:327
  94.7 1.0 copy-done.13
  95.7 5.6 %shard_map.232 = (bf16[2048,256]{1,0:T(8,128)(2,1)}, bf16[1536,256]{1,0:T(8,128)(2,1)}, f32[1,256]{1,0:T(1,128)}) custom-call(bf16[2048,256]{1,0:T(8,128)(2,1)} %bitcast.42, s32[16,128]{1,0:T(8,128)} %reshape_squeeze.3.srow_ref, s32[32,64]{1,0:T(8,128)} %bitcast.37, bf16[512,256]{1,0:T(8,128)(2,1)} %bitcast.34, bf16[512,256]{1,0:T(8,128)(2,1)} %bitcast.45, ...), custom_call_target="tpu_custom_call" | custom-call | tf_op jit(solution)/shard_map/pallas_call | solution.py:495
  101.3 4.9 %all-to-all-start.2 = ((bf16[32,64,256]{2,1,0:T(8,128)(2,1)}), bf16[32,64,256]{2,1,0:T(8,128)(2,1)S(1)}, u32[]{:S(2)}, u32[]{:S(2)}) async-start(bf16[32,64,256]{2,1,0:T(8,128)(2,1)} %bitcast.43), calls=%async_computation.2 | async-start | bytes 2097152 | tf_op jit(solution)/shard_map/all_to_all | solution.py:327
  106.3 0.6 pad_add_fusion.place_ref.refs_0_
  106.9 0.0 copy-start.8
  106.9 10.5 %shard_map.234.coef_hbm = f32[24,5,128,256]{3,2,1,0:T(8,128)} custom-call(bf16[24,128,256]{2,1,0:T(8,128)(2,1)} %get-tuple-element.45.x_ref, f32[24,128,256]{2,1,0:T(8,128)} %get-tuple-element.46.state_ref, s32[128,1]{1,0:T(8,128)} %copy.31.lens_ref, bf16[256,768]{1,0:T(8,128)(2,1)} %wx_ref.5, bf16[256,768]{1,0:T(8,128)(2,1)} %wh_ref.5, ...), custom_call_target="tpu_custom_call" | custom-call | tf_op jit(solution)/shard_map/pallas_call | solution.py:479
  117.4 2.8 %shard_map.233 = (bf16[512,256]{1,0:T(8,128)(2,1)}, f32[512,256]{1,0:T(8,128)}, bf16[784,256]{1,0:T(8,128)(2,1)}) custom-call(bf16[512,256]{1,0:T(8,128)(2,1)} %bitcast.35, bf16[512,256]{1,0:T(8,128)(2,1)} %bitcast.46, f32[512,1]{1,0:T(8,128)} %copy.33.keep_ref, bf16[1536,256]{1,0:T(8,128)(2,1)} %get-tuple-element.40.mid_ref, ...), custom_call_target="tpu_custom_call" | custom-call | tf_op jit(solution)/shard_map/pallas_call | solution.py:512
  120.3 14.3 %all-to-all-done.2 = bf16[32,64,256]{2,1,0:T(8,128)(2,1)S(1)} async-done(((bf16[32,64,256]{2,1,0:T(8,128)(2,1)}), bf16[32,64,256]{2,1,0:T(8,128)(2,1)S(1)}, u32[]{:S(2)}, u32[]{:S(2)}) %all-to-all-start.2) | async-done | bytes 1048608 | tf_op jit(solution)/shard_map/all_to_all | solution.py:327
  134.6 18.7 %shard_map.235 = (bf16[2048,256]{1,0:T(8,128)(2,1)}, f32[128,256]{1,0:T(8,128)}, bf16[24,128,1024]{2,1,0:T(8,128)(2,1)}, f32[8,768]{1,0:T(8,128)S(1)}) custom-call(bf16[2048,256]{1,0:T(8,128)(2,1)S(1)} %bitcast.33, s32[128,24]{1,0:T(8,128)S(1)} %copy-done.4, s32[24,128]{1,0:T(8,128)S(1)} %copy-done.7, bf16[128,256]{1,0:T(8,128)(2,1)S(1)} %bitcast.39, ...), custom_call_target="tpu_custom_call" | custom-call | tf_op jit(solution)/shard_map/pallas_call | solution.py:522
  153.3 0.0 copy-start.9
  153.3 0.6 copy-done.9
  153.9 8.9 %shard_map.237 = (bf16[1280,256]{1,0:T(8,128)(2,1)}, bf16[1280,256]{1,0:T(8,128)(2,1)}) custom-call(s32[2]{0:T(128)} %pad_add_fusion.place_ref.refs_0_, bf16[24,128,256]{2,1,0:T(8,128)(2,1)} %get-tuple-element.45.x_ref, bf16[24,128,256]{2,1,0:T(8,128)(2,1)} %get-tuple-element.50.prior_ref, bf16[24,128,1024]{2,1,0:T(8,128)(2,1)} %get-tuple-element.51.gate_ref, ...), custom_call_target="tpu_custom_call" | custom-call | tf_op jit(solution)/shard_map/pallas_call | solution.py:546
  162.8 0.0 collective-permute-start
  162.8 2.3 collective-permute-done.got_ref
  165.1 1.1 copy-done.3
  166.2 0.7 shard_map.238
  166.9 1.6 collective-permute-start.1
  168.5 1.1 collective-permute-start.2
  169.6 2.2 collective-permute-start.3
  171.7 2.3 collective-permute-done.1
  174.1 3.0 %collective-permute-done.2 = bf16[320,256]{1,0:T(8,128)(2,1)S(1)} collective-permute-done((bf16[320,256]{1,0:T(8,128)(2,1)S(1)}, bf16[320,256]{1,0:T(8,128)(2,1)S(1)}, u32[]{:S(2)}, u32[]{:S(2)}) %collective-permute-start.2) | collective-permute-done | bytes 163872 | tf_op jit(solution)/shard_map/ppermute | solution.py:396
  177.1 1.7 collective-permute-done.3
  178.8 0.1 add_convert_fusion
  178.9 0.1 reshape.84
  178.9 16.6 %all_to_all.30 = bf16[32,10,256]{2,1,0:T(8,128)(2,1)S(1)} all-to-all(bf16[32,10,256]{2,1,0:T(8,128)(2,1)S(1)} %reshape.84), channel_id=1, replica_groups=mesh['replica'=8,'outer'=4,'link'=8] {'outer','link'}, dimensions={0} | all-to-all | bytes 327680 | tf_op jit(solution)/shard_map/all_to_all | solution.py:327
  195.5 0.1 reduce_sum.12
  195.6 15.7 %all_to_all.31 = bf16[32,10,256]{2,1,0:T(8,128)(2,1)S(1)} all-to-all(bf16[32,10,256]{2,1,0:T(8,128)(2,1)S(1)} %broadcast_in_dim.41), channel_id=1, replica_groups=mesh['replica'=8,'outer'=4,'link'=8] {'outer','link'}, dimensions={0} | all-to-all | bytes 327680 | tf_op jit(solution)/shard_map/all_to_all | solution.py:327
  211.3 4.5 %all-to-all-start.3 = ((bf16[32,64,256]{2,1,0:T(8,128)(2,1)}), bf16[32,64,256]{2,1,0:T(8,128)(2,1)S(1)}, u32[]{:S(2)}, u32[]{:S(2)}) async-start(bf16[32,64,256]{2,1,0:T(8,128)(2,1)} %bitcast.20), calls=%async_computation.3 | async-start | bytes 2097152 | tf_op jit(solution)/shard_map/all_to_all | solution.py:327
  215.8 0.1 reshape.85.refs_1_
  215.9 0.8 collective-permute-start.6
  216.6 1.3 collective-permute-start.4
  218.0 3.4 %collective-permute-start.5 = (bf16[320,256]{1,0:T(8,128)(2,1)S(1)}, bf16[320,256]{1,0:T(8,128)(2,1)S(1)}, u32[]{:S(2)}, u32[]{:S(2)}) collective-permute-start(bf16[320,256]{1,0:T(8,128)(2,1)S(1)} %reshape.85.refs_1_), channel_id=1, source_target_pairs={{0,128},{32,160},{64,192},{96,224},{128,0},{160,32},{192,64},{224,... | collective-permute-start | bytes 491528 | tf_op jit(solution)/shard_map/ppermute | solution.py:402
  221.3 0.0 collective-permute-start.7
  221.3 1.5 collective-permute-done.6.refs_4_
  222.8 0.0 collective-permute-start.10
  222.8 0.0 collective-permute-done.4.refs_2_
  222.8 0.5 collective-permute-start.8
  223.3 1.4 collective-permute-done.5.refs_3_
  224.8 0.0 collective-permute-done.10.refs_8_
  224.8 1.4 collective-permute-done.9.refs_7_
  226.2 2.1 shard_map.239
  228.3 14.3 %all-to-all-done.3 = bf16[32,64,256]{2,1,0:T(8,128)(2,1)S(1)} async-done(((bf16[32,64,256]{2,1,0:T(8,128)(2,1)}), bf16[32,64,256]{2,1,0:T(8,128)(2,1)S(1)}, u32[]{:S(2)}, u32[]{:S(2)}) %all-to-all-start.3) | async-done | bytes 1048608 | tf_op jit(solution)/shard_map/all_to_all | solution.py:327
  242.6 1.0 copy-done.11
  243.6 2.9 %shard_map.236 = f32[512,256]{1,0:T(8,128)} custom-call(bf16[2048,256]{1,0:T(8,128)(2,1)} %bitcast.40, s32[16,128]{1,0:T(8,128)} %reshape_squeeze.3.srow_ref, f32[512,256]{1,0:T(8,128)} %get-tuple-element.48.direct_ref), custom_call_target="tpu_custom_call" | custom-call | tf_op jit(solution)/shard_map/pallas_call | solution.py:566
  (30 shorter events, 0.1 us)
Async XLA Ops:
  0.6 15.0 %copy-start.15 = (s32[1,128]{1,0:T(1,128)S(1)}, s32[1,128]{1,0:T(1,128)}, u32[]{:S(2)}) copy-start(s32[1,128]{1,0:T(1,128)} %param.18) | copy-start | bytes 1540
  0.7 1.0 copy-start.2
  1.6 0.7 copy-start.5
  2.3 13.3 %copy-start.14 = (s32[1,128,24]{1,2,0:T(8,128)S(1)}, s32[1,128,24]{1,2,0:T(8,128)}, u32[]{:S(2)}) copy-start(s32[1,128,24]{1,2,0:T(8,128)} %param.17) | copy-start | bytes 36868
  2.3 14.8 %copy-start.16 = (f32[768]{0:T(1024)S(1)}, f32[768]{0:T(1024)}, u32[]{:S(2)}) copy-start(f32[768]{0:T(1024)} %param.25) | copy-start | bytes 9220
  4.1 62.5 %copy-start.17 = (s32[1,512]{1,0:T(1,128)S(1)}, s32[1,512]{1,0:T(1,128)}, u32[]{:S(2)}) copy-start(s32[1,512]{1,0:T(1,128)} %param.19) | copy-start | bytes 6148
  4.1 63.9 %copy-start.6 = (s32[1,32,1,64]{3,2,1,0:T(1,128)S(1)}, s32[1,32,1,64]{3,2,1,0:T(1,128)}, u32[]{:S(2)}) copy-start(s32[1,32,1,64]{3,2,1,0:T(1,128)} %param.20) | copy-start | bytes 24580
  4.1 40.1 %all-to-all-start = ((bf16[32,64,256]{2,1,0:T(8,128)(2,1)}), bf16[32,64,256]{2,1,0:T(8,128)(2,1)S(1)}, u32[]{:S(2)}, u32[]{:S(2)}) async-start(bf16[32,64,256]{2,1,0:T(8,128)(2,1)} %bitcast.4), calls=%async_computation | async-start | bytes 2097152 | tf_op jit(solution)/shard_map/all_to_all | solution.py:327
  44.3 1.0 copy-start.12
  61.3 33.4 %all-to-all-start.1 = ((bf16[32,64,256]{2,1,0:T(8,128)(2,1)}), bf16[32,64,256]{2,1,0:T(8,128)(2,1)S(1)}, u32[]{:S(2)}, u32[]{:S(2)}) async-start(bf16[32,64,256]{2,1,0:T(8,128)(2,1)} %bitcast.44), calls=%async_computation.1 | async-start | bytes 2097152 | tf_op jit(solution)/shard_map/all_to_all | solution.py:327
  94.7 1.0 copy-start.13
  101.3 33.2 %all-to-all-start.2 = ((bf16[32,64,256]{2,1,0:T(8,128)(2,1)}), bf16[32,64,256]{2,1,0:T(8,128)(2,1)S(1)}, u32[]{:S(2)}, u32[]{:S(2)}) async-start(bf16[32,64,256]{2,1,0:T(8,128)(2,1)} %bitcast.43), calls=%async_computation.2 | async-start | bytes 2097152 | tf_op jit(solution)/shard_map/all_to_all | solution.py:327
  106.9 27.7 %copy-start = (bf16[256,768]{1,0:T(8,128)(2,1)S(1)}, bf16[256,768]{1,0:T(8,128)(2,1)}, u32[]{:S(2)}) copy-start(bf16[256,768]{1,0:T(8,128)(2,1)} %wx_ref.5) | copy-start | bytes 1179652
  106.9 27.7 %copy-start.1 = (bf16[256,768]{1,0:T(8,128)(2,1)S(1)}, bf16[256,768]{1,0:T(8,128)(2,1)}, u32[]{:S(2)}) copy-start(bf16[256,768]{1,0:T(8,128)(2,1)} %wh_ref.5) | copy-start | bytes 1179652
  106.9 27.7 %copy-start.4 = (s32[128,24]{1,0:T(8,128)S(1)}, s32[128,24]{1,0:T(8,128)}, u32[]{:S(2)}) copy-start(s32[128,24]{1,0:T(8,128)} %copy.30.slot_ref) | copy-start | bytes 36868
  106.9 27.7 %copy-start.7 = (s32[24,128]{1,0:T(8,128)S(1)}, s32[24,128]{1,0:T(8,128)}, u32[]{:S(2)}) copy-start(s32[24,128]{1,0:T(8,128)} %fusion.row_ref) | copy-start | bytes 36868
  106.9 27.7 %copy-start.8 = (bf16[1,128,256]{2,1,0:T(8,128)(2,1)S(1)}, bf16[1,128,256]{2,1,0:T(8,128)(2,1)}, u32[]{:S(2)}) copy-start(bf16[1,128,256]{2,1,0:T(8,128)(2,1)} %param.22) | copy-start | bytes 196612
  153.3 0.6 copy-start.9
  153.9 11.2 %copy-start.10 = (s32[2]{0:T(128)S(1)}, s32[2]{0:T(128)}, u32[]{:S(2)}) copy-start(s32[2]{0:T(128)} %pad_add_fusion.place_ref.refs_0_) | copy-start | bytes 28
  162.8 2.3 collective-permute-start
  165.1 1.1 copy-start.3
  166.9 7.1 %collective-permute-start.1 = (bf16[320,256]{1,0:T(8,128)(2,1)S(1)}, bf16[320,256]{1,0:T(8,128)(2,1)S(1)}, u32[]{:S(2)}, u32[]{:S(2)}) collective-permute-start(bf16[320,256]{1,0:T(8,128)(2,1)S(1)} %get-tuple-element.57), channel_id=1, source_target_pairs={{0,64},{32,96},{64,128},{96,160},{128,192},{160,224},{192,0},{224,... | collective-permute-start | bytes 491528 | tf_op jit(solution)/shard_map/ppermute | solution.py:396
  168.5 8.6 %collective-permute-start.2 = (bf16[320,256]{1,0:T(8,128)(2,1)S(1)}, bf16[320,256]{1,0:T(8,128)(2,1)S(1)}, u32[]{:S(2)}, u32[]{:S(2)}) collective-permute-start(bf16[320,256]{1,0:T(8,128)(2,1)S(1)} %get-tuple-element.58), channel_id=1, source_target_pairs={{0,128},{32,160},{64,192},{96,224},{128,0},{160,32},{192,64},{224,... | collective-permute-start | bytes 491528 | tf_op jit(solution)/shard_map/ppermute | solution.py:396
  169.6 9.2 %collective-permute-start.3 = (bf16[320,256]{1,0:T(8,128)(2,1)S(1)}, bf16[320,256]{1,0:T(8,128)(2,1)S(1)}, u32[]{:S(2)}, u32[]{:S(2)}) collective-permute-start(bf16[320,256]{1,0:T(8,128)(2,1)S(1)} %get-tuple-element.59), channel_id=1, source_target_pairs={{0,192},{32,224},{64,0},{96,32},{128,64},{160,96},{192,128},{224,1... | collective-permute-start | bytes 491528 | tf_op jit(solution)/shard_map/ppermute | solution.py:396
  211.3 31.3 %all-to-all-start.3 = ((bf16[32,64,256]{2,1,0:T(8,128)(2,1)}), bf16[32,64,256]{2,1,0:T(8,128)(2,1)S(1)}, u32[]{:S(2)}, u32[]{:S(2)}) async-start(bf16[32,64,256]{2,1,0:T(8,128)(2,1)} %bitcast.20), calls=%async_computation.3 | async-start | bytes 2097152 | tf_op jit(solution)/shard_map/all_to_all | solution.py:327
  215.9 7.0 %collective-permute-start.6 = (bf16[320,256]{1,0:T(8,128)(2,1)S(1)}, bf16[320,256]{1,0:T(8,128)(2,1)S(1)}, u32[]{:S(2)}, u32[]{:S(2)}) collective-permute-start(bf16[320,256]{1,0:T(8,128)(2,1)S(1)} %reshape.85.refs_1_), channel_id=1, source_target_pairs={{0,192},{32,224},{64,0},{96,32},{128,64},{160,96},{192,128},{224,1... | collective-permute-start | bytes 491528 | tf_op jit(solution)/shard_map/ppermute | solution.py:402
  216.6 6.2 %collective-permute-start.4 = (bf16[320,256]{1,0:T(8,128)(2,1)S(1)}, bf16[320,256]{1,0:T(8,128)(2,1)S(1)}, u32[]{:S(2)}, u32[]{:S(2)}) collective-permute-start(bf16[320,256]{1,0:T(8,128)(2,1)S(1)} %reshape.85.refs_1_), channel_id=1, source_target_pairs={{0,64},{32,96},{64,128},{96,160},{128,192},{160,224},{192,0},{224,... | collective-permute-start | bytes 491528 | tf_op jit(solution)/shard_map/ppermute | solution.py:402
  218.0 6.8 %collective-permute-start.5 = (bf16[320,256]{1,0:T(8,128)(2,1)S(1)}, bf16[320,256]{1,0:T(8,128)(2,1)S(1)}, u32[]{:S(2)}, u32[]{:S(2)}) collective-permute-start(bf16[320,256]{1,0:T(8,128)(2,1)S(1)} %reshape.85.refs_1_), channel_id=1, source_target_pairs={{0,128},{32,160},{64,192},{96,224},{128,0},{160,32},{192,64},{224,... | collective-permute-start | bytes 491528 | tf_op jit(solution)/shard_map/ppermute | solution.py:402
  221.3 3.5 %collective-permute-start.7 = (bf16[320,256]{1,0:T(8,128)(2,1)S(1)}, bf16[320,256]{1,0:T(8,128)(2,1)S(1)}, u32[]{:S(2)}, u32[]{:S(2)}) collective-permute-start(bf16[320,256]{1,0:T(8,128)(2,1)S(1)} %reshape.85.refs_1_), channel_id=1, source_target_pairs={{0,32},{32,0},{64,96},{96,64},{128,160},{160,128},{192,224},{224,1... | collective-permute-start | bytes 491528 | tf_op jit(solution)/shard_map/ppermute | solution.py:404
  222.8 2.0 collective-permute-start.10
  222.8 2.0 collective-permute-start.8
  224.8 1.4 collective-permute-start.9
  242.6 1.0 copy-start.11

commit v3 on v2

--- a/solution.py
+++ b/solution.py
@@ -8,6 +8,7 @@
 F32 = jnp.float32
 BF = jnp.bfloat16
 INTERPRET = False
+BACK = 49
 OL = ("outer", "link")
 
 
@@ -75,37 +76,48 @@
         copy.wait()
 
 
-def fetch_hops(table_ref, slot_ref, out_ref, per=4):
+def fetch_hops(table_ref, slot_ref, out_ref, wide_ref, per=4):
     flows, hops = slot_ref.shape
     slots = table_ref.shape[0]
-    table = table_ref[...]
     cols = slot_ref[...]
-    for t in range(0, hops, per):
+    for t in range(hops):
+        wide_ref[t] = jnp.broadcast_to(cols[:, t : t + 1], (flows, 128))
+    lanes = lax.broadcasted_iota(jnp.int32, (per * flows, 128), 1)
+
+    def step(i, carry):
+        at = pl.ds(i * per, per)
+        idx = wide_ref[at].reshape(per * flows, 128)
         sel = jnp.concatenate(
-            [pick_cols(cols[:, k : k + 1], slots) for k in range(t, t + per)], axis=0
+            [jnp.where(lanes + b == idx, 1.0, 0.0).astype(BF) for b in range(0, slots, 128)],
+            axis=1,
         )
-        rows = dot(sel, table).astype(out_ref.dtype)
-        for k in range(per):
-            out_ref[t + k] = rows[k * flows : (k + 1) * flows]
+        rows = dot(sel, table_ref[...])
+        out_ref[at] = rows.reshape(per, flows, rows.shape[1]).astype(out_ref.dtype)
+        return carry
+
+    lax.fori_loop(0, hops // per, step, 0, unroll=6)
 
 
 def sum_slots(row_ref, rows, buf_ref, out_hbm, sem, block=512):
     hops = row_ref.shape[0]
     slots = buf_ref.shape[0]
     idx = row_ref[...]
-    copies = []
-    for k, q in enumerate(range(0, slots, block)):
+
+    def step(k, carry):
+        q = pl.multiple_of(k * block, block)
         sel = jnp.concatenate([pick_rows(idx[t : t + 1, :], block, q) for t in range(hops)], axis=1)
-        buf_ref[q : q + block, :] = dot(sel, rows).astype(BF)
-        copies.append(send(buf_ref, out_hbm, sem, q, block, k))
-        copies[-1].start()
-    return copies
+        buf_ref[pl.ds(q, block), :] = dot(sel, rows).astype(BF)
+        send(buf_ref, out_hbm, sem, q, block, k).start()
+        return carry
+
+    lax.fori_loop(0, slots // block, step, 0, unroll=1)
+    return [send(buf_ref, out_hbm, sem, k * block, block, k) for k in range(slots // block)]
 
 
 def forward_kernel(
     table_ref, slot_ref, row_ref, lens_ref, path_ref, wx_ref, wh_ref, bias_ref,
     x_hbm, state_hbm, prior_hbm, part_hbm, pathout_ref,
-    x_ref, state_ref, prior_ref, gi_ref, hb_ref, part_ref, sem, sem_part,
+    x_ref, state_ref, prior_ref, gi_ref, hb_ref, part_ref, wide_ref, sem, sem_part,
 ):
     hops, flows, width = x_ref.shape
     outs = [
@@ -113,7 +125,7 @@
         pltpu.make_async_copy(state_ref, state_hbm, sem.at[1]),
         pltpu.make_async_copy(prior_ref, prior_hbm, sem.at[2]),
     ]
-    fetch_hops(table_ref, slot_ref, x_ref)
+    fetch_hops(table_ref, slot_ref, x_ref, wide_ref)
     outs[0].start()
     per = 4
     for t in range(0, hops, per):
@@ -135,7 +147,7 @@
         hb_ref[t] = h.astype(BF)
         return h
 
-    h = lax.fori_loop(0, hops, step, path_ref[...].astype(F32), unroll=4)
+    h = lax.fori_loop(0, hops, step, path_ref[...].astype(F32), unroll=2)
     outs[1].start()
     outs[2].start()
     pathout_ref[...] = h.astype(BF)
@@ -219,21 +231,28 @@
 
 
 def backward_kernel(
-    table_ref, slot_ref, row_ref, pgrad_ref, wx_ref, wh_ref, coef_hbm,
-    part_hbm, pathgrad_ref, gate_hbm, db_ref,
-    hg_ref, coef_ref, gate_ref, dx_ref, part_ref, sem_in, sem_out, sem_part,
+    place_ref, table_ref, slot_ref, pgrad_ref, wx_ref, wh_ref, mlp_hbm, coef_hbm, x_hbm, prior_hbm,
+    pathgrad_ref, dx_hbm, mine_ref, other_ref,
+    hg_ref, coef_ref, gate_ref, dx_ref, x_ref, prior_ref, pack_ref, db_ref, wide_ref, sem_in, sem,
 ):
     hops, flows, width = hg_ref.shape
+    rows = hops * flows
 
     def load(t):
         return pltpu.make_async_copy(coef_hbm.at[t], coef_ref.at[t], sem_in.at[t])
 
-    def store(t):
-        return pltpu.make_async_copy(gate_ref.at[t], gate_hbm.at[t], sem_out.at[t])
-
     for t in range(hops - 1, -1, -1):
         load(t).start()
-    fetch_hops(table_ref, slot_ref, hg_ref)
+    extra = [
+        pltpu.make_async_copy(x_hbm, x_ref, sem.at[0]),
+        pltpu.make_async_copy(prior_hbm, prior_ref, sem.at[1]),
+        pltpu.make_async_copy(
+            mlp_hbm, pack_ref.at[pl.ds(6 * width, mlp_hbm.shape[0]), :], sem.at[3]
+        ),
+    ]
+    for copy in extra:
+        copy.start()
+    fetch_hops(table_ref, slot_ref, hg_ref, wide_ref)
     db_ref[...] = jnp.zeros(db_ref.shape, F32)
 
     def fold(v):
@@ -246,73 +265,56 @@
         az = g * coef_ref[t, 1]
         ar = g * coef_ref[t, 2]
         an = g * coef_ref[t, 3]
-        dgs = jnp.concatenate(
-            [az.astype(BF), ar.astype(BF), (an * coef_ref[t, 4]).astype(BF)], axis=1
-        )
-        nxt = g * coef_ref[t, 0] + dot_nt(dgs, wh_ref[...])
-        gate_ref[t, :, :width] = an.astype(BF)
-        gate_ref[t, :, width:] = dgs
-        store(t).start()
+        anb = an.astype(BF)
+        azb = az.astype(BF)
+        arb = ar.astype(BF)
+        cnb = (an * coef_ref[t, 4]).astype(BF)
+        nxt = g * coef_ref[t, 0] + dot_nt(jnp.concatenate([azb, arb, cnb], axis=1), wh_ref[...])
+        for k, gate in enumerate((anb, azb, arb, cnb)):
+            gate_ref[k, t] = gate
+        dx_ref[t] = dot_nt(jnp.concatenate([azb, arb, anb], axis=1), wx_ref[...]).astype(BF)
         db_ref[:, :width] += fold(az)
         db_ref[:, width : 2 * width] += fold(ar)
         db_ref[:, 2 * width :] += fold(an)
         return nxt
 
-    g = lax.fori_loop(0, hops, step, pgrad_ref[...].astype(F32), unroll=4)
+    g = lax.fori_loop(0, hops, step, pgrad_ref[...].astype(F32), unroll=2)
+    dx_out = pltpu.make_async_copy(dx_ref, dx_hbm, sem.at[2])
+    dx_out.start()
     pathgrad_ref[...] = g
-    wx = jnp.concatenate([wx_ref[:, 2 * width :], wx_ref[:, : 2 * width]], axis=1)
-    per = 4
-    for t in range(0, hops, per):
-        rows = gate_ref[t : t + per, :, : 3 * width].reshape(per * flows, 3 * width)
-        dx_ref[t * flows : (t + per) * flows, :] = dot_nt(rows, wx).astype(BF)
-    for copy in sum_slots(row_ref, dx_ref[...], part_ref, part_hbm, sem_part):
+    for copy in extra:
         copy.wait()
-    for t in range(hops):
-        store(t).wait()
-
-
-def weight_kernel(
-    place_ref, x_ref, prior_ref, gate_ref, db_ref, mlp_ref,
-    mine_ref, other_ref, pack_ref, awx_ref, awh_ref,
-):
-    per, flows, width = x_ref.shape
-    i = pl.program_id(0)
-    rows = per * flows
-    gates = gate_ref[...].reshape(rows, 4 * width)
-    gx = dot_tn(x_ref[...].reshape(rows, width), gates[:, : 3 * width])
-    gh = dot_tn(prior_ref[...].reshape(rows, width), gates[:, width:])
-
-    @pl.when(i == 0)
-    def _():
-        awx_ref[...] = gx
-        awh_ref[...] = gh
-
-    @pl.when(i > 0)
-    def _():
-        awx_ref[...] += gx
-        awh_ref[...] += gh
-
-    @pl.when(i == pl.num_programs(0) - 1)
-    def _():
-        for k in range(3):
-            s = slice(k * width, (k + 1) * width)
-            to = (k + 2) % 3
-            pack_ref[to * width : (to + 1) * width, :] = awx_ref[:, s].astype(BF)
-            pack_ref[(3 + k) * width : (4 + k) * width, :] = awh_ref[:, s].astype(BF)
-        base = 9 * width
-        pack_ref[6 * width : base + 16, :] = mlp_ref[...]
-        b = jnp.sum(db_ref[...], axis=0, keepdims=True)
-        tail = jnp.concatenate(
-            [b[:, k * width : (k + 1) * width] for k in range(3)] + [jnp.zeros((13, width), F32)],
-            axis=0,
-        )
-        pack_ref[base + 16 : base + 32, :] = tail.astype(BF)
-        rest = pack_ref.shape[0] - base - 32
-        pack_ref[base + 32 :, :] = jnp.zeros((rest, width), BF)
-        half = mine_ref.shape[0]
-        core = place_ref[1]
-        mine_ref[...] = pack_ref[pl.ds(pl.multiple_of(core * half, 256), half), :]
-        other_ref[...] = pack_ref[pl.ds(pl.multiple_of((1 - core) * half, 256), half), :]
+    base = 9 * width
+
+    def outer(k, carry):
+        to = pl.multiple_of(lax.rem(k + 2, 3) * width, width)
+        col = gate_ref[k].reshape(rows, width)
+        pack_ref[pl.ds(to, width), :] = dot_tn(x_ref[...].reshape(rows, width), col).astype(BF)
+        to = pl.multiple_of((k + 3) * width, width)
+        col = gate_ref[k + 1].reshape(rows, width)
+        pack_ref[pl.ds(to, width), :] = dot_tn(prior_ref[...].reshape(rows, width), col).astype(BF)
+        return carry
+
+    lax.fori_loop(0, 3, outer, 0, unroll=1)
+    b = jnp.sum(db_ref[...], axis=0, keepdims=True)
+    tail = jnp.concatenate(
+        [b[:, k * width : (k + 1) * width] for k in range(3)] + [jnp.zeros((13, width), F32)],
+        axis=0,
+    )
+    pack_ref[base + 16 : base + 32, :] = tail.astype(BF)
+    pack_ref[base + 32 :, :] = jnp.zeros((pack_ref.shape[0] - base - 32, width), BF)
+    half = mine_ref.shape[0]
+    core = place_ref[1]
+    mine_ref[...] = pack_ref[pl.ds(pl.multiple_of(core * half, 256), half), :]
+    other_ref[...] = pack_ref[pl.ds(pl.multiple_of((1 - core) * half, 256), half), :]
+    dx_out.wait()
+
+
+def sums_kernel(row_ref, dx_ref, out_hbm, buf_ref, sem):
+    hops, flows, width = dx_ref.shape
+    rows = dx_ref[...].reshape(hops * flows, width)
+    for copy in sum_slots(row_ref, rows, buf_ref, out_hbm, sem):
+        copy.wait()
 
 
 def finish_kernel(got_ref, srow_ref, direct_ref, out_ref):
@@ -345,6 +347,30 @@
         rows = pl.ds(pl.multiple_of(lax.rem(x + k, chips) * part, 64), part)
         both = pack_ref[rows, :].astype(F32) + got_ref[rows, :].astype(F32)
         out_refs[k][...] = both.astype(BF)
+
+
+def link_join_kernel(place_ref, *refs):
+    out_ref = refs[-1]
+    count = out_ref.shape[0]
+    for k in range(count):
+        out_ref[lax.rem(place_ref[3] - k + count, count)] = refs[k][...]
+
+
+def outer_join_kernel(place_ref, *refs):
+    out_ref = refs[-1]
+    count = len(refs) - 1
+    rows = refs[0].shape[0]
+    for k in range(count):
+        to = lax.rem(place_ref[2] - k + count, count)
+        out_ref[pl.ds(pl.multiple_of(to * rows, 16), rows), :] = refs[k][...]
+
+
+def around(piece, axis):
+    count = lax.axis_size(axis)
+    got = [piece]
+    for k in range(1, count):
+        got.append(lax.ppermute(piece, axis, [(i, (i + k) % count) for i in range(count)]))
+    return got
 
 
 def unpack_kernel(place_ref, *refs, scale):
@@ -375,7 +401,8 @@
 
 def whereabouts():
     rep = lax.axis_index("replica")
-    return jnp.stack([rep // 2, rep % 2]).astype(jnp.int32)
+    spots = [rep // 2, rep % 2, lax.axis_index("outer"), lax.axis_index("link")]
+    return jnp.stack(spots).astype(jnp.int32)
 
 
 def sum_everywhere(mine, other, place, scale):
@@ -393,10 +420,19 @@
     mine = call(
         pair_kernel, (sds((part, width), BF),) * chips, in_specs=[smem, vmem, vmem]
     )(place, mine, got)
-    got = [lax.ppermute(mine[k], "replica", ahead[k]) for k in range(1, chips)]
+    got = []
+    for k in range(1, chips):
+        got.append(lax.ppermute(mine[k], "replica", ahead[k]))
     mine = sum((g.astype(F32) for g in got), mine[0].astype(F32)).astype(BF)
     mine = total(swap(mine.reshape(group, part // group, width)))
-    mine = swap(jnp.broadcast_to(mine[None], (group,) + mine.shape)).reshape(part, width)
+    got = around(mine, "link")
+    mine = call(
+        link_join_kernel, sds((len(got),) + mine.shape, BF), in_specs=[smem] + [vmem] * len(got)
+    )(place, *got).reshape(-1, width)
+    got = around(mine, "outer")
+    mine = call(
+        outer_join_kernel, sds((part, width), BF), in_specs=[smem] + [vmem] * len(got)
+    )(place, *got)
     whole = [mine]
     for k in range(1, chips):
         whole.append(lax.ppermute(mine, "replica", ahead[k]))
@@ -467,13 +503,14 @@
             pltpu.VMEM((hops, flows, wide), F32),
             pltpu.VMEM((hops, flows, width), BF),
             *rows_out,
+            pltpu.VMEM((hops, flows, 128), jnp.int32),
             pltpu.SemaphoreType.DMA((3,)),
             pltpu.SemaphoreType.DMA((slots // 512,)),
         ],
     )(fetched, slot_col, slot_row, lens_col, path_in[0], gru_wx, gru_wh, bias)
     arrived = swap_named(part, group)
 
-    per = 4
+    per = 2
     steps = lambda *tail: pl.BlockSpec((per,) + tail, lambda i: (i,) + (0,) * len(tail))
     whole = lambda *shape: pl.BlockSpec(shape, lambda i: (0,) * len(shape))
     coef = call(
@@ -519,50 +556,39 @@
         mib=58,
     )(link_rows, link_grad[0], keep, mids, db1, mlp_w1, mlp_w2, mlp_b2[None])
 
-    dpart, path_back, gates, db = call(
+    path_back, dx, mine, other = call(
         backward_kernel,
         (
-            sds((slots, width), BF),
             sds((flows, width), F32),
-            sds((hops, flows, 4 * width), BF),
-            sds((8, wide), F32),
+            sds((hops, flows, width), BF),
+            sds((5 * width, width), BF),
+            sds((5 * width, width), BF),
         ),
-        mib=51,
-        in_specs=[vmem] * 6 + [hbm],
-        out_specs=[hbm, vmem, hbm, vmem],
+        mib=BACK,
+        in_specs=[smem] + [vmem] * 5 + [hbm] * 4,
+        out_specs=[vmem, hbm, vmem, vmem],
         scratch_shapes=[
             pltpu.VMEM((hops, flows, width), BF),
             pltpu.VMEM((hops, 5, flows, width), F32),
-            pltpu.VMEM((hops, flows, 4 * width), BF),
-            pltpu.VMEM((hops * flows, width), BF),
-            *rows_out,
+            pltpu.VMEM((4, hops, flows, width), BF),
+            pltpu.VMEM((hops, flows, width), BF),
+            pltpu.VMEM((hops, flows, width), BF),
+            pltpu.VMEM((hops, flows, width), BF),
+            pltpu.VMEM((10 * width, width), BF),
+            pltpu.VMEM((8, wide), F32),
+            pltpu.VMEM((hops, flows, 128), jnp.int32),
             pltpu.SemaphoreType.DMA((hops,)),
-            pltpu.SemaphoreType.DMA((hops,)),
-            pltpu.SemaphoreType.DMA((slots // 512,)),
+            pltpu.SemaphoreType.DMA((4,)),
         ],
-    )(returned, slot_col, slot_row, path_grad[0], gru_wx, gru_wh, coef)
+    )(place, returned, slot_col, path_grad[0], gru_wx, gru_wh, mlp_pack, coef, x, priors)
+    dpart = call(
+        sums_kernel,
+        sds((slots, width), BF),
+        mib=58,
+        out_specs=hbm,
+        scratch_shapes=rows_out + [pltpu.SemaphoreType.DMA((slots // 512,))],
+    )(slot_row, dx)
     owned = swap_named(dpart, group)
-
-    mine, other = call(
-        weight_kernel,
-        (sds((5 * width, width), BF),) * 2,
-        mib=58,
-        grid=(hops // per,),
-        in_specs=[
-            smem,
-            steps(flows, width),
-            steps(flows, width),
-            steps(flows, 4 * width),
-            whole(8, wide),
-            whole(3 * width + 16, width),
-        ],
-        out_specs=[whole(5 * width, width)] * 2,
-        scratch_shapes=[
-            pltpu.VMEM((10 * width, width), BF),
-            pltpu.VMEM((width, wide), F32),
-            pltpu.VMEM((width, wide), F32),
-        ],
-    )(place, x, priors, gates, db, mlp_pack)
     link_back = call(finish_kernel, sds((links, width), F32), mib=58)(owned, serve_row, direct)
 
     count = lax.axis_size("replica") * lax.axis_size("outer") * lax.axis_size("link")

time: 248 us -> 253 us (1.020); the launches traced: 246 us -> 248 us
  blocking collectives: 32.3 us -> 0 us
  starting transfers between devices: 37 us -> 60.2 us
  waiting for transfers between devices: 93.5 us -> 103 us
    all_to_all x2 -> x0, blocking collectives: 32.3 us -> none  [swap(): lax.all_to_all(blocks, axes, split_axis=0, concat_axis=0, tiled=True, axi...]
    ppermute x3 -> x13, waiting for transfers between devices: 7.04 us -> 26.8 us  [the longest x10 19.7 us: around(): lax.ppermute(piece, axis, [(i, (i + k) % count) for i in range(count)])]
    ppermute x3 -> x13, starting transfers between devices: 4.84 us -> 24.1 us  [the longest x10 19.3 us: around(): lax.ppermute(piece, axis, [(i, (i + k) % count) for i in range(count)])]
    all_to_all x4 -> x5, waiting for transfers between devices: 79.8 us -> 68.5 us  [swap(): lax.all_to_all(blocks, axes, split_axis=0, concat_axis=0, tiled=True, axi...]
    all_to_all x4 -> x5, starting transfers between devices: 26.2 us -> 31.1 us  [swap(): lax.all_to_all(blocks, axes, split_axis=0, concat_axis=0, tiled=True, axi...]
    pallas_call x1, Pallas kernels: 10.5 us -> 13.6 us  [body(): call(coef_kernel, sds((hops, 5, flows, width), F32), mib=58, grid=(hops /...]
    pallas_call x2 -> x4, Pallas kernels: 27.6 us -> 25.3 us  [the longest x1 18 us: body(): call(backward_kernel, (sds((flows, width), F32), sds((hops, flows, width)...]
    unnamed x37 -> x31, local copies, waits for them, and re-layouts: 6.84 us -> 6.2 us
  transfers between devices with their start and end apart: 15 -> 26, of which waited for: 11 -> 16; matrix products, arithmetic and copies ran while one was open for 2% -> 2% of each run, Pallas kernels for 6% -> 10%
where the time goes in v3:
time: 253 us; the launch traced here: 248 us
  waiting for transfers between devices  103 us (41%)
  Pallas kernels  71.9 us (28%)
  starting transfers between devices  60.2 us (24%)
  local copies, waits for them, and re-layouts  10.6 us (4%)
    all_to_all x5, waiting for transfers between devices, swap(): lax.all_to_all(blocks, axes, split_axis=0, concat_axis=0, tiled=True, axi...  68.5 us
    all_to_all x5, starting transfers between devices, swap(): lax.all_to_all(blocks, axes, split_axis=0, concat_axis=0, tiled=True, axi...  31.1 us
    ppermute x10, waiting for transfers between devices, around(): lax.ppermute(piece, axis, [(i, (i + k) % count) for i in range(count)])  19.7 us
    ppermute x10, starting transfers between devices, around(): lax.ppermute(piece, axis, [(i, (i + k) % count) for i in range(count)])  19.3 us
    pallas_call x1, Pallas kernels, body(): call(backward_kernel, (sds((flows, width), F32), sds((hops, flows, width)...  18 us
    pallas_call x1, Pallas kernels, body(): call(forward_kernel, (sds((hops, flows, width), BF), sds((hops, flows, wi...  17 us
    pallas_call x1, Pallas kernels, body(): call(coef_kernel, sds((hops, 5, flows, width), F32), mib=58, grid=(hops /...  13.6 us
    ppermute x3, waiting for transfers between devices, sum_everywhere(): got.append(lax.ppermute(mine[k], 'replica', ahead[k]))  7.04 us
  transfers between devices with their start and end apart: 26, of which 16 were waited for; matrix products, arithmetic and copies ran while one was open for 2% of the time, Pallas kernels for 10%

profile of v3, /device:TPU:2, one launch (start us, length us, event | category | flops | bytes accessed | tf_op | source)
XLA Modules:
  0.0 248.3 jit_solution(8426370573236749091)
XLA Ops:
  0.7 0.9 copy-done.2
  1.6 0.7 copy-done.5
  2.3 1.8 shard_map.230
  4.1 11.5 %all-to-all-start = ((bf16[32,64,256]{2,1,0:T(8,128)(2,1)}), bf16[32,64,256]{2,1,0:T(8,128)(2,1)S(1)}, u32[]{:S(2)}, u32[]{:S(2)}) async-start(bf16[32,64,256]{2,1,0:T(8,128)(2,1)} %bitcast.4), calls=%async_computation | async-start | bytes 2097152 | tf_op jit(solution)/shard_map/all_to_all | solution.py:329
  15.6 0.6 broadcast_in_dim.28.bias_ref
  16.2 0.7 copy.30.slot_ref
  17.0 0.7 copy.31.lens_ref
  17.7 0.6 fusion.row_ref
  18.3 26.0 %all-to-all-done = bf16[32,64,256]{2,1,0:T(8,128)(2,1)S(1)} async-done(((bf16[32,64,256]{2,1,0:T(8,128)(2,1)}), bf16[32,64,256]{2,1,0:T(8,128)(2,1)S(1)}, u32[]{:S(2)}, u32[]{:S(2)}) %all-to-all-start) | async-done | bytes 1048608 | tf_op jit(solution)/shard_map/all_to_all | solution.py:329
  44.3 1.0 copy-done.9
  45.3 17.0 %shard_map.231 = (bf16[24,128,256]{2,1,0:T(8,128)(2,1)}, f32[24,128,256]{2,1,0:T(8,128)}, bf16[24,128,256]{2,1,0:T(8,128)(2,1)}, bf16[2048,256]{1,0:T(8,128)(2,1)}, bf16[128,256]{1,0:T(8,128)(2,1)}) custom-call(bf16[2048,256]{1,0:T(8,128)(2,1)} %bitcast.44, s32[128,24]{1,0:T(8,128)} %copy.30.slot_ref, s32[24,128]{1,0:T(8,128)} %fusion.row_ref, ...), custom_call_target="tpu_custom_call" | custom-call | tf_op jit(solution)/shard_map/pallas_call | solution.py:488
  62.3 5.1 %all-to-all-start.1 = ((bf16[32,64,256]{2,1,0:T(8,128)(2,1)}), bf16[32,64,256]{2,1,0:T(8,128)(2,1)S(1)}, u32[]{:S(2)}, u32[]{:S(2)}) async-start(bf16[32,64,256]{2,1,0:T(8,128)(2,1)} %bitcast.47), calls=%async_computation.1 | async-start | bytes 2097152 | tf_op jit(solution)/shard_map/all_to_all | solution.py:329
  67.4 0.5 broadcast.14
  67.9 0.7 reduce.4
  68.6 0.7 reshape_squeeze.3.srow_ref
  69.2 0.9 copy.33.keep_ref
  70.1 25.5 %all-to-all-done.1 = bf16[32,64,256]{2,1,0:T(8,128)(2,1)S(1)} async-done(((bf16[32,64,256]{2,1,0:T(8,128)(2,1)}), bf16[32,64,256]{2,1,0:T(8,128)(2,1)S(1)}, u32[]{:S(2)}, u32[]{:S(2)}) %all-to-all-start.1) | async-done | bytes 1048608 | tf_op jit(solution)/shard_map/all_to_all | solution.py:329
  95.6 1.0 copy-done.10
  96.7 5.6 %shard_map.232 = (bf16[2048,256]{1,0:T(8,128)(2,1)}, bf16[1536,256]{1,0:T(8,128)(2,1)}, f32[1,256]{1,0:T(1,128)}) custom-call(bf16[2048,256]{1,0:T(8,128)(2,1)} %bitcast.45, s32[16,128]{1,0:T(8,128)} %reshape_squeeze.3.srow_ref, s32[32,64]{1,0:T(8,128)} %bitcast.39, bf16[512,256]{1,0:T(8,128)(2,1)} %bitcast.36, bf16[512,256]{1,0:T(8,128)(2,1)} %bitcast.48, ...), custom_call_target="tpu_custom_call" | custom-call | tf_op jit(solution)/shard_map/pallas_call | solution.py:532
  102.3 5.1 %all-to-all-start.2 = ((bf16[32,64,256]{2,1,0:T(8,128)(2,1)}), bf16[32,64,256]{2,1,0:T(8,128)(2,1)S(1)}, u32[]{:S(2)}, u32[]{:S(2)}) async-start(bf16[32,64,256]{2,1,0:T(8,128)(2,1)} %bitcast.46), calls=%async_computation.2 | async-start | bytes 2097152 | tf_op jit(solution)/shard_map/all_to_all | solution.py:329
  107.5 13.6 %shard_map.234.coef_hbm = f32[24,5,128,256]{3,2,1,0:T(8,128)} custom-call(bf16[24,128,256]{2,1,0:T(8,128)(2,1)} %get-tuple-element.44.x_ref.x_hbm, f32[24,128,256]{2,1,0:T(8,128)} %get-tuple-element.45.state_ref, s32[128,1]{1,0:T(8,128)} %copy.31.lens_ref, bf16[256,768]{1,0:T(8,128)(2,1)} %wx_ref.5, bf16[256,768]{1,0:T(8,128)(2,1)} %wh_ref.5, ...), custom_call_target="tpu_custom_call" | custom-call | tf_op jit(solution)/shard_map/pallas_call | solution.py:516
  121.1 2.9 %shard_map.233 = (bf16[512,256]{1,0:T(8,128)(2,1)}, f32[512,256]{1,0:T(8,128)}, bf16[784,256]{1,0:T(8,128)(2,1)}) custom-call(bf16[512,256]{1,0:T(8,128)(2,1)} %bitcast.37, bf16[512,256]{1,0:T(8,128)(2,1)} %bitcast.49, f32[512,1]{1,0:T(8,128)} %copy.33.keep_ref, bf16[1536,256]{1,0:T(8,128)(2,1)} %get-tuple-element.38.mid_ref, ...), custom_call_target="tpu_custom_call" | custom-call | tf_op jit(solution)/shard_map/pallas_call | solution.py:549
  124.0 11.4 %all-to-all-done.2 = bf16[32,64,256]{2,1,0:T(8,128)(2,1)S(1)} async-done(((bf16[32,64,256]{2,1,0:T(8,128)(2,1)}), bf16[32,64,256]{2,1,0:T(8,128)(2,1)S(1)}, u32[]{:S(2)}, u32[]{:S(2)}) %all-to-all-start.2) | async-done | bytes 1048608 | tf_op jit(solution)/shard_map/all_to_all | solution.py:329
  135.5 1.0 copy-done.4
  136.5 18.0 %shard_map.235 = (f32[128,256]{1,0:T(8,128)}, bf16[24,128,256]{2,1,0:T(8,128)(2,1)}, bf16[1280,256]{1,0:T(8,128)(2,1)S(1)}, bf16[1280,256]{1,0:T(8,128)(2,1)S(1)}) custom-call(s32[4]{0:T(128)S(1)} %pad_add_fusion.place_ref.refs_0_, bf16[2048,256]{1,0:T(8,128)(2,1)S(1)} %bitcast.35, s32[128,24]{1,0:T(8,128)S(1)} %copy-done.3, bf16[128,256]{1,0:T(8,128)(2,1)S(1)} %bitcast.41, ...), custom_call_target="tpu_custom_call" | custom-call | tf_op jit(solution)/shard_map/pallas_call | solution.py:559
  154.5 0.1 collective-permute-start
  154.6 2.1 collective-permute-done.got_ref
  156.7 0.7 shard_map.238
  157.4 1.6 collective-permute-start.1
  159.0 1.1 collective-permute-start.2
  160.1 2.2 collective-permute-start.3
  162.2 2.3 collective-permute-done.1
  164.5 3.0 %collective-permute-done.2 = bf16[320,256]{1,0:T(8,128)(2,1)S(1)} collective-permute-done((bf16[320,256]{1,0:T(8,128)(2,1)S(1)}, bf16[320,256]{1,0:T(8,128)(2,1)S(1)}, u32[]{:S(2)}, u32[]{:S(2)}) %collective-permute-start.2) | collective-permute-done | bytes 163872 | tf_op jit(solution)/shard_map/ppermute | solution.py:425
  167.5 1.7 collective-permute-done.3
  169.4 0.8 reshape.83
  170.1 4.9 %all-to-all-start.4 = ((bf16[32,10,256]{2,1,0:T(8,128)(2,1)}), bf16[32,10,256]{2,1,0:T(8,128)(2,1)S(1)}, u32[]{:S(2)}, u32[]{:S(2)}) async-start(bf16[32,10,256]{2,1,0:T(8,128)(2,1)} %reshape.83), calls=%async_computation.4 | async-start | bytes 524288 | tf_op jit(solution)/shard_map/all_to_all | solution.py:329
  175.1 6.2 %shard_map.236 = bf16[2048,256]{1,0:T(8,128)(2,1)} custom-call(s32[24,128]{1,0:T(8,128)} %fusion.row_ref, bf16[24,128,256]{2,1,0:T(8,128)(2,1)} %get-tuple-element.47.dx_ref), custom_call_target="tpu_custom_call" | custom-call | tf_op jit(solution)/shard_map/pallas_call | solution.py:584
  181.3 5.6 %all-to-all-done.4 = bf16[32,10,256]{2,1,0:T(8,128)(2,1)S(1)} async-done(((bf16[32,10,256]{2,1,0:T(8,128)(2,1)}), bf16[32,10,256]{2,1,0:T(8,128)(2,1)S(1)}, u32[]{:S(2)}, u32[]{:S(2)}) %all-to-all-start.4) | async-done | bytes 163872 | tf_op jit(solution)/shard_map/all_to_all | solution.py:329
  186.9 4.5 %all-to-all-start.3 = ((bf16[32,64,256]{2,1,0:T(8,128)(2,1)}), bf16[32,64,256]{2,1,0:T(8,128)(2,1)S(1)}, u32[]{:S(2)}, u32[]{:S(2)}) async-start(bf16[32,64,256]{2,1,0:T(8,128)(2,1)} %bitcast.42), calls=%async_computation.3 | async-start | bytes 2097152 | tf_op jit(solution)/shard_map/all_to_all | solution.py:329
  191.5 3.1 %collective-permute-start.10 = (bf16[10,256]{1,0:T(8,128)(2,1)S(1)}, bf16[10,256]{1,0:T(8,128)(2,1)S(1)}, u32[]{:S(2)}, u32[]{:S(2)}) collective-permute-start(bf16[10,256]{1,0:T(8,128)(2,1)S(1)} %reduce_sum.12.refs_0_), channel_id=1, source_target_pairs={{0,7},{1,0},{2,1},{3,2},{4,3},{5,4},{6,5},{7,6},{8,15},{9,8},{10,9... | collective-permute-start | bytes 15368 | tf_op jit(solution)/shard_map/ppermute | solution.py:372
  194.6 2.4 collective-permute-start.9
  196.9 1.5 collective-permute-start.8
  198.4 3.6 %collective-permute-start.7 = (bf16[10,256]{1,0:T(8,128)(2,1)S(1)}, bf16[10,256]{1,0:T(8,128)(2,1)S(1)}, u32[]{:S(2)}, u32[]{:S(2)}) collective-permute-start(bf16[10,256]{1,0:T(8,128)(2,1)S(1)} %reduce_sum.12.refs_0_), channel_id=1, source_target_pairs={{0,4},{1,5},{2,6},{3,7},{4,0},{5,1},{6,2},{7,3},{8,12},{9,13},{10,... | collective-permute-start | bytes 15368 | tf_op jit(solution)/shard_map/ppermute | solution.py:372
  202.0 0.2 collective-permute-start.6
  202.2 13.9 %collective-permute-done.10.refs_7_ = bf16[10,256]{1,0:T(8,128)(2,1)S(1)} collective-permute-done((bf16[10,256]{1,0:T(8,128)(2,1)S(1)}, bf16[10,256]{1,0:T(8,128)(2,1)S(1)}, u32[]{:S(2)}, u32[]{:S(2)}) %collective-permute-start.10) | collective-permute-done | bytes 5152 | tf_op jit(solution)/shard_map/ppermute | solution.py:372
  216.1 4.3 %collective-permute-start.4 = (bf16[10,256]{1,0:T(8,128)(2,1)S(1)}, bf16[10,256]{1,0:T(8,128)(2,1)S(1)}, u32[]{:S(2)}, u32[]{:S(2)}) collective-permute-start(bf16[10,256]{1,0:T(8,128)(2,1)S(1)} %reduce_sum.12.refs_0_), channel_id=1, source_target_pairs={{0,1},{1,2},{2,3},{3,4},{4,5},{5,6},{6,7},{7,0},{8,9},{9,10},{10,1... | collective-permute-start | bytes 15368 | tf_op jit(solution)/shard_map/ppermute | solution.py:372
  220.4 1.4 collective-permute-done.5.refs_2_
  221.8 0.6 shard_map.239
  222.4 2.6 %collective-permute-start.13 = (bf16[80,256]{1,0:T(8,128)(2,1)S(1)}, bf16[80,256]{1,0:T(8,128)(2,1)S(1)}, u32[]{:S(2)}, u32[]{:S(2)}) collective-permute-start(bf16[80,256]{1,0:T(8,128)(2,1)S(1)} %reshape.84.refs_0_), channel_id=1, source_target_pairs={{0,24},{8,0},{16,8},{24,16},{1,25},{9,1},{17,9},{25,17},{2,26},{10... | collective-permute-start | bytes 122888 | tf_op jit(solution)/shard_map/ppermute | solution.py:372
  225.0 0.9 collective-permute-start.12
  225.9 0.8 collective-permute-start.11
  226.7 3.8 %collective-permute-done.12.refs_2_ = bf16[80,256]{1,0:T(8,128)(2,1)S(1)} collective-permute-done((bf16[80,256]{1,0:T(8,128)(2,1)S(1)}, bf16[80,256]{1,0:T(8,128)(2,1)S(1)}, u32[]{:S(2)}, u32[]{:S(2)}) %collective-permute-start.12) | collective-permute-done | bytes 40992 | tf_op jit(solution)/shard_map/ppermute | solution.py:372
  230.5 0.6 collective-permute-done.11.refs_1_
  231.1 0.6 shard_map.240.refs_1_
  231.7 0.8 collective-permute-start.16
  232.5 1.7 collective-permute-start.15
  234.2 2.4 collective-permute-start.14
  236.5 0.5 collective-permute-done.16.refs_4_
  237.1 2.2 collective-permute-done.15.refs_3_
  239.3 1.6 collective-permute-done.14.refs_2_
  240.9 1.4 collective-permute-done.18.refs_6_
  242.3 2.1 shard_map.241
  244.4 1.0 copy-done.8
  245.4 2.9 %shard_map.237 = f32[512,256]{1,0:T(8,128)} custom-call(bf16[2048,256]{1,0:T(8,128)(2,1)} %bitcast.43, s32[16,128]{1,0:T(8,128)} %reshape_squeeze.3.srow_ref, f32[512,256]{1,0:T(8,128)} %get-tuple-element.48.direct_ref), custom_call_target="tpu_custom_call" | custom-call | tf_op jit(solution)/shard_map/pallas_call | solution.py:592
  (45 shorter events, 0.4 us)
Async XLA Ops:
  0.6 1.0 copy-start.2
  1.6 0.7 copy-start.5
  2.3 13.3 %copy-start.13 = (f32[768]{0:T(1024)S(1)}, f32[768]{0:T(1024)}, u32[]{:S(2)}) copy-start(f32[768]{0:T(1024)} %param.25) | copy-start | bytes 9220
  2.3 13.9 %copy-start.11 = (s32[1,128,24]{1,2,0:T(8,128)S(1)}, s32[1,128,24]{1,2,0:T(8,128)}, u32[]{:S(2)}) copy-start(s32[1,128,24]{1,2,0:T(8,128)} %param.17) | copy-start | bytes 36868
  2.3 13.9 %copy-start.12 = (s32[1,128]{1,0:T(1,128)S(1)}, s32[1,128]{1,0:T(1,128)}, u32[]{:S(2)}) copy-start(s32[1,128]{1,0:T(1,128)} %param.18) | copy-start | bytes 1540
  4.1 40.2 %all-to-all-start = ((bf16[32,64,256]{2,1,0:T(8,128)(2,1)}), bf16[32,64,256]{2,1,0:T(8,128)(2,1)S(1)}, u32[]{:S(2)}, u32[]{:S(2)}) async-start(bf16[32,64,256]{2,1,0:T(8,128)(2,1)} %bitcast.4), calls=%async_computation | async-start | bytes 2097152 | tf_op jit(solution)/shard_map/all_to_all | solution.py:329
  44.3 1.0 copy-start.9
  45.3 22.6 %copy-start.6 = (s32[1,32,1,64]{3,2,1,0:T(1,128)S(1)}, s32[1,32,1,64]{3,2,1,0:T(1,128)}, u32[]{:S(2)}) copy-start(s32[1,32,1,64]{3,2,1,0:T(1,128)} %param.20) | copy-start | bytes 24580
  62.3 7.0 %copy-start.14 = (s32[1,512]{1,0:T(1,128)S(1)}, s32[1,512]{1,0:T(1,128)}, u32[]{:S(2)}) copy-start(s32[1,512]{1,0:T(1,128)} %param.19) | copy-start | bytes 6148
  62.3 33.3 %all-to-all-start.1 = ((bf16[32,64,256]{2,1,0:T(8,128)(2,1)}), bf16[32,64,256]{2,1,0:T(8,128)(2,1)S(1)}, u32[]{:S(2)}, u32[]{:S(2)}) async-start(bf16[32,64,256]{2,1,0:T(8,128)(2,1)} %bitcast.47), calls=%async_computation.1 | async-start | bytes 2097152 | tf_op jit(solution)/shard_map/all_to_all | solution.py:329
  95.6 1.0 copy-start.10
  102.3 33.2 %all-to-all-start.2 = ((bf16[32,64,256]{2,1,0:T(8,128)(2,1)}), bf16[32,64,256]{2,1,0:T(8,128)(2,1)S(1)}, u32[]{:S(2)}, u32[]{:S(2)}) async-start(bf16[32,64,256]{2,1,0:T(8,128)(2,1)} %bitcast.46), calls=%async_computation.2 | async-start | bytes 2097152 | tf_op jit(solution)/shard_map/all_to_all | solution.py:329
  121.1 14.4 %copy-start = (bf16[256,768]{1,0:T(8,128)(2,1)S(1)}, bf16[256,768]{1,0:T(8,128)(2,1)}, u32[]{:S(2)}) copy-start(bf16[256,768]{1,0:T(8,128)(2,1)} %wx_ref.5) | copy-start | bytes 1179652
  121.1 14.4 %copy-start.1 = (bf16[256,768]{1,0:T(8,128)(2,1)S(1)}, bf16[256,768]{1,0:T(8,128)(2,1)}, u32[]{:S(2)}) copy-start(bf16[256,768]{1,0:T(8,128)(2,1)} %wh_ref.5) | copy-start | bytes 1179652
  121.1 14.4 %copy-start.3 = (s32[128,24]{1,0:T(8,128)S(1)}, s32[128,24]{1,0:T(8,128)}, u32[]{:S(2)}) copy-start(s32[128,24]{1,0:T(8,128)} %copy.30.slot_ref) | copy-start | bytes 36868
  121.1 14.4 %copy-start.7 = (bf16[1,128,256]{2,1,0:T(8,128)(2,1)S(1)}, bf16[1,128,256]{2,1,0:T(8,128)(2,1)}, u32[]{:S(2)}) copy-start(bf16[1,128,256]{2,1,0:T(8,128)(2,1)} %param.22) | copy-start | bytes 196612
  135.5 1.0 copy-start.4
  154.5 2.2 collective-permute-start
  157.4 7.1 %collective-permute-start.1 = (bf16[320,256]{1,0:T(8,128)(2,1)S(1)}, bf16[320,256]{1,0:T(8,128)(2,1)S(1)}, u32[]{:S(2)}, u32[]{:S(2)}) collective-permute-start(bf16[320,256]{1,0:T(8,128)(2,1)S(1)} %get-tuple-element.53), channel_id=1, source_target_pairs={{0,64},{32,96},{64,128},{96,160},{128,192},{160,224},{192,0},{224,... | collective-permute-start | bytes 491528 | tf_op jit(solution)/shard_map/ppermute | solution.py:425
  159.0 8.6 %collective-permute-start.2 = (bf16[320,256]{1,0:T(8,128)(2,1)S(1)}, bf16[320,256]{1,0:T(8,128)(2,1)S(1)}, u32[]{:S(2)}, u32[]{:S(2)}) collective-permute-start(bf16[320,256]{1,0:T(8,128)(2,1)S(1)} %get-tuple-element.54), channel_id=1, source_target_pairs={{0,128},{32,160},{64,192},{96,224},{128,0},{160,32},{192,64},{224,... | collective-permute-start | bytes 491528 | tf_op jit(solution)/shard_map/ppermute | solution.py:425
  160.1 9.2 %collective-permute-start.3 = (bf16[320,256]{1,0:T(8,128)(2,1)S(1)}, bf16[320,256]{1,0:T(8,128)(2,1)S(1)}, u32[]{:S(2)}, u32[]{:S(2)}) collective-permute-start(bf16[320,256]{1,0:T(8,128)(2,1)S(1)} %get-tuple-element.55), channel_id=1, source_target_pairs={{0,192},{32,224},{64,0},{96,32},{128,64},{160,96},{192,128},{224,1... | collective-permute-start | bytes 491528 | tf_op jit(solution)/shard_map/ppermute | solution.py:425
  170.1 16.8 %all-to-all-start.4 = ((bf16[32,10,256]{2,1,0:T(8,128)(2,1)}), bf16[32,10,256]{2,1,0:T(8,128)(2,1)S(1)}, u32[]{:S(2)}, u32[]{:S(2)}) async-start(bf16[32,10,256]{2,1,0:T(8,128)(2,1)} %reshape.83), calls=%async_computation.4 | async-start | bytes 524288 | tf_op jit(solution)/shard_map/all_to_all | solution.py:329
  186.9 57.5 %all-to-all-start.3 = ((bf16[32,64,256]{2,1,0:T(8,128)(2,1)}), bf16[32,64,256]{2,1,0:T(8,128)(2,1)S(1)}, u32[]{:S(2)}, u32[]{:S(2)}) async-start(bf16[32,64,256]{2,1,0:T(8,128)(2,1)} %bitcast.42), calls=%async_computation.3 | async-start | bytes 2097152 | tf_op jit(solution)/shard_map/all_to_all | solution.py:329
  191.5 24.6 %collective-permute-start.10 = (bf16[10,256]{1,0:T(8,128)(2,1)S(1)}, bf16[10,256]{1,0:T(8,128)(2,1)S(1)}, u32[]{:S(2)}, u32[]{:S(2)}) collective-permute-start(bf16[10,256]{1,0:T(8,128)(2,1)S(1)} %reduce_sum.12.refs_0_), channel_id=1, source_target_pairs={{0,7},{1,0},{2,1},{3,2},{4,3},{5,4},{6,5},{7,6},{8,15},{9,8},{10,9... | collective-permute-start | bytes 15368 | tf_op jit(solution)/shard_map/ppermute | solution.py:372
  194.6 21.5 %collective-permute-start.9 = (bf16[10,256]{1,0:T(8,128)(2,1)S(1)}, bf16[10,256]{1,0:T(8,128)(2,1)S(1)}, u32[]{:S(2)}, u32[]{:S(2)}) collective-permute-start(bf16[10,256]{1,0:T(8,128)(2,1)S(1)} %reduce_sum.12.refs_0_), channel_id=1, source_target_pairs={{0,6},{1,7},{2,0},{3,1},{4,2},{5,3},{6,4},{7,5},{8,14},{9,15},{10,... | collective-permute-start | bytes 15368 | tf_op jit(solution)/shard_map/ppermute | solution.py:372
  196.9 23.5 %collective-permute-start.8 = (bf16[10,256]{1,0:T(8,128)(2,1)S(1)}, bf16[10,256]{1,0:T(8,128)(2,1)S(1)}, u32[]{:S(2)}, u32[]{:S(2)}) collective-permute-start(bf16[10,256]{1,0:T(8,128)(2,1)S(1)} %reduce_sum.12.refs_0_), channel_id=1, source_target_pairs={{0,5},{1,6},{2,7},{3,0},{4,1},{5,2},{6,3},{7,4},{8,13},{9,14},{10,... | collective-permute-start | bytes 15368 | tf_op jit(solution)/shard_map/ppermute | solution.py:372
  198.4 22.0 %collective-permute-start.7 = (bf16[10,256]{1,0:T(8,128)(2,1)S(1)}, bf16[10,256]{1,0:T(8,128)(2,1)S(1)}, u32[]{:S(2)}, u32[]{:S(2)}) collective-permute-start(bf16[10,256]{1,0:T(8,128)(2,1)S(1)} %reduce_sum.12.refs_0_), channel_id=1, source_target_pairs={{0,4},{1,5},{2,6},{3,7},{4,0},{5,1},{6,2},{7,3},{8,12},{9,13},{10,... | collective-permute-start | bytes 15368 | tf_op jit(solution)/shard_map/ppermute | solution.py:372
  202.0 18.4 %collective-permute-start.6 = (bf16[10,256]{1,0:T(8,128)(2,1)S(1)}, bf16[10,256]{1,0:T(8,128)(2,1)S(1)}, u32[]{:S(2)}, u32[]{:S(2)}) collective-permute-start(bf16[10,256]{1,0:T(8,128)(2,1)S(1)} %reduce_sum.12.refs_0_), channel_id=1, source_target_pairs={{0,3},{1,4},{2,5},{3,6},{4,7},{5,0},{6,1},{7,2},{8,11},{9,12},{10,... | collective-permute-start | bytes 15368 | tf_op jit(solution)/shard_map/ppermute | solution.py:372
  216.1 5.8 %collective-permute-start.5 = (bf16[10,256]{1,0:T(8,128)(2,1)S(1)}, bf16[10,256]{1,0:T(8,128)(2,1)S(1)}, u32[]{:S(2)}, u32[]{:S(2)}) collective-permute-start(bf16[10,256]{1,0:T(8,128)(2,1)S(1)} %reduce_sum.12.refs_0_), channel_id=1, source_target_pairs={{0,2},{1,3},{2,4},{3,5},{4,6},{5,7},{6,0},{7,1},{8,10},{9,11},{10,... | collective-permute-start | bytes 15368 | tf_op jit(solution)/shard_map/ppermute | solution.py:372
  216.1 5.8 %collective-permute-start.4 = (bf16[10,256]{1,0:T(8,128)(2,1)S(1)}, bf16[10,256]{1,0:T(8,128)(2,1)S(1)}, u32[]{:S(2)}, u32[]{:S(2)}) collective-permute-start(bf16[10,256]{1,0:T(8,128)(2,1)S(1)} %reduce_sum.12.refs_0_), channel_id=1, source_target_pairs={{0,1},{1,2},{2,3},{3,4},{4,5},{5,6},{6,7},{7,0},{8,9},{9,10},{10,1... | collective-permute-start | bytes 15368 | tf_op jit(solution)/shard_map/ppermute | solution.py:372
  222.4 4.2 %collective-permute-start.13 = (bf16[80,256]{1,0:T(8,128)(2,1)S(1)}, bf16[80,256]{1,0:T(8,128)(2,1)S(1)}, u32[]{:S(2)}, u32[]{:S(2)}) collective-permute-start(bf16[80,256]{1,0:T(8,128)(2,1)S(1)} %reshape.84.refs_0_), channel_id=1, source_target_pairs={{0,24},{8,0},{16,8},{24,16},{1,25},{9,1},{17,9},{25,17},{2,26},{10... | collective-permute-start | bytes 122888 | tf_op jit(solution)/shard_map/ppermute | solution.py:372
  225.0 5.5 %collective-permute-start.12 = (bf16[80,256]{1,0:T(8,128)(2,1)S(1)}, bf16[80,256]{1,0:T(8,128)(2,1)S(1)}, u32[]{:S(2)}, u32[]{:S(2)}) collective-permute-start(bf16[80,256]{1,0:T(8,128)(2,1)S(1)} %reshape.84.refs_0_), channel_id=1, source_target_pairs={{0,16},{8,24},{16,0},{24,8},{1,17},{9,25},{17,1},{25,9},{2,18},{10... | collective-permute-start | bytes 122888 | tf_op jit(solution)/shard_map/ppermute | solution.py:372
  225.9 5.2 %collective-permute-start.11 = (bf16[80,256]{1,0:T(8,128)(2,1)S(1)}, bf16[80,256]{1,0:T(8,128)(2,1)S(1)}, u32[]{:S(2)}, u32[]{:S(2)}) collective-permute-start(bf16[80,256]{1,0:T(8,128)(2,1)S(1)} %reshape.84.refs_0_), channel_id=1, source_target_pairs={{0,8},{8,16},{16,24},{24,0},{1,9},{9,17},{17,25},{25,1},{2,10},{10... | collective-permute-start | bytes 122888 | tf_op jit(solution)/shard_map/ppermute | solution.py:372
  231.7 5.4 %collective-permute-start.16 = (bf16[320,256]{1,0:T(8,128)(2,1)S(1)}, bf16[320,256]{1,0:T(8,128)(2,1)S(1)}, u32[]{:S(2)}, u32[]{:S(2)}) collective-permute-start(bf16[320,256]{1,0:T(8,128)(2,1)S(1)} %shard_map.240.refs_1_), channel_id=1, source_target_pairs={{0,192},{32,224},{64,0},{96,32},{128,64},{160,96},{192,128},{224,1... | collective-permute-start | bytes 491528 | tf_op jit(solution)/shard_map/ppermute | solution.py:438
  232.5 6.8 %collective-permute-start.15 = (bf16[320,256]{1,0:T(8,128)(2,1)S(1)}, bf16[320,256]{1,0:T(8,128)(2,1)S(1)}, u32[]{:S(2)}, u32[]{:S(2)}) collective-permute-start(bf16[320,256]{1,0:T(8,128)(2,1)S(1)} %shard_map.240.refs_1_), channel_id=1, source_target_pairs={{0,128},{32,160},{64,192},{96,224},{128,0},{160,32},{192,64},{224,... | collective-permute-start | bytes 491528 | tf_op jit(solution)/shard_map/ppermute | solution.py:438
  234.2 6.7 %collective-permute-start.14 = (bf16[320,256]{1,0:T(8,128)(2,1)S(1)}, bf16[320,256]{1,0:T(8,128)(2,1)S(1)}, u32[]{:S(2)}, u32[]{:S(2)}) collective-permute-start(bf16[320,256]{1,0:T(8,128)(2,1)S(1)} %shard_map.240.refs_1_), channel_id=1, source_target_pairs={{0,64},{32,96},{64,128},{96,160},{128,192},{160,224},{192,0},{224,... | collective-permute-start | bytes 491528 | tf_op jit(solution)/shard_map/ppermute | solution.py:438
  236.5 4.4 %collective-permute-start.17 = (bf16[320,256]{1,0:T(8,128)(2,1)S(1)}, bf16[320,256]{1,0:T(8,128)(2,1)S(1)}, u32[]{:S(2)}, u32[]{:S(2)}) collective-permute-start(bf16[320,256]{1,0:T(8,128)(2,1)S(1)} %shard_map.240.refs_1_), channel_id=1, source_target_pairs={{0,32},{32,0},{64,96},{96,64},{128,160},{160,128},{192,224},{224,1... | collective-permute-start | bytes 491528 | tf_op jit(solution)/shard_map/ppermute | solution.py:440
  237.1 3.8 %collective-permute-start.20 = (bf16[320,256]{1,0:T(8,128)(2,1)S(1)}, bf16[320,256]{1,0:T(8,128)(2,1)S(1)}, u32[]{:S(2)}, u32[]{:S(2)}) collective-permute-start(bf16[320,256]{1,0:T(8,128)(2,1)S(1)} %collective-permute-done.16.refs_4_), channel_id=1, source_target_pairs={{0,32},{32,0},{64,96},{96,64},{128,160},{160,128},{192,224},{224,1... | collective-permute-start | bytes 491528 | tf_op jit(solution)/shard_map/ppermute | solution.py:440
  239.3 1.6 collective-permute-start.19
  240.9 1.4 collective-permute-start.18
  244.4 1.0 copy-start.8

commit v4 on v2

--- a/solution.py
+++ b/solution.py
@@ -93,13 +93,16 @@
     hops = row_ref.shape[0]
     slots = buf_ref.shape[0]
     idx = row_ref[...]
-    copies = []
-    for k, q in enumerate(range(0, slots, block)):
+
+    def step(k, carry):
+        q = pl.multiple_of(k * block, block)
         sel = jnp.concatenate([pick_rows(idx[t : t + 1, :], block, q) for t in range(hops)], axis=1)
-        buf_ref[q : q + block, :] = dot(sel, rows).astype(BF)
-        copies.append(send(buf_ref, out_hbm, sem, q, block, k))
-        copies[-1].start()
-    return copies
+        buf_ref[pl.ds(q, block), :] = dot(sel, rows).astype(BF)
+        send(buf_ref, out_hbm, sem, q, block, k).start()
+        return carry
+
+    lax.fori_loop(0, slots // block, step, 0, unroll=2)
+    return [send(buf_ref, out_hbm, sem, k * block, block, k) for k in range(slots // block)]
 
 
 def forward_kernel(
@@ -347,6 +350,34 @@
         out_refs[k][...] = both.astype(BF)
 
 
+def ring_sum_kernel(place_ref, *refs):
+    count = len(refs) // 2
+    rows = refs[count].shape[0]
+    for k in range(count):
+        at = pl.ds(pl.multiple_of(lax.rem(place_ref[2] + k, count) * rows, 16), rows)
+        value = refs[0][at, :].astype(F32)
+        for ref in refs[1:count]:
+            value = value + ref[at, :].astype(F32)
+        refs[count + k][...] = value.astype(BF)
+
+
+def outer_join_kernel(place_ref, *refs):
+    out_ref = refs[-1]
+    count = len(refs) - 1
+    rows = refs[0].shape[0]
+    for k in range(count):
+        to = lax.rem(place_ref[2] - k + count, count)
+        out_ref[pl.ds(pl.multiple_of(to * rows, 16), rows), :] = refs[k][...]
+
+
+def around(piece, axis):
+    count = lax.axis_size(axis)
+    got = [piece]
+    for k in range(1, count):
+        got.append(lax.ppermute(piece, axis, [(i, (i + k) % count) for i in range(count)]))
+    return got
+
+
 def unpack_kernel(place_ref, *refs, scale):
     x = place_ref[0]
     core = place_ref[1]
@@ -375,14 +406,14 @@
 
 def whereabouts():
     rep = lax.axis_index("replica")
-    return jnp.stack([rep // 2, rep % 2]).astype(jnp.int32)
+    spots = [rep // 2, rep % 2, lax.axis_index("outer"), lax.axis_index("link")]
+    return jnp.stack(spots).astype(jnp.int32)
 
 
 def sum_everywhere(mine, other, place, scale):
     rows, width = mine.shape
     rows = 2 * rows
     reps = lax.axis_size("replica")
-    group = lax.axis_size("outer") * lax.axis_size("link")
     chips = reps // 2
     part = rows // reps
     pairs = [(i, i ^ 1) for i in range(reps)]
@@ -394,9 +425,23 @@
         pair_kernel, (sds((part, width), BF),) * chips, in_specs=[smem, vmem, vmem]
     )(place, mine, got)
     got = [lax.ppermute(mine[k], "replica", ahead[k]) for k in range(1, chips)]
+    lines = lax.axis_size("outer")
+    mine = call(
+        ring_sum_kernel,
+        (sds((part // lines, width), BF),) * lines,
+        in_specs=[smem] + [vmem] * chips,
+    )(place, mine[0], *got)
+    got = []
+    for k in range(1, lines):
+        hops = [(i, (i + k) % lines) for i in range(lines)]
+        got.append(lax.ppermute(mine[k], "outer", hops))
     mine = sum((g.astype(F32) for g in got), mine[0].astype(F32)).astype(BF)
-    mine = total(swap(mine.reshape(group, part // group, width)))
-    mine = swap(jnp.broadcast_to(mine[None], (group,) + mine.shape)).reshape(part, width)
+    count = lax.axis_size("link")
+    mine = total(swap(jnp.broadcast_to(mine[None], (count,) + mine.shape), "link"))
+    got = around(mine, "outer")
+    mine = call(
+        outer_join_kernel, sds((part, width), BF), in_specs=[smem] + [vmem] * len(got)
+    )(place, *got)
     whole = [mine]
     for k in range(1, chips):
         whole.append(lax.ppermute(mine, "replica", ahead[k]))

time: 248 us -> 238 us (0.960)
  blocking collectives: 32.3 us -> 14.7 us
  starting transfers between devices: 37 us -> 44.8 us
    all_to_all x2 -> x1, blocking collectives: 32.3 us -> 14.7 us  [swap(): lax.all_to_all(blocks, axes, split_axis=0, concat_axis=0, tiled=True, axi...]
    all_to_all x4, waiting for transfers between devices: 79.8 us -> 68.9 us  [swap(): lax.all_to_all(blocks, axes, split_axis=0, concat_axis=0, tiled=True, axi...]
    ppermute x0 -> x6, starting transfers between devices: none -> 9.72 us  [the longest x3 6.01 us: around(): lax.ppermute(piece, axis, [(i, (i + k) % count) for i in range(count)])]
    ppermute x0 -> x6, waiting for transfers between devices: none -> 6.62 us  [the longest x3 3.54 us: around(): lax.ppermute(piece, axis, [(i, (i + k) % count) for i in range(count)])]
  transfers between devices with their start and end apart: 15 -> 21, of which waited for: 11 -> 17; matrix products, arithmetic and copies ran while one was open for 2% -> 3% of each run, Pallas kernels for 6% -> 7%
where the time goes in v4:
time: 238 us; the launch traced here: 236 us
  waiting for transfers between devices  91.2 us (38%)
  Pallas kernels  72 us (30%)
  starting transfers between devices  44.8 us (19%)
  blocking collectives  14.7 us (6%)
  local copies, waits for them, and re-layouts  10.5 us (4%)
    all_to_all x4, waiting for transfers between devices, swap(): lax.all_to_all(blocks, axes, split_axis=0, concat_axis=0, tiled=True, axi...  68.9 us
    all_to_all x4, starting transfers between devices, swap(): lax.all_to_all(blocks, axes, split_axis=0, concat_axis=0, tiled=True, axi...  26.4 us
    pallas_call x1, Pallas kernels, body(): call(backward_kernel, (sds((slots, width), BF), sds((flows, width), F32),...  19.1 us
    pallas_call x1, Pallas kernels, body(): call(forward_kernel, (sds((hops, flows, width), BF), sds((hops, flows, wi...  16.4 us
    all_to_all x1, blocking collectives, swap(): lax.all_to_all(blocks, axes, split_axis=0, concat_axis=0, tiled=True, axi...  14.7 us
    pallas_call x1, Pallas kernels, body(): call(coef_kernel, sds((hops, 5, flows, width), F32), mib=58, grid=(hops /...  10.5 us
    pallas_call x1, Pallas kernels, body(): call(weight_kernel, (sds((5 * width, width), BF),) * 2, mib=58, grid=(hop...  8.9 us
    ppermute x3, waiting for transfers between devices, sum_everywhere(): got = [lax.ppermute(mine[k], 'replica', ahead[k]) for k in range(1, chips)]  7.04 us
  transfers between devices with their start and end apart: 21, of which 17 were waited for; matrix products, arithmetic and copies ran while one was open for 3% of the time, Pallas kernels for 7%

profile of v4, /device:TPU:2, one launch (start us, length us, event | category | flops | bytes accessed | tf_op | source)
XLA Modules:
  0.0 236.1 jit_solution(3585725120988521432)
XLA Ops:
  0.7 0.0 copy-start.2
  0.7 0.9 copy-done.2
  1.6 0.7 copy-done.5
  2.3 1.8 shard_map.230
  4.1 0.0 copy-start.17
  4.2 11.5 %all-to-all-start = ((bf16[32,64,256]{2,1,0:T(8,128)(2,1)}), bf16[32,64,256]{2,1,0:T(8,128)(2,1)S(1)}, u32[]{:S(2)}, u32[]{:S(2)}) async-start(bf16[32,64,256]{2,1,0:T(8,128)(2,1)} %bitcast.4), calls=%async_computation | async-start | bytes 2097152 | tf_op jit(solution)/shard_map/all_to_all | solution.py:330
  15.7 0.7 copy.36.slot_ref
  16.4 0.7 copy.37.lens_ref
  17.2 0.6 broadcast_in_dim.34.bias_ref
  17.8 0.6 fusion.row_ref
  18.4 25.9 %all-to-all-done = bf16[32,64,256]{2,1,0:T(8,128)(2,1)S(1)} async-done(((bf16[32,64,256]{2,1,0:T(8,128)(2,1)}), bf16[32,64,256]{2,1,0:T(8,128)(2,1)S(1)}, u32[]{:S(2)}, u32[]{:S(2)}) %all-to-all-start) | async-done | bytes 1048608 | tf_op jit(solution)/shard_map/all_to_all | solution.py:330
  44.3 1.0 copy-done.12
  45.3 16.4 %shard_map.231 = (bf16[24,128,256]{2,1,0:T(8,128)(2,1)}, f32[24,128,256]{2,1,0:T(8,128)}, bf16[24,128,256]{2,1,0:T(8,128)(2,1)}, bf16[2048,256]{1,0:T(8,128)(2,1)}, bf16[128,256]{1,0:T(8,128)(2,1)}) custom-call(bf16[2048,256]{1,0:T(8,128)(2,1)} %bitcast.43, s32[128,24]{1,0:T(8,128)} %copy.36.slot_ref, s32[24,128]{1,0:T(8,128)} %fusion.row_ref, ...), custom_call_target="tpu_custom_call" | custom-call | tf_op jit(solution)/shard_map/pallas_call | solution.py:497
  61.7 5.1 %all-to-all-start.1 = ((bf16[32,64,256]{2,1,0:T(8,128)(2,1)}), bf16[32,64,256]{2,1,0:T(8,128)(2,1)S(1)}, u32[]{:S(2)}, u32[]{:S(2)}) async-start(bf16[32,64,256]{2,1,0:T(8,128)(2,1)} %bitcast.46), calls=%async_computation.1 | async-start | bytes 2097152 | tf_op jit(solution)/shard_map/all_to_all | solution.py:330
  66.8 0.9 copy.39.keep_ref
  67.7 0.5 broadcast.15
  68.2 0.7 reduce.4
  68.9 0.7 reshape_squeeze.3.srow_ref
  69.5 25.5 %all-to-all-done.1 = bf16[32,64,256]{2,1,0:T(8,128)(2,1)S(1)} async-done(((bf16[32,64,256]{2,1,0:T(8,128)(2,1)}), bf16[32,64,256]{2,1,0:T(8,128)(2,1)S(1)}, u32[]{:S(2)}, u32[]{:S(2)}) %all-to-all-start.1) | async-done | bytes 1048608 | tf_op jit(solution)/shard_map/all_to_all | solution.py:330
  95.1 1.0 copy-done.13
  96.0 5.6 %shard_map.232 = (bf16[2048,256]{1,0:T(8,128)(2,1)}, bf16[1536,256]{1,0:T(8,128)(2,1)}, f32[1,256]{1,0:T(1,128)}) custom-call(bf16[2048,256]{1,0:T(8,128)(2,1)} %bitcast.44, s32[16,128]{1,0:T(8,128)} %reshape_squeeze.3.srow_ref, s32[32,64]{1,0:T(8,128)} %bitcast.39, bf16[512,256]{1,0:T(8,128)(2,1)} %bitcast.36, bf16[512,256]{1,0:T(8,128)(2,1)} %bitcast.47, ...), custom_call_target="tpu_custom_call" | custom-call | tf_op jit(solution)/shard_map/pallas_call | solution.py:540
  101.7 5.1 %all-to-all-start.2 = ((bf16[32,64,256]{2,1,0:T(8,128)(2,1)}), bf16[32,64,256]{2,1,0:T(8,128)(2,1)S(1)}, u32[]{:S(2)}, u32[]{:S(2)}) async-start(bf16[32,64,256]{2,1,0:T(8,128)(2,1)} %bitcast.45), calls=%async_computation.2 | async-start | bytes 2097152 | tf_op jit(solution)/shard_map/all_to_all | solution.py:330
  106.8 0.6 pad_add_fusion.place_ref.refs_0_
  107.4 10.5 %shard_map.234.coef_hbm = f32[24,5,128,256]{3,2,1,0:T(8,128)} custom-call(bf16[24,128,256]{2,1,0:T(8,128)(2,1)} %get-tuple-element.49.x_ref, f32[24,128,256]{2,1,0:T(8,128)} %get-tuple-element.50.state_ref, s32[128,1]{1,0:T(8,128)} %copy.37.lens_ref, bf16[256,768]{1,0:T(8,128)(2,1)} %wx_ref.5, bf16[256,768]{1,0:T(8,128)(2,1)} %wh_ref.5, ...), custom_call_target="tpu_custom_call" | custom-call | tf_op jit(solution)/shard_map/pallas_call | solution.py:524
  118.0 2.9 %shard_map.233 = (bf16[512,256]{1,0:T(8,128)(2,1)}, f32[512,256]{1,0:T(8,128)}, bf16[784,256]{1,0:T(8,128)(2,1)}) custom-call(bf16[512,256]{1,0:T(8,128)(2,1)} %bitcast.37, bf16[512,256]{1,0:T(8,128)(2,1)} %bitcast.48, f32[512,1]{1,0:T(8,128)} %copy.39.keep_ref, bf16[1536,256]{1,0:T(8,128)(2,1)} %get-tuple-element.44.mid_ref, ...), custom_call_target="tpu_custom_call" | custom-call | tf_op jit(solution)/shard_map/pallas_call | solution.py:557
  120.8 14.1 %all-to-all-done.2 = bf16[32,64,256]{2,1,0:T(8,128)(2,1)S(1)} async-done(((bf16[32,64,256]{2,1,0:T(8,128)(2,1)}), bf16[32,64,256]{2,1,0:T(8,128)(2,1)S(1)}, u32[]{:S(2)}, u32[]{:S(2)}) %all-to-all-start.2) | async-done | bytes 1048608 | tf_op jit(solution)/shard_map/all_to_all | solution.py:330
  134.9 19.1 %shard_map.235 = (bf16[2048,256]{1,0:T(8,128)(2,1)}, f32[128,256]{1,0:T(8,128)}, bf16[24,128,1024]{2,1,0:T(8,128)(2,1)}, f32[8,768]{1,0:T(8,128)S(1)}) custom-call(bf16[2048,256]{1,0:T(8,128)(2,1)S(1)} %bitcast.35, s32[128,24]{1,0:T(8,128)S(1)} %copy-done.4, s32[24,128]{1,0:T(8,128)S(1)} %copy-done.7, bf16[128,256]{1,0:T(8,128)(2,1)S(1)} %bitcast.41, ...), custom_call_target="tpu_custom_call" | custom-call | tf_op jit(solution)/shard_map/pallas_call | solution.py:567
  154.0 0.6 copy-done.9
  154.6 8.9 %shard_map.237 = (bf16[1280,256]{1,0:T(8,128)(2,1)}, bf16[1280,256]{1,0:T(8,128)(2,1)}) custom-call(s32[4]{0:T(128)} %pad_add_fusion.place_ref.refs_0_, bf16[24,128,256]{2,1,0:T(8,128)(2,1)} %get-tuple-element.49.x_ref, bf16[24,128,256]{2,1,0:T(8,128)(2,1)} %get-tuple-element.54.prior_ref, bf16[24,128,1024]{2,1,0:T(8,128)(2,1)} %get-tuple-element.55.gate_ref, ...), custom_call_target="tpu_custom_call" | custom-call | tf_op jit(solution)/shard_map/pallas_call | solution.py:591
  163.5 2.3 collective-permute-done.got_ref
  165.8 1.1 copy-done.3
  166.9 0.7 shard_map.238
  167.6 1.6 collective-permute-start.1
  169.2 1.1 collective-permute-start.2
  170.3 2.2 collective-permute-start.3
  172.5 2.3 collective-permute-done.1.refs_1_
  174.8 3.0 %collective-permute-done.2.refs_2_ = bf16[320,256]{1,0:T(8,128)(2,1)S(1)} collective-permute-done((bf16[320,256]{1,0:T(8,128)(2,1)S(1)}, bf16[320,256]{1,0:T(8,128)(2,1)S(1)}, u32[]{:S(2)}, u32[]{:S(2)}) %collective-permute-start.2) | collective-permute-done | bytes 163872 | tf_op jit(solution)/shard_map/ppermute | solution.py:427
  177.8 1.7 collective-permute-done.3.refs_3_
  179.5 0.6 shard_map.239
  180.1 0.3 collective-permute-start.4
  180.5 2.2 collective-permute-start.5
  182.7 1.2 collective-permute-start.6
  183.9 2.2 collective-permute-done.4
  186.1 0.9 collective-permute-done.6
  187.0 14.7 %all_to_all.25 = bf16[8,80,256]{2,1,0:T(8,128)(2,1)S(1)} all-to-all(bf16[8,80,256]{2,1,0:T(8,128)(2,1)S(1)} %broadcast_in_dim.41), channel_id=1, replica_groups=mesh['replica'=8,'outer'=4,'link'=8] {'link'}, dimensions={0} | all-to-all | bytes 655360 | tf_op jit(solution)/shard_map/all_to_all | solution.py:330
  201.7 4.6 %all-to-all-start.3 = ((bf16[32,64,256]{2,1,0:T(8,128)(2,1)}), bf16[32,64,256]{2,1,0:T(8,128)(2,1)S(1)}, u32[]{:S(2)}, u32[]{:S(2)}) async-start(bf16[32,64,256]{2,1,0:T(8,128)(2,1)} %bitcast.20), calls=%async_computation.3 | async-start | bytes 2097152 | tf_op jit(solution)/shard_map/all_to_all | solution.py:330
  206.4 1.9 collective-permute-start.7
  208.3 2.7 %collective-permute-start.8 = (bf16[80,256]{1,0:T(8,128)(2,1)S(1)}, bf16[80,256]{1,0:T(8,128)(2,1)S(1)}, u32[]{:S(2)}, u32[]{:S(2)}) collective-permute-start(bf16[80,256]{1,0:T(8,128)(2,1)S(1)} %reduce_sum.12.refs_0_), channel_id=1, source_target_pairs={{0,16},{8,24},{16,0},{24,8},{1,17},{9,25},{17,1},{25,9},{2,18},{10... | collective-permute-start | bytes 122888 | tf_op jit(solution)/shard_map/ppermute | solution.py:377
  211.0 1.4 collective-permute-start.9
  212.4 0.6 collective-permute-done.7.refs_1_
  213.1 0.9 collective-permute-done.8.refs_2_
  213.9 2.0 collective-permute-done.9.refs_3_
  216.0 0.6 shard_map.240.refs_1_
  216.5 0.4 collective-permute-start.10
  216.9 1.3 collective-permute-start.11
  218.2 2.1 collective-permute-start.12
  220.4 1.6 collective-permute-done.10.refs_2_
  221.9 1.9 collective-permute-done.11.refs_3_
  223.9 1.5 collective-permute-done.12.refs_4_
  225.3 1.4 collective-permute-done.16.refs_8_
  226.7 2.1 shard_map.241
  228.8 3.4 %all-to-all-done.3 = bf16[32,64,256]{2,1,0:T(8,128)(2,1)S(1)} async-done(((bf16[32,64,256]{2,1,0:T(8,128)(2,1)}), bf16[32,64,256]{2,1,0:T(8,128)(2,1)S(1)}, u32[]{:S(2)}, u32[]{:S(2)}) %all-to-all-start.3) | async-done | bytes 1048608 | tf_op jit(solution)/shard_map/all_to_all | solution.py:330
  232.2 1.0 copy-done.11
  233.2 2.9 %shard_map.236 = f32[512,256]{1,0:T(8,128)} custom-call(bf16[2048,256]{1,0:T(8,128)(2,1)} %bitcast.42, s32[16,128]{1,0:T(8,128)} %reshape_squeeze.3.srow_ref, f32[512,256]{1,0:T(8,128)} %get-tuple-element.52.direct_ref), custom_call_target="tpu_custom_call" | custom-call | tf_op jit(solution)/shard_map/pallas_call | solution.py:611
  (41 shorter events, 0.2 us)
Async XLA Ops:
  0.6 15.0 %copy-start.15 = (s32[1,128]{1,0:T(1,128)S(1)}, s32[1,128]{1,0:T(1,128)}, u32[]{:S(2)}) copy-start(s32[1,128]{1,0:T(1,128)} %param.18) | copy-start | bytes 1540
  0.7 1.0 copy-start.2
  1.6 0.7 copy-start.5
  2.3 13.4 %copy-start.14 = (s32[1,128,24]{1,2,0:T(8,128)S(1)}, s32[1,128,24]{1,2,0:T(8,128)}, u32[]{:S(2)}) copy-start(s32[1,128,24]{1,2,0:T(8,128)} %param.17) | copy-start | bytes 36868
  2.3 14.8 %copy-start.16 = (f32[768]{0:T(1024)S(1)}, f32[768]{0:T(1024)}, u32[]{:S(2)}) copy-start(f32[768]{0:T(1024)} %param.25) | copy-start | bytes 9220
  4.1 62.6 %copy-start.17 = (s32[1,512]{1,0:T(1,128)S(1)}, s32[1,512]{1,0:T(1,128)}, u32[]{:S(2)}) copy-start(s32[1,512]{1,0:T(1,128)} %param.19) | copy-start | bytes 6148
  4.2 64.0 %copy-start.6 = (s32[1,32,1,64]{3,2,1,0:T(1,128)S(1)}, s32[1,32,1,64]{3,2,1,0:T(1,128)}, u32[]{:S(2)}) copy-start(s32[1,32,1,64]{3,2,1,0:T(1,128)} %param.20) | copy-start | bytes 24580
  4.2 40.1 %all-to-all-start = ((bf16[32,64,256]{2,1,0:T(8,128)(2,1)}), bf16[32,64,256]{2,1,0:T(8,128)(2,1)S(1)}, u32[]{:S(2)}, u32[]{:S(2)}) async-start(bf16[32,64,256]{2,1,0:T(8,128)(2,1)} %bitcast.4), calls=%async_computation | async-start | bytes 2097152 | tf_op jit(solution)/shard_map/all_to_all | solution.py:330
  44.3 1.0 copy-start.12
  61.7 33.4 %all-to-all-start.1 = ((bf16[32,64,256]{2,1,0:T(8,128)(2,1)}), bf16[32,64,256]{2,1,0:T(8,128)(2,1)S(1)}, u32[]{:S(2)}, u32[]{:S(2)}) async-start(bf16[32,64,256]{2,1,0:T(8,128)(2,1)} %bitcast.46), calls=%async_computation.1 | async-start | bytes 2097152 | tf_op jit(solution)/shard_map/all_to_all | solution.py:330
  95.1 1.0 copy-start.13
  101.7 33.2 %all-to-all-start.2 = ((bf16[32,64,256]{2,1,0:T(8,128)(2,1)}), bf16[32,64,256]{2,1,0:T(8,128)(2,1)S(1)}, u32[]{:S(2)}, u32[]{:S(2)}) async-start(bf16[32,64,256]{2,1,0:T(8,128)(2,1)} %bitcast.45), calls=%async_computation.2 | async-start | bytes 2097152 | tf_op jit(solution)/shard_map/all_to_all | solution.py:330
  107.4 27.5 %copy-start = (bf16[256,768]{1,0:T(8,128)(2,1)S(1)}, bf16[256,768]{1,0:T(8,128)(2,1)}, u32[]{:S(2)}) copy-start(bf16[256,768]{1,0:T(8,128)(2,1)} %wx_ref.5) | copy-start | bytes 1179652
  107.4 27.5 %copy-start.1 = (bf16[256,768]{1,0:T(8,128)(2,1)S(1)}, bf16[256,768]{1,0:T(8,128)(2,1)}, u32[]{:S(2)}) copy-start(bf16[256,768]{1,0:T(8,128)(2,1)} %wh_ref.5) | copy-start | bytes 1179652
  107.4 27.5 %copy-start.4 = (s32[128,24]{1,0:T(8,128)S(1)}, s32[128,24]{1,0:T(8,128)}, u32[]{:S(2)}) copy-start(s32[128,24]{1,0:T(8,128)} %copy.36.slot_ref) | copy-start | bytes 36868
  107.4 27.5 %copy-start.7 = (s32[24,128]{1,0:T(8,128)S(1)}, s32[24,128]{1,0:T(8,128)}, u32[]{:S(2)}) copy-start(s32[24,128]{1,0:T(8,128)} %fusion.row_ref) | copy-start | bytes 36868
  107.4 27.5 %copy-start.8 = (bf16[1,128,256]{2,1,0:T(8,128)(2,1)S(1)}, bf16[1,128,256]{2,1,0:T(8,128)(2,1)}, u32[]{:S(2)}) copy-start(bf16[1,128,256]{2,1,0:T(8,128)(2,1)} %param.22) | copy-start | bytes 196612
  154.0 0.6 copy-start.9
  154.6 11.2 %copy-start.10 = (s32[4]{0:T(128)S(1)}, s32[4]{0:T(128)}, u32[]{:S(2)}) copy-start(s32[4]{0:T(128)} %pad_add_fusion.place_ref.refs_0_) | copy-start | bytes 52
  163.5 2.3 collective-permute-start
  165.8 1.1 copy-start.3
  167.6 7.1 %collective-permute-start.1 = (bf16[320,256]{1,0:T(8,128)(2,1)S(1)}, bf16[320,256]{1,0:T(8,128)(2,1)S(1)}, u32[]{:S(2)}, u32[]{:S(2)}) collective-permute-start(bf16[320,256]{1,0:T(8,128)(2,1)S(1)} %get-tuple-element.61), channel_id=1, source_target_pairs={{0,64},{32,96},{64,128},{96,160},{128,192},{160,224},{192,0},{224,... | collective-permute-start | bytes 491528 | tf_op jit(solution)/shard_map/ppermute | solution.py:427
  169.2 8.6 %collective-permute-start.2 = (bf16[320,256]{1,0:T(8,128)(2,1)S(1)}, bf16[320,256]{1,0:T(8,128)(2,1)S(1)}, u32[]{:S(2)}, u32[]{:S(2)}) collective-permute-start(bf16[320,256]{1,0:T(8,128)(2,1)S(1)} %get-tuple-element.62), channel_id=1, source_target_pairs={{0,128},{32,160},{64,192},{96,224},{128,0},{160,32},{192,64},{224,... | collective-permute-start | bytes 491528 | tf_op jit(solution)/shard_map/ppermute | solution.py:427
  170.3 9.2 %collective-permute-start.3 = (bf16[320,256]{1,0:T(8,128)(2,1)S(1)}, bf16[320,256]{1,0:T(8,128)(2,1)S(1)}, u32[]{:S(2)}, u32[]{:S(2)}) collective-permute-start(bf16[320,256]{1,0:T(8,128)(2,1)S(1)} %get-tuple-element.63), channel_id=1, source_target_pairs={{0,192},{32,224},{64,0},{96,32},{128,64},{160,96},{192,128},{224,1... | collective-permute-start | bytes 491528 | tf_op jit(solution)/shard_map/ppermute | solution.py:427
  180.1 5.9 %collective-permute-start.4 = (bf16[80,256]{1,0:T(8,128)(2,1)S(1)}, bf16[80,256]{1,0:T(8,128)(2,1)S(1)}, u32[]{:S(2)}, u32[]{:S(2)}) collective-permute-start(bf16[80,256]{1,0:T(8,128)(2,1)S(1)} %get-tuple-element.65), channel_id=1, source_target_pairs={{0,8},{8,16},{16,24},{24,0},{1,9},{9,17},{17,25},{25,1},{2,10},{10... | collective-permute-start | bytes 122888 | tf_op jit(solution)/shard_map/ppermute | solution.py:437
  180.5 5.6 %collective-permute-start.5 = (bf16[80,256]{1,0:T(8,128)(2,1)S(1)}, bf16[80,256]{1,0:T(8,128)(2,1)S(1)}, u32[]{:S(2)}, u32[]{:S(2)}) collective-permute-start(bf16[80,256]{1,0:T(8,128)(2,1)S(1)} %get-tuple-element.66), channel_id=1, source_target_pairs={{0,16},{8,24},{16,0},{24,8},{1,17},{9,25},{17,1},{25,9},{2,18},{10... | collective-permute-start | bytes 122888 | tf_op jit(solution)/shard_map/ppermute | solution.py:437
  182.7 4.2 %collective-permute-start.6 = (bf16[80,256]{1,0:T(8,128)(2,1)S(1)}, bf16[80,256]{1,0:T(8,128)(2,1)S(1)}, u32[]{:S(2)}, u32[]{:S(2)}) collective-permute-start(bf16[80,256]{1,0:T(8,128)(2,1)S(1)} %get-tuple-element.67), channel_id=1, source_target_pairs={{0,24},{8,0},{16,8},{24,16},{1,25},{9,1},{17,9},{25,17},{2,26},{10... | collective-permute-start | bytes 122888 | tf_op jit(solution)/shard_map/ppermute | solution.py:437
  201.7 30.5 %all-to-all-start.3 = ((bf16[32,64,256]{2,1,0:T(8,128)(2,1)}), bf16[32,64,256]{2,1,0:T(8,128)(2,1)S(1)}, u32[]{:S(2)}, u32[]{:S(2)}) async-start(bf16[32,64,256]{2,1,0:T(8,128)(2,1)} %bitcast.20), calls=%async_computation.3 | async-start | bytes 2097152 | tf_op jit(solution)/shard_map/all_to_all | solution.py:330
  206.4 6.7 %collective-permute-start.7 = (bf16[80,256]{1,0:T(8,128)(2,1)S(1)}, bf16[80,256]{1,0:T(8,128)(2,1)S(1)}, u32[]{:S(2)}, u32[]{:S(2)}) collective-permute-start(bf16[80,256]{1,0:T(8,128)(2,1)S(1)} %reduce_sum.12.refs_0_), channel_id=1, source_target_pairs={{0,8},{8,16},{16,24},{24,0},{1,9},{9,17},{17,25},{25,1},{2,10},{10... | collective-permute-start | bytes 122888 | tf_op jit(solution)/shard_map/ppermute | solution.py:377
  208.3 5.6 %collective-permute-start.8 = (bf16[80,256]{1,0:T(8,128)(2,1)S(1)}, bf16[80,256]{1,0:T(8,128)(2,1)S(1)}, u32[]{:S(2)}, u32[]{:S(2)}) collective-permute-start(bf16[80,256]{1,0:T(8,128)(2,1)S(1)} %reduce_sum.12.refs_0_), channel_id=1, source_target_pairs={{0,16},{8,24},{16,0},{24,8},{1,17},{9,25},{17,1},{25,9},{2,18},{10... | collective-permute-start | bytes 122888 | tf_op jit(solution)/shard_map/ppermute | solution.py:377
  211.0 5.0 %collective-permute-start.9 = (bf16[80,256]{1,0:T(8,128)(2,1)S(1)}, bf16[80,256]{1,0:T(8,128)(2,1)S(1)}, u32[]{:S(2)}, u32[]{:S(2)}) collective-permute-start(bf16[80,256]{1,0:T(8,128)(2,1)S(1)} %reduce_sum.12.refs_0_), channel_id=1, source_target_pairs={{0,24},{8,0},{16,8},{24,16},{1,25},{9,1},{17,9},{25,17},{2,26},{10... | collective-permute-start | bytes 122888 | tf_op jit(solution)/shard_map/ppermute | solution.py:377
  216.5 5.4 %collective-permute-start.10 = (bf16[320,256]{1,0:T(8,128)(2,1)S(1)}, bf16[320,256]{1,0:T(8,128)(2,1)S(1)}, u32[]{:S(2)}, u32[]{:S(2)}) collective-permute-start(bf16[320,256]{1,0:T(8,128)(2,1)S(1)} %shard_map.240.refs_1_), channel_id=1, source_target_pairs={{0,64},{32,96},{64,128},{96,160},{128,192},{160,224},{192,0},{224,... | collective-permute-start | bytes 491528 | tf_op jit(solution)/shard_map/ppermute | solution.py:447
  216.9 6.9 %collective-permute-start.11 = (bf16[320,256]{1,0:T(8,128)(2,1)S(1)}, bf16[320,256]{1,0:T(8,128)(2,1)S(1)}, u32[]{:S(2)}, u32[]{:S(2)}) collective-permute-start(bf16[320,256]{1,0:T(8,128)(2,1)S(1)} %shard_map.240.refs_1_), channel_id=1, source_target_pairs={{0,128},{32,160},{64,192},{96,224},{128,0},{160,32},{192,64},{224,... | collective-permute-start | bytes 491528 | tf_op jit(solution)/shard_map/ppermute | solution.py:447
  218.2 7.1 %collective-permute-start.12 = (bf16[320,256]{1,0:T(8,128)(2,1)S(1)}, bf16[320,256]{1,0:T(8,128)(2,1)S(1)}, u32[]{:S(2)}, u32[]{:S(2)}) collective-permute-start(bf16[320,256]{1,0:T(8,128)(2,1)S(1)} %shard_map.240.refs_1_), channel_id=1, source_target_pairs={{0,192},{32,224},{64,0},{96,32},{128,64},{160,96},{192,128},{224,1... | collective-permute-start | bytes 491528 | tf_op jit(solution)/shard_map/ppermute | solution.py:447
  220.4 5.0 %collective-permute-start.13 = (bf16[320,256]{1,0:T(8,128)(2,1)S(1)}, bf16[320,256]{1,0:T(8,128)(2,1)S(1)}, u32[]{:S(2)}, u32[]{:S(2)}) collective-permute-start(bf16[320,256]{1,0:T(8,128)(2,1)S(1)} %shard_map.240.refs_1_), channel_id=1, source_target_pairs={{0,32},{32,0},{64,96},{96,64},{128,160},{160,128},{192,224},{224,1... | collective-permute-start | bytes 491528 | tf_op jit(solution)/shard_map/ppermute | solution.py:449
  221.9 3.4 %collective-permute-start.14 = (bf16[320,256]{1,0:T(8,128)(2,1)S(1)}, bf16[320,256]{1,0:T(8,128)(2,1)S(1)}, u32[]{:S(2)}, u32[]{:S(2)}) collective-permute-start(bf16[320,256]{1,0:T(8,128)(2,1)S(1)} %collective-permute-done.10.refs_2_), channel_id=1, source_target_pairs={{0,32},{32,0},{64,96},{96,64},{128,160},{160,128},{192,224},{224,1... | collective-permute-start | bytes 491528 | tf_op jit(solution)/shard_map/ppermute | solution.py:449
  223.8 1.5 collective-permute-start.15
  225.3 1.4 collective-permute-start.16
  232.2 1.0 copy-start.11
